TPU v7x, 32 devices: a whole 2x2x4 slice. The times are simulated.
32 devices in a mesh: groups: 2 (over y), by: 4 (over z), bx: 2 (over x), bz: 2 (over core).
Axes of the slice: x: 2, y: 2, z: 4, core: 2. Of those that a mesh axis runs over, the one named last changes fastest.
Arguments:
- estimate: float32 [64, 64, 512], P(('groups', 'bz'), 'bx', 'by'), parts along dimension 0, may hold values from 0.5 to 2
- recorded: bfloat16 [6, 64, 64, 512], P(None, ('groups', 'bz'), ('bx', 'by')), parts along dimension 1, may hold values from 0.099609375 to 4
- profiles: float32 [6, 3, 15], replicated, may hold values from 0.02 to 0.12
- view_boxes: int32 [12, 6], P('groups'), parts along dimension 0, may hold values from 0 to 512, as said below
Outputs:
- refined: float32 [64, 64, 512], P(('groups', 'bz'), 'bx', 'by'), parts along dimension 0
There are 2 independent parts, one for each index of `groups`. A program takes and returns all parts, laid end to end along the dimension named above; an argument that names none is the same for every part. Nothing has to cross between parts.
Inputs may be any that keep to these rules, and one draw needn't show every extreme that they name: `view_boxes`: every box has lower bound below upper bound, within the grid of 32 x 64 x 512 cells; the first view's box is the whole grid.
All inputs are finite; a program needn't handle non-finite values.
Results may differ from a plain program's by a relative error of at most 0.0003.
Values may be sent and summed in bfloat16 or wider, within the bound.
No kernel may reach another device: no remote copies, remote signals or barrier semaphores. Data moves between devices by JAX's collectives and lax.ppermute only.
A program may use at most 128 MiB of HBM per device.

v0:
```python
import jax
import jax.numpy as jnp
from jax import lax
from jax.sharding import PartitionSpec as P

TAPS = 15


BACKGROUND = 0.05


def extended(cells, sides, width):
    for axis, dim in sides:
        count = lax.axis_size(axis)
        ends = count - 1
        head = lax.slice_in_dim(cells, 0, width, axis=dim)
        tail = lax.slice_in_dim(cells, cells.shape[dim] - width, cells.shape[dim], axis=dim)
        cells = jnp.concatenate(
            [
                lax.ppermute(tail, axis, [(i, (i + 1) % count) for i in range(ends)]),
                cells,
                lax.ppermute(head, axis, [((i + 1) % count, i) for i in range(ends)]),
            ],
            axis=dim,
        )
    return cells


def band_matrix(kernel, length):
    extent = length - kernel.shape[0] + 1
    source = lax.broadcasted_iota(jnp.int32, (length, extent), 0)
    target = lax.broadcasted_iota(jnp.int32, (length, extent), 1)
    offset = source - target
    matrix = jnp.zeros((length, extent), jnp.float32)
    for tap_id in range(kernel.shape[0]):
        matrix = matrix + jnp.where(offset == tap_id, kernel[tap_id], 0.0)
    return matrix


def valid_axis(volume, kernel, axis_id):
    matrix = band_matrix(kernel, volume.shape[axis_id])
    forms = ("zxy,zw->wxy", "zxy,xw->zwy", "zxy,yw->zxw")
    return jnp.einsum(forms[axis_id], volume, matrix, precision=lax.Precision.HIGHEST)


def valid_all(volume, kernels):
    volume = valid_axis(volume, kernels[0], 0)
    volume = valid_axis(volume, kernels[1], 1)
    return valid_axis(volume, kernels[2], 2)


def box_inside(box, start_z, start_x, start_y, count_z, count_x, count_y):
    planes = start_z + jnp.arange(count_z, dtype=jnp.int32)
    rows_x = start_x + jnp.arange(count_x, dtype=jnp.int32)
    cols_y = start_y + jnp.arange(count_y, dtype=jnp.int32)
    along_z = ((planes >= box[0]) & (planes < box[1])).astype(jnp.float32)
    along_x = ((rows_x >= box[2]) & (rows_x < box[3])).astype(jnp.float32)
    along_y = ((cols_y >= box[4]) & (cols_y < box[5])).astype(jnp.float32)
    return along_z[:, None, None] * along_x[None, :, None] * along_y[None, None, :]


def local(estimate, recorded, profiles, view_boxes):
    reach = TAPS // 2
    block_z, block_x, block_y = estimate.shape
    count_views = recorded.shape[0]
    blocks = lax.all_to_all(recorded, "by", split_axis=3, concat_axis=2, tiled=True)
    start_z = lax.axis_index("bz") * block_z
    start_x = lax.axis_index("bx") * block_x
    start_y = lax.axis_index("by") * block_y
    summed = jnp.zeros(estimate.shape, jnp.float32)
    coverage = jnp.zeros(estimate.shape, jnp.float32)
    padded_est = extended(
        estimate.astype(jnp.bfloat16), (("bz", 0), ("bx", 1), ("by", 2)), reach
    ).astype(estimate.dtype)
    for view_id in range(count_views):
        kernels = profiles[view_id]
        inside = box_inside(
            view_boxes[view_id], start_z, start_x, start_y, block_z, block_x, block_y
        )
        blurred = valid_all(padded_est, kernels)
        quotient = inside * blocks[view_id].astype(jnp.float32) / (blurred + BACKGROUND)
        padded_quot = extended(
            quotient.astype(jnp.bfloat16), (("bz", 0), ("bx", 1), ("by", 2)), reach
        ).astype(quotient.dtype)
        returned = valid_all(padded_quot, kernels[:, ::-1])
        summed = summed + inside * returned
        coverage = coverage + inside
    return estimate * summed / coverage


def solution(mesh):
    placed = (
        P(("groups", "bz"), "bx", "by"),
        P(None, ("groups", "bz"), ("bx", "by"), None),
        P(),
        P("groups", None),
    )
    return jax.shard_map(
        local,
        mesh=mesh,
        in_specs=placed,
        out_specs=P(("groups", "bz"), "bx", "by"),
        check_vma=False,
    )
```

profile of v0, /device:TPU:0, one launch (start us, length us, event | category | flops | bytes accessed | tf_op | source)
XLA Modules:
  0.0 578.0 jit_solution(10769138898373561154)
XLA Ops:
  5.5 9.6 %copy.7 = bf16[6,16,8,512]{1,2,0,3:T(8,128)(2,1)} copy(bf16[6,16,8,512]{3,2,1,0:T(8,128)(2,1)} %param.5) | data formatting | bytes 1572864 | tf_op args[1]
  15.1 8.5 %reshape.1578 = bf16[4,2,49152]{2,1,0:T(2,128)(2,1)} reshape(bf16[512,6,8,16]{3,2,1,0:T(8,128)(2,1)} %bitcast.797) | data formatting | bytes 1572864
  23.6 6.4 %all-to-all-start = ((bf16[4,2,49152]{2,1,0:T(2,128)(2,1)}), bf16[4,2,49152]{2,1,0:T(2,128)(2,1)S(1)}, u32[]{:S(2)}, u32[]{:S(2)}) async-start(bf16[4,2,49152]{2,1,0:T(2,128)(2,1)} %reshape.1578), calls=%async_computation | async-start | bytes 1572864 | tf_op jit(solution)/shard_map/all_to_all | solution.py:66
  84.8 4.8 collective-permute-start.4
  96.0 9.6 %fusion.1540 = f32[16,46,142]{2,0,1:T(8,128)S(1)} fusion(bf16[30,46,142]{2,0,1:T(8,128)(2,1)S(1)} %pad_maximum_fusion, f32[]{:T(128)} %bitcast.73, f32[]{:T(128)} %bitcast.72, f32[]{:T(128)} %bitcast.71, f32[]{:T(128)} %bitcast.70, f32[]{:T(128)} %bitcast.69, f32[]{:T(128)} %bitcast.68, f32[]{:T(128)} %bitcast.67, f32[]{:T(128)} %bitcast.66, ...), kind=kOutput, calls=%fused_computation.1259 | convolution fusion | flops 37645920 | bytes 810028 | tf_op jit(solution)/shard_map/zxy,zw->wxy/dot_general | solution.py:43
  105.6 9.7 %fusion.1537 = f32[16,46,142]{2,0,1:T(8,128)S(1)} fusion(bf16[30,46,142]{2,0,1:T(8,128)(2,1)S(1)} %pad_maximum_fusion, f32[]{:T(128)} %bitcast.181, f32[]{:T(128)} %bitcast.180, f32[]{:T(128)} %bitcast.179, f32[]{:T(128)} %bitcast.178, f32[]{:T(128)} %bitcast.177, f32[]{:T(128)} %bitcast.176, f32[]{:T(128)} %bitcast.175, f32[]{:T(128)} %bitcast.174, ...), kind=kOutput, calls=%fused_computation.1256 | convolution fusion | flops 37645920 | bytes 810028 | tf_op jit(solution)/shard_map/zxy,zw->wxy/dot_general | solution.py:43
  115.3 9.7 %fusion.1534 = f32[16,46,142]{2,0,1:T(8,128)S(1)} fusion(bf16[30,46,142]{2,0,1:T(8,128)(2,1)S(1)} %pad_maximum_fusion, f32[]{:T(128)} %bitcast.289, f32[]{:T(128)} %bitcast.288, f32[]{:T(128)} %bitcast.287, f32[]{:T(128)} %bitcast.286, f32[]{:T(128)} %bitcast.285, f32[]{:T(128)} %bitcast.284, f32[]{:T(128)} %bitcast.283, f32[]{:T(128)} %bitcast.282, ...), kind=kOutput, calls=%fused_computation.1253 | convolution fusion | flops 37645920 | bytes 810028 | tf_op jit(solution)/shard_map/zxy,zw->wxy/dot_general | solution.py:43
  125.0 9.8 %fusion.1531 = f32[16,46,142]{2,0,1:T(8,128)S(1)} fusion(bf16[30,46,142]{2,0,1:T(8,128)(2,1)S(1)} %pad_maximum_fusion, f32[]{:T(128)} %bitcast.397, f32[]{:T(128)} %bitcast.396, f32[]{:T(128)} %bitcast.395, f32[]{:T(128)} %bitcast.394, f32[]{:T(128)} %bitcast.393, f32[]{:T(128)} %bitcast.392, f32[]{:T(128)} %bitcast.391, f32[]{:T(128)} %bitcast.390, ...), kind=kOutput, calls=%fused_computation.1250 | convolution fusion | flops 37645920 | bytes 810028 | tf_op jit(solution)/shard_map/zxy,zw->wxy/dot_general | solution.py:43
  134.8 11.4 %convolution_bitcast_fusion.11 = f32[16,32,142]{2,1,0:T(8,128)} fusion(f32[16,46,142]{2,0,1:T(8,128)S(1)} %fusion.1540, f32[]{:T(128)} %bitcast.57, f32[]{:T(128)} %bitcast.56, f32[]{:T(128)} %bitcast.55, f32[]{:T(128)} %bitcast.54, f32[]{:T(128)} %bitcast.53, f32[]{:T(128)} %bitcast.52, f32[]{:T(128)} %bitcast.51, f32[]{:T(128)} %bitcast.50, f32[]{:T(128)} %bitcast.49, ...), kind=kOutput, calls=%fused_computation.11 | convolution fusion | flops 40198848 | bytes 708924 | tf_op jit(solution)/shard_map/zxy,xw->zwy/dot_general | solution.py:43
  146.2 10.3 %convolution_bitcast_fusion.9 = f32[16,32,142]{2,1,0:T(8,128)S(1)} fusion(f32[16,46,142]{2,0,1:T(8,128)S(1)} %fusion.1537, f32[]{:T(128)} %bitcast.165, f32[]{:T(128)} %bitcast.164, f32[]{:T(128)} %bitcast.163, f32[]{:T(128)} %bitcast.162, f32[]{:T(128)} %bitcast.161, f32[]{:T(128)} %bitcast.160, f32[]{:T(128)} %bitcast.159, f32[]{:T(128)} %bitcast.158, ...), kind=kOutput, calls=%fused_computation.9 | convolution fusion | flops 40198848 | bytes 708924 | tf_op jit(solution)/shard_map/zxy,xw->zwy/dot_general | solution.py:43
  156.5 10.6 %convolution_bitcast_fusion.7 = f32[16,32,142]{2,1,0:T(8,128)S(1)} fusion(f32[16,46,142]{2,0,1:T(8,128)S(1)} %fusion.1534, f32[]{:T(128)} %bitcast.273, f32[]{:T(128)} %bitcast.272, f32[]{:T(128)} %bitcast.271, f32[]{:T(128)} %bitcast.270, f32[]{:T(128)} %bitcast.269, f32[]{:T(128)} %bitcast.268, f32[]{:T(128)} %bitcast.267, f32[]{:T(128)} %bitcast.266, ...), kind=kOutput, calls=%fused_computation.7 | convolution fusion | flops 40198848 | bytes 708924 | tf_op jit(solution)/shard_map/zxy,xw->zwy/dot_general | solution.py:43
  167.1 10.2 %convolution_bitcast_fusion.5 = f32[16,32,142]{2,1,0:T(8,128)S(1)} fusion(f32[16,46,142]{2,0,1:T(8,128)S(1)} %fusion.1531, f32[]{:T(128)} %bitcast.381, f32[]{:T(128)} %bitcast.380, f32[]{:T(128)} %bitcast.379, f32[]{:T(128)} %bitcast.378, f32[]{:T(128)} %bitcast.377, f32[]{:T(128)} %bitcast.376, f32[]{:T(128)} %bitcast.375, f32[]{:T(128)} %bitcast.374, ...), kind=kOutput, calls=%fused_computation.5 | convolution fusion | flops 40198848 | bytes 708924 | tf_op jit(solution)/shard_map/zxy,xw->zwy/dot_general | solution.py:43
  177.3 9.8 %fusion.1528 = f32[16,46,142]{2,0,1:T(8,128)S(1)} fusion(bf16[30,46,142]{2,0,1:T(8,128)(2,1)S(1)} %pad_maximum_fusion, f32[]{:T(128)} %bitcast.505, f32[]{:T(128)} %bitcast.504, f32[]{:T(128)} %bitcast.503, f32[]{:T(128)} %bitcast.502, f32[]{:T(128)} %bitcast.501, f32[]{:T(128)} %bitcast.500, f32[]{:T(128)} %bitcast.499, f32[]{:T(128)} %bitcast.498, ...), kind=kOutput, calls=%fused_computation.1247 | convolution fusion | flops 37645920 | bytes 810028 | tf_op jit(solution)/shard_map/zxy,zw->wxy/dot_general | solution.py:43
  187.1 10.3 %convolution_bitcast_fusion.3 = f32[16,32,142]{2,1,0:T(8,128)S(1)} fusion(f32[16,46,142]{2,0,1:T(8,128)S(1)} %fusion.1528, f32[]{:T(128)} %bitcast.489, f32[]{:T(128)} %bitcast.488, f32[]{:T(128)} %bitcast.487, f32[]{:T(128)} %bitcast.486, f32[]{:T(128)} %bitcast.485, f32[]{:T(128)} %bitcast.484, f32[]{:T(128)} %bitcast.483, f32[]{:T(128)} %bitcast.482, ...), kind=kOutput, calls=%fused_computation.3 | convolution fusion | flops 40198848 | bytes 708924 | tf_op jit(solution)/shard_map/zxy,xw->zwy/dot_general | solution.py:43
  197.5 9.8 %fusion.1525 = f32[16,46,142]{2,0,1:T(8,128)S(1)} fusion(bf16[30,46,142]{2,0,1:T(8,128)(2,1)S(1)} %pad_maximum_fusion, f32[]{:T(128)} %bitcast.613, f32[]{:T(128)} %bitcast.612, f32[]{:T(128)} %bitcast.611, f32[]{:T(128)} %bitcast.610, f32[]{:T(128)} %bitcast.609, f32[]{:T(128)} %bitcast.608, f32[]{:T(128)} %bitcast.607, f32[]{:T(128)} %bitcast.606, ...), kind=kOutput, calls=%fused_computation.1244 | convolution fusion | flops 37645920 | bytes 810028 | tf_op jit(solution)/shard_map/zxy,zw->wxy/dot_general | solution.py:43
  207.3 10.1 %convolution_bitcast_fusion.1 = f32[16,32,142]{2,1,0:T(8,128)S(1)} fusion(f32[16,46,142]{2,0,1:T(8,128)S(1)} %fusion.1525, f32[]{:T(128)} %bitcast.597, f32[]{:T(128)} %bitcast.596, f32[]{:T(128)} %bitcast.595, f32[]{:T(128)} %bitcast.594, f32[]{:T(128)} %bitcast.593, f32[]{:T(128)} %bitcast.592, f32[]{:T(128)} %bitcast.591, f32[]{:T(128)} %bitcast.590, ...), kind=kOutput, calls=%fused_computation.1 | convolution fusion | flops 40198848 | bytes 708924 | tf_op jit(solution)/shard_map/zxy,xw->zwy/dot_general | solution.py:43
  217.4 5.9 %reshape.1579 = bf16[512,6,8,16]{3,2,1,0:T(8,128)(2,1)} reshape(bf16[4,2,49152]{2,1,0:T(2,128)(2,1)S(1)} %all-to-all-done) | data formatting | bytes 1572864
  223.3 6.6 %copy.8 = bf16[6,16,8,4,128]{4,2,3,1,0:T(8,128)(2,1)S(1)} copy(bf16[6,16,8,4,128]{1,2,0,4,3:T(8,128)(2,1)} %bitcast.796) | data formatting | bytes 1572864 | tf_op jit(solution)/shard_map/all_to_all | solution.py:66
  229.9 11.2 %fusion.13 = bf16[16,32,128]{2,1,0:T(8,128)(2,1)S(1)} fusion(f32[16,32,142]{2,1,0:T(8,128)} %convolution_bitcast_fusion.11, bf16[6,16,4,8,128]{4,3,2,1,0:T(8,128)(2,1)S(1)} %bitcast.798, f32[128]{0:T(128)S(1)} %and_convert_fusion.15, f32[16,32]{1,0:T(8,128)S(1)} %broadcast_multiply_fusion.5, f32[]{:T(128)} %bitcast.90, f32[]{:T(128)} %bitcast.89, ...), kind=kOutput, calls=%fused_computation.37 | convolution fusion | flops 112884480 | bytes 555580 | tf_op jit(solution)/shard_map/zxy,yw->zxw/dot_general | solution.py:43
  245.5 10.1 %fusion.14 = bf16[16,32,128]{2,1,0:T(8,128)(2,1)S(1)} fusion(f32[16,32,142]{2,1,0:T(8,128)S(1)} %convolution_bitcast_fusion.9, bf16[6,16,4,8,128]{4,3,2,1,0:T(8,128)(2,1)S(1)} %bitcast.799, f32[128]{0:T(128)S(1)} %get-tuple-element.658, f32[16,32]{1,0:T(8,128)S(1)} %broadcast_multiply_fusion.4, f32[]{:T(128)} %bitcast.198, f32[]{:T(128)} %bitcast.197, ...), kind=kOutput, calls=%fused_computation.38 | convolution fusion | flops 112884480 | bytes 555580 | tf_op jit(solution)/shard_map/zxy,yw->zxw/dot_general | solution.py:43
  260.0 9.8 %fusion.15 = bf16[16,32,128]{2,1,0:T(8,128)(2,1)S(1)} fusion(f32[16,32,142]{2,1,0:T(8,128)S(1)} %convolution_bitcast_fusion.7, bf16[6,16,4,8,128]{4,3,2,1,0:T(8,128)(2,1)S(1)} %bitcast.800, f32[128]{0:T(128)S(1)} %get-tuple-element.657, f32[16,32]{1,0:T(8,128)S(1)} %broadcast_multiply_fusion.3, f32[]{:T(128)} %bitcast.306, f32[]{:T(128)} %bitcast.305, ...), kind=kOutput, calls=%fused_computation.39 | convolution fusion | flops 112884480 | bytes 555580 | tf_op jit(solution)/shard_map/zxy,yw->zxw/dot_general | solution.py:43
  271.1 9.8 %fusion.16 = bf16[16,32,128]{2,1,0:T(8,128)(2,1)S(1)} fusion(f32[16,32,142]{2,1,0:T(8,128)S(1)} %convolution_bitcast_fusion.5, bf16[6,16,4,8,128]{4,3,2,1,0:T(8,128)(2,1)S(1)} %bitcast.801, f32[128]{0:T(128)S(1)} %get-tuple-element.656, f32[16,32]{1,0:T(8,128)S(1)} %broadcast_multiply_fusion.2, f32[]{:T(128)} %bitcast.414, f32[]{:T(128)} %bitcast.413, ...), kind=kOutput, calls=%fused_computation.40 | convolution fusion | flops 112884480 | bytes 555580 | tf_op jit(solution)/shard_map/zxy,yw->zxw/dot_general | solution.py:43
  281.0 10.3 %fusion.17 = bf16[16,32,128]{2,1,0:T(8,128)(2,1)S(1)} fusion(f32[16,32,142]{2,1,0:T(8,128)S(1)} %convolution_bitcast_fusion.3, bf16[6,16,4,8,128]{4,3,2,1,0:T(8,128)(2,1)S(1)} %bitcast.802, f32[128]{0:T(128)S(1)} %get-tuple-element.655, f32[16,32]{1,0:T(8,128)S(1)} %broadcast_multiply_fusion.1, f32[]{:T(128)} %bitcast.522, f32[]{:T(128)} %bitcast.521, ...), kind=kOutput, calls=%fused_computation.41 | convolution fusion | flops 112884480 | bytes 555580 | tf_op jit(solution)/shard_map/zxy,yw->zxw/dot_general | solution.py:43
  291.3 9.6 %fusion.18 = bf16[16,32,128]{2,1,0:T(8,128)(2,1)S(1)} fusion(f32[16,32,142]{2,1,0:T(8,128)S(1)} %convolution_bitcast_fusion.1, bf16[6,16,4,8,128]{4,3,2,1,0:T(8,128)(2,1)S(1)} %bitcast.803, f32[128]{0:T(128)S(1)} %and_convert_fusion, f32[16,32]{1,0:T(8,128)S(1)} %broadcast_multiply_fusion, f32[]{:T(128)} %bitcast.630, f32[]{:T(128)} %bitcast.629, ...), kind=kOutput, calls=%fused_computation.42 | convolution fusion | flops 112884480 | bytes 555580 | tf_op jit(solution)/shard_map/zxy,yw->zxw/dot_general | solution.py:43
  355.1 5.0 collective-permute-start.10
  361.8 4.6 collective-permute-start.16
  368.0 4.6 collective-permute-start.22
  375.1 9.9 %fusion.41 = f32[16,46,142]{2,0,1:T(8,128)S(1)} fusion(bf16[30,46,142]{2,1,0:T(8,128)(2,1)S(1)} %pad_maximum_fusion.1, f32[]{:T(128)} %bitcast.38, f32[]{:T(128)} %bitcast.37, f32[]{:T(128)} %bitcast.36, f32[]{:T(128)} %bitcast.35, f32[]{:T(128)} %bitcast.34, f32[]{:T(128)} %bitcast.33, f32[]{:T(128)} %bitcast.32, f32[]{:T(128)} %bitcast.31, f32[]{:T(128)} %bitcast.30, ...), kind=kOutput, calls=%fused_computation.66 | convolution fusion | flops 37645920 | bytes 810028 | tf_op jit(solution)/shard_map/zxy,zw->wxy/dot_general | solution.py:43
  385.1 10.4 %convolution_bitcast_fusion.10 = f32[16,32,142]{2,1,0:T(8,128)S(1)} fusion(f32[16,46,142]{2,0,1:T(8,128)S(1)} %fusion.41, f32[]{:T(128)} %bitcast.21, f32[]{:T(128)} %bitcast.20, f32[]{:T(128)} %bitcast.19, f32[]{:T(128)} %bitcast.18, f32[]{:T(128)} %bitcast.17, f32[]{:T(128)} %bitcast.16, f32[]{:T(128)} %bitcast.15, f32[]{:T(128)} %bitcast.14, ...), kind=kOutput, calls=%fused_computation.10 | convolution fusion | flops 40198848 | bytes 708924 | tf_op jit(solution)/shard_map/zxy,xw->zwy/dot_general | solution.py:43
  395.5 4.6 collective-permute-start.28
  402.1 9.9 %fusion.39 = f32[16,46,142]{2,0,1:T(8,128)S(1)} fusion(bf16[30,46,142]{2,1,0:T(8,128)(2,1)S(1)} %pad_maximum_fusion.2, f32[]{:T(128)} %bitcast.148, f32[]{:T(128)} %bitcast.147, f32[]{:T(128)} %bitcast.146, f32[]{:T(128)} %bitcast.145, f32[]{:T(128)} %bitcast.144, f32[]{:T(128)} %bitcast.143, f32[]{:T(128)} %bitcast.142, f32[]{:T(128)} %bitcast.141, ...), kind=kOutput, calls=%fused_computation.64 | convolution fusion | flops 37645920 | bytes 810028 | tf_op jit(solution)/shard_map/zxy,zw->wxy/dot_general | solution.py:43
  412.1 10.3 %convolution_bitcast_fusion.8 = f32[16,32,142]{2,1,0:T(8,128)S(1)} fusion(f32[16,46,142]{2,0,1:T(8,128)S(1)} %fusion.39, f32[]{:T(128)} %bitcast.131, f32[]{:T(128)} %bitcast.130, f32[]{:T(128)} %bitcast.129, f32[]{:T(128)} %bitcast.128, f32[]{:T(128)} %bitcast.127, f32[]{:T(128)} %bitcast.126, f32[]{:T(128)} %bitcast.125, f32[]{:T(128)} %bitcast.124, ...), kind=kOutput, calls=%fused_computation.8 | convolution fusion | flops 40198848 | bytes 708924 | tf_op jit(solution)/shard_map/zxy,xw->zwy/dot_general | solution.py:43
  422.3 4.6 collective-permute-start.34
  428.9 9.8 %fusion.37 = f32[16,46,142]{2,0,1:T(8,128)S(1)} fusion(bf16[30,46,142]{2,1,0:T(8,128)(2,1)S(1)} %pad_maximum_fusion.3, f32[]{:T(128)} %bitcast.256, f32[]{:T(128)} %bitcast.255, f32[]{:T(128)} %bitcast.254, f32[]{:T(128)} %bitcast.253, f32[]{:T(128)} %bitcast.252, f32[]{:T(128)} %bitcast.251, f32[]{:T(128)} %bitcast.250, f32[]{:T(128)} %bitcast.249, ...), kind=kOutput, calls=%fused_computation.62 | convolution fusion | flops 37645920 | bytes 810028 | tf_op jit(solution)/shard_map/zxy,zw->wxy/dot_general | solution.py:43
  438.7 10.0 %convolution_bitcast_fusion.6 = f32[16,32,142]{2,1,0:T(8,128)S(1)} fusion(f32[16,46,142]{2,0,1:T(8,128)S(1)} %fusion.37, f32[]{:T(128)} %bitcast.239, f32[]{:T(128)} %bitcast.238, f32[]{:T(128)} %bitcast.237, f32[]{:T(128)} %bitcast.236, f32[]{:T(128)} %bitcast.235, f32[]{:T(128)} %bitcast.234, f32[]{:T(128)} %bitcast.233, f32[]{:T(128)} %bitcast.232, ...), kind=kOutput, calls=%fused_computation.6 | convolution fusion | flops 40198848 | bytes 708924 | tf_op jit(solution)/shard_map/zxy,xw->zwy/dot_general | solution.py:43
  448.8 4.7 collective-permute-start.40
  454.2 9.9 %fusion.35 = f32[16,46,142]{2,0,1:T(8,128)S(1)} fusion(bf16[30,46,142]{2,1,0:T(8,128)(2,1)S(1)} %pad_maximum_fusion.4, f32[]{:T(128)} %bitcast.364, f32[]{:T(128)} %bitcast.363, f32[]{:T(128)} %bitcast.362, f32[]{:T(128)} %bitcast.361, f32[]{:T(128)} %bitcast.360, f32[]{:T(128)} %bitcast.359, f32[]{:T(128)} %bitcast.358, f32[]{:T(128)} %bitcast.357, ...), kind=kOutput, calls=%fused_computation.60 | convolution fusion | flops 37645920 | bytes 810028 | tf_op jit(solution)/shard_map/zxy,zw->wxy/dot_general | solution.py:43
  464.2 10.3 %convolution_bitcast_fusion.4 = f32[16,32,142]{2,1,0:T(8,128)S(1)} fusion(f32[16,46,142]{2,0,1:T(8,128)S(1)} %fusion.35, f32[]{:T(128)} %bitcast.347, f32[]{:T(128)} %bitcast.346, f32[]{:T(128)} %bitcast.345, f32[]{:T(128)} %bitcast.344, f32[]{:T(128)} %bitcast.343, f32[]{:T(128)} %bitcast.342, f32[]{:T(128)} %bitcast.341, f32[]{:T(128)} %bitcast.340, ...), kind=kOutput, calls=%fused_computation.4 | convolution fusion | flops 40198848 | bytes 708924 | tf_op jit(solution)/shard_map/zxy,xw->zwy/dot_general | solution.py:43
  475.2 10.1 %fusion.33 = f32[16,46,142]{2,0,1:T(8,128)S(1)} fusion(bf16[30,46,142]{2,1,0:T(8,128)(2,1)S(1)} %pad_maximum_fusion.5, f32[]{:T(128)} %bitcast.472, f32[]{:T(128)} %bitcast.471, f32[]{:T(128)} %bitcast.470, f32[]{:T(128)} %bitcast.469, f32[]{:T(128)} %bitcast.468, f32[]{:T(128)} %bitcast.467, f32[]{:T(128)} %bitcast.466, f32[]{:T(128)} %bitcast.465, ...), kind=kOutput, calls=%fused_computation.58 | convolution fusion | flops 37645920 | bytes 810028 | tf_op jit(solution)/shard_map/zxy,zw->wxy/dot_general | solution.py:43
  485.3 10.7 %convolution_bitcast_fusion.2 = f32[16,32,142]{2,1,0:T(8,128)S(1)} fusion(f32[16,46,142]{2,0,1:T(8,128)S(1)} %fusion.33, f32[]{:T(128)} %bitcast.455, f32[]{:T(128)} %bitcast.454, f32[]{:T(128)} %bitcast.453, f32[]{:T(128)} %bitcast.452, f32[]{:T(128)} %bitcast.451, f32[]{:T(128)} %bitcast.450, f32[]{:T(128)} %bitcast.449, f32[]{:T(128)} %bitcast.448, ...), kind=kOutput, calls=%fused_computation.2 | convolution fusion | flops 40198848 | bytes 708924 | tf_op jit(solution)/shard_map/zxy,xw->zwy/dot_general | solution.py:43
  496.0 9.9 %convolution_multiply_fusion.5 = f32[16,32,128]{2,1,0:T(8,128)S(1)} fusion(f32[16,32,142]{2,1,0:T(8,128)S(1)} %convolution_bitcast_fusion.10, f32[128]{0:T(128)S(1)} %and_convert_fusion.15, f32[16,32]{1,0:T(8,128)S(1)} %broadcast_multiply_fusion.5, f32[]{:T(128)} %bitcast.108, f32[]{:T(128)} %bitcast.107, f32[]{:T(128)} %bitcast.106, f32[]{:T(128)} %bitcast.105, ...), kind=kOutput, calls=%fused_computation.32 | convolution fusion | flops 112622336 | bytes 555580 | tf_op jit(solution)/shard_map/zxy,yw->zxw/dot_general | solution.py:43
  506.6 10.2 %fusion.31 = f32[16,46,142]{2,0,1:T(8,128)S(1)} fusion(bf16[30,46,142]{2,1,0:T(8,128)(2,1)S(1)} %pad_maximum_fusion.6, f32[]{:T(128)} %bitcast.580, f32[]{:T(128)} %bitcast.579, f32[]{:T(128)} %bitcast.578, f32[]{:T(128)} %bitcast.577, f32[]{:T(128)} %bitcast.576, f32[]{:T(128)} %bitcast.575, f32[]{:T(128)} %bitcast.574, f32[]{:T(128)} %bitcast.573, ...), kind=kOutput, calls=%fused_computation.56 | convolution fusion | flops 37645920 | bytes 810028 | tf_op jit(solution)/shard_map/zxy,zw->wxy/dot_general | solution.py:43
  516.8 10.4 %convolution_bitcast_fusion = f32[16,32,142]{2,1,0:T(8,128)S(1)} fusion(f32[16,46,142]{2,0,1:T(8,128)S(1)} %fusion.31, f32[]{:T(128)} %bitcast.563, f32[]{:T(128)} %bitcast.562, f32[]{:T(128)} %bitcast.561, f32[]{:T(128)} %bitcast.560, f32[]{:T(128)} %bitcast.559, f32[]{:T(128)} %bitcast.558, f32[]{:T(128)} %bitcast.557, f32[]{:T(128)} %bitcast.556, ...), kind=kOutput, calls=%fused_computation | convolution fusion | flops 40198848 | bytes 708924 | tf_op jit(solution)/shard_map/zxy,xw->zwy/dot_general | solution.py:43
  527.2 10.0 %fusion.8 = f32[16,32,128]{2,1,0:T(8,128)S(1)} fusion(f32[16,32,128]{2,1,0:T(8,128)S(1)} %convolution_multiply_fusion.5, f32[16,32,142]{2,1,0:T(8,128)S(1)} %convolution_bitcast_fusion.8, f32[128]{0:T(128)S(1)} %get-tuple-element.658, f32[16,32]{1,0:T(8,128)S(1)} %broadcast_multiply_fusion.4, f32[]{:T(128)} %bitcast.216, f32[]{:T(128)} %bitcast.215, ...), kind=kOutput, calls=%fused_computation.29 | convolution fusion | flops 112687872 | bytes 817724 | tf_op jit(solution)/shard_map/zxy,yw->zxw/dot_general | solution.py:43
  537.2 9.9 %fusion.6 = f32[16,32,128]{2,1,0:T(8,128)S(1)} fusion(f32[16,32,128]{2,1,0:T(8,128)S(1)} %fusion.8, f32[16,32,142]{2,1,0:T(8,128)S(1)} %convolution_bitcast_fusion.6, f32[128]{0:T(128)S(1)} %get-tuple-element.657, f32[16,32]{1,0:T(8,128)S(1)} %broadcast_multiply_fusion.3, f32[]{:T(128)} %bitcast.324, f32[]{:T(128)} %bitcast.323, f32[]{:T(128)} %bitcast.322, ...), kind=kOutput, calls=%fused_computation.25 | convolution fusion | flops 112687872 | bytes 817724 | tf_op jit(solution)/shard_map/zxy,yw->zxw/dot_general | solution.py:43
  547.1 10.1 %fusion.4 = f32[16,32,128]{2,1,0:T(8,128)S(1)} fusion(f32[16,32,128]{2,1,0:T(8,128)S(1)} %fusion.6, f32[16,32,142]{2,1,0:T(8,128)S(1)} %convolution_bitcast_fusion.4, f32[128]{0:T(128)S(1)} %get-tuple-element.656, f32[16,32]{1,0:T(8,128)S(1)} %broadcast_multiply_fusion.2, f32[]{:T(128)} %bitcast.432, f32[]{:T(128)} %bitcast.431, f32[]{:T(128)} %bitcast.430, ...), kind=kOutput, calls=%fused_computation.21 | convolution fusion | flops 112687872 | bytes 817724 | tf_op jit(solution)/shard_map/zxy,yw->zxw/dot_general | solution.py:43
  557.2 9.9 %fusion.2 = f32[16,32,128]{2,1,0:T(8,128)S(1)} fusion(f32[16,32,128]{2,1,0:T(8,128)S(1)} %fusion.4, f32[16,32,142]{2,1,0:T(8,128)S(1)} %convolution_bitcast_fusion.2, f32[128]{0:T(128)S(1)} %get-tuple-element.655, f32[16,32]{1,0:T(8,128)S(1)} %broadcast_multiply_fusion.1, f32[]{:T(128)} %bitcast.540, f32[]{:T(128)} %bitcast.539, f32[]{:T(128)} %bitcast.538, ...), kind=kOutput, calls=%fused_computation.17 | convolution fusion | flops 112687872 | bytes 817724 | tf_op jit(solution)/shard_map/zxy,yw->zxw/dot_general | solution.py:43
  567.2 10.7 %fusion.12 = f32[16,32,128]{2,1,0:T(8,128)} fusion(f32[16,32,128]{2,1,0:T(8,128)S(1)} %copy-done.1, f32[16,32,128]{2,1,0:T(8,128)S(1)} %fusion.2, f32[16,32,142]{2,1,0:T(8,128)S(1)} %convolution_bitcast_fusion, f32[128]{0:T(128)S(1)} %and_convert_fusion, f32[16,32]{1,0:T(8,128)S(1)} %broadcast_multiply_fusion, f32[128]{0:T(128)S(1)} %get-tuple-element.655, ...), kind=kOutput, calls=%fused_computation.36 | convolution fusion | flops 113474304 | bytes 1092668 | tf_op jit(solution)/shard_map/zxy,yw->zxw/dot_general | solution.py:43
  (174 shorter events, 142.0 us)
Async XLA Ops:
  1.1 74.3 %collective-permute-start.1 = (bf16[7,32,128]{2,0,1:T(8,128)(2,1)S(1)}, bf16[7,32,128]{2,0,1:T(8,128)(2,1)S(1)}, u32[]{:S(2)}, u32[]{:S(2)}) collective-permute-start(bf16[7,32,128]{2,0,1:T(8,128)(2,1)S(1)} %get-tuple-element.46), channel_id=1, source_target_pairs={{1,0},{3,2},{5,4},{7,6},{9,8},{11,10},{13,12},{15,14},{17,16},{19,... | collective-permute-start | bytes 172040 | tf_op jit(solution)/shard_map/ppermute | solution.py:22
  2.4 73.0 %collective-permute-start = (bf16[7,32,128]{2,0,1:T(8,128)(2,1)S(1)}, bf16[7,32,128]{2,0,1:T(8,128)(2,1)S(1)}, u32[]{:S(2)}, u32[]{:S(2)}) collective-permute-start(bf16[7,32,128]{2,0,1:T(8,128)(2,1)S(1)} %get-tuple-element.45), channel_id=1, source_target_pairs={{0,1},{2,3},{4,5},{6,7},{8,9},{10,11},{12,13},{14,15},{16,17},{18,... | collective-permute-start | bytes 172040 | tf_op jit(solution)/shard_map/ppermute | solution.py:20
  23.6 6.5 %copy-start = (f32[6,3,15]{2,1,0:T(4,128)S(1)}, f32[6,3,15]{2,1,0:T(4,128)}, u32[]{:S(2)}) copy-start(f32[6,3,15]{2,1,0:T(4,128)} %param.6) | copy-start | bytes 3244
  23.6 10.0 %copy-start.2 = (s32[6,6]{1,0:T(8,128)S(1)}, s32[6,6]{1,0:T(8,128)}, u32[]{:S(2)}) copy-start(s32[6,6]{1,0:T(8,128)} %param.7) | copy-start | bytes 436
  23.6 193.8 %all-to-all-start = ((bf16[4,2,49152]{2,1,0:T(2,128)(2,1)}), bf16[4,2,49152]{2,1,0:T(2,128)(2,1)S(1)}, u32[]{:S(2)}, u32[]{:S(2)}) async-start(bf16[4,2,49152]{2,1,0:T(2,128)(2,1)} %reshape.1578), calls=%async_computation | async-start | bytes 1572864 | tf_op jit(solution)/shard_map/all_to_all | solution.py:66
  75.5 7.2 %collective-permute-start.3 = (bf16[30,7,128]{2,0,1:T(8,128)(2,1)S(1)}, bf16[30,7,128]{2,0,1:T(8,128)(2,1)S(1)}, u32[]{:S(2)}, u32[]{:S(2)}) collective-permute-start(bf16[30,7,128]{2,0,1:T(8,128)(2,1)S(1)} %get-tuple-element.20), channel_id=1, source_target_pairs={{2,0},{3,1},{6,4},{7,5},{10,8},{11,9},{14,12},{15,13},{18,16},{19,... | collective-permute-start | bytes 161288 | tf_op jit(solution)/shard_map/ppermute | solution.py:22
  76.8 6.4 %collective-permute-start.2 = (bf16[30,7,128]{2,0,1:T(8,128)(2,1)S(1)}, bf16[30,7,128]{2,0,1:T(8,128)(2,1)S(1)}, u32[]{:S(2)}, u32[]{:S(2)}) collective-permute-start(bf16[30,7,128]{2,0,1:T(8,128)(2,1)S(1)} %get-tuple-element.19), channel_id=1, source_target_pairs={{0,2},{1,3},{4,6},{5,7},{8,10},{9,11},{12,14},{13,15},{16,18},{17,... | collective-permute-start | bytes 161288 | tf_op jit(solution)/shard_map/ppermute | solution.py:20
  83.5 10.6 %collective-permute-start.5 = (bf16[30,46,7]{2,0,1:T(8,128)(2,1)S(1)}, bf16[30,46,7]{2,0,1:T(8,128)(2,1)S(1)}, u32[]{:S(2)}, u32[]{:S(2)}) collective-permute-start(bf16[30,46,7]{2,0,1:T(8,128)(2,1)S(1)} %get-tuple-element.6), channel_id=1, source_target_pairs={{4,0},{8,4},{12,8},{5,1},{9,5},{13,9},{6,2},{10,6},{14,10},{7,3},{... | collective-permute-start | bytes 57968 | tf_op jit(solution)/shard_map/ppermute | solution.py:22
  84.8 10.5 %collective-permute-start.4 = (bf16[30,46,7]{2,0,1:T(8,128)(2,1)S(1)}, bf16[30,46,7]{2,0,1:T(8,128)(2,1)S(1)}, u32[]{:S(2)}, u32[]{:S(2)}) collective-permute-start(bf16[30,46,7]{2,0,1:T(8,128)(2,1)S(1)} %get-tuple-element.5), channel_id=1, source_target_pairs={{0,4},{4,8},{8,12},{1,5},{5,9},{9,13},{2,6},{6,10},{10,14},{3,7},{... | collective-permute-start | bytes 57968 | tf_op jit(solution)/shard_map/ppermute | solution.py:20
  241.2 59.7 %collective-permute-start.7 = (bf16[7,32,128]{2,1,0:T(8,128)(2,1)S(1)}, bf16[7,32,128]{2,1,0:T(8,128)(2,1)S(1)}, u32[]{:S(2)}, u32[]{:S(2)}) collective-permute-start(bf16[7,32,128]{2,1,0:T(8,128)(2,1)S(1)} %get-tuple-element.44), channel_id=1, source_target_pairs={{1,0},{3,2},{5,4},{7,6},{9,8},{11,10},{13,12},{15,14},{17,16},{19,... | collective-permute-start | bytes 172040 | tf_op jit(solution)/shard_map/ppermute | solution.py:22
  242.5 61.5 %collective-permute-start.6 = (bf16[7,32,128]{2,1,0:T(8,128)(2,1)S(1)}, bf16[7,32,128]{2,1,0:T(8,128)(2,1)S(1)}, u32[]{:S(2)}, u32[]{:S(2)}) collective-permute-start(bf16[7,32,128]{2,1,0:T(8,128)(2,1)S(1)} %get-tuple-element.43), channel_id=1, source_target_pairs={{0,1},{2,3},{4,5},{6,7},{8,9},{10,11},{12,13},{14,15},{16,17},{18,... | collective-permute-start | bytes 172040 | tf_op jit(solution)/shard_map/ppermute | solution.py:20
  255.6 49.7 %collective-permute-start.13 = (bf16[7,32,128]{2,1,0:T(8,128)(2,1)S(1)}, bf16[7,32,128]{2,1,0:T(8,128)(2,1)S(1)}, u32[]{:S(2)}, u32[]{:S(2)}) collective-permute-start(bf16[7,32,128]{2,1,0:T(8,128)(2,1)S(1)} %get-tuple-element.42), channel_id=1, source_target_pairs={{1,0},{3,2},{5,4},{7,6},{9,8},{11,10},{13,12},{15,14},{17,16},{19,... | collective-permute-start | bytes 172040 | tf_op jit(solution)/shard_map/ppermute | solution.py:22
  256.9 51.4 %collective-permute-start.12 = (bf16[7,32,128]{2,1,0:T(8,128)(2,1)S(1)}, bf16[7,32,128]{2,1,0:T(8,128)(2,1)S(1)}, u32[]{:S(2)}, u32[]{:S(2)}) collective-permute-start(bf16[7,32,128]{2,1,0:T(8,128)(2,1)S(1)} %get-tuple-element.41), channel_id=1, source_target_pairs={{0,1},{2,3},{4,5},{6,7},{8,9},{10,11},{12,13},{14,15},{16,17},{18,... | collective-permute-start | bytes 172040 | tf_op jit(solution)/shard_map/ppermute | solution.py:20
  269.8 39.9 %collective-permute-start.19 = (bf16[7,32,128]{2,1,0:T(8,128)(2,1)S(1)}, bf16[7,32,128]{2,1,0:T(8,128)(2,1)S(1)}, u32[]{:S(2)}, u32[]{:S(2)}) collective-permute-start(bf16[7,32,128]{2,1,0:T(8,128)(2,1)S(1)} %get-tuple-element.40), channel_id=1, source_target_pairs={{1,0},{3,2},{5,4},{7,6},{9,8},{11,10},{13,12},{15,14},{17,16},{19,... | collective-permute-start | bytes 172040 | tf_op jit(solution)/shard_map/ppermute | solution.py:22
  300.9 11.8 %collective-permute-start.18 = (bf16[7,32,128]{2,1,0:T(8,128)(2,1)S(1)}, bf16[7,32,128]{2,1,0:T(8,128)(2,1)S(1)}, u32[]{:S(2)}, u32[]{:S(2)}) collective-permute-start(bf16[7,32,128]{2,1,0:T(8,128)(2,1)S(1)} %get-tuple-element.39), channel_id=1, source_target_pairs={{0,1},{2,3},{4,5},{6,7},{8,9},{10,11},{12,13},{14,15},{16,17},{18,... | collective-permute-start | bytes 172040 | tf_op jit(solution)/shard_map/ppermute | solution.py:20
  304.0 10.1 %collective-permute-start.25 = (bf16[7,32,128]{2,1,0:T(8,128)(2,1)S(1)}, bf16[7,32,128]{2,1,0:T(8,128)(2,1)S(1)}, u32[]{:S(2)}, u32[]{:S(2)}) collective-permute-start(bf16[7,32,128]{2,1,0:T(8,128)(2,1)S(1)} %get-tuple-element.38), channel_id=1, source_target_pairs={{1,0},{3,2},{5,4},{7,6},{9,8},{11,10},{13,12},{15,14},{17,16},{19,... | collective-permute-start | bytes 172040 | tf_op jit(solution)/shard_map/ppermute | solution.py:22
  305.3 11.8 %collective-permute-start.24 = (bf16[7,32,128]{2,1,0:T(8,128)(2,1)S(1)}, bf16[7,32,128]{2,1,0:T(8,128)(2,1)S(1)}, u32[]{:S(2)}, u32[]{:S(2)}) collective-permute-start(bf16[7,32,128]{2,1,0:T(8,128)(2,1)S(1)} %get-tuple-element.37), channel_id=1, source_target_pairs={{0,1},{2,3},{4,5},{6,7},{8,9},{10,11},{12,13},{14,15},{16,17},{18,... | collective-permute-start | bytes 172040 | tf_op jit(solution)/shard_map/ppermute | solution.py:20
  308.4 10.1 %collective-permute-start.31 = (bf16[7,32,128]{2,1,0:T(8,128)(2,1)S(1)}, bf16[7,32,128]{2,1,0:T(8,128)(2,1)S(1)}, u32[]{:S(2)}, u32[]{:S(2)}) collective-permute-start(bf16[7,32,128]{2,1,0:T(8,128)(2,1)S(1)} %get-tuple-element.36), channel_id=1, source_target_pairs={{1,0},{3,2},{5,4},{7,6},{9,8},{11,10},{13,12},{15,14},{17,16},{19,... | collective-permute-start | bytes 172040 | tf_op jit(solution)/shard_map/ppermute | solution.py:22
  309.7 13.4 %collective-permute-start.30 = (bf16[7,32,128]{2,1,0:T(8,128)(2,1)S(1)}, bf16[7,32,128]{2,1,0:T(8,128)(2,1)S(1)}, u32[]{:S(2)}, u32[]{:S(2)}) collective-permute-start(bf16[7,32,128]{2,1,0:T(8,128)(2,1)S(1)} %get-tuple-element.35), channel_id=1, source_target_pairs={{0,1},{2,3},{4,5},{6,7},{8,9},{10,11},{12,13},{14,15},{16,17},{18,... | collective-permute-start | bytes 172040 | tf_op jit(solution)/shard_map/ppermute | solution.py:20
  312.8 11.7 %collective-permute-start.37 = (bf16[7,32,128]{2,1,0:T(8,128)(2,1)S(1)}, bf16[7,32,128]{2,1,0:T(8,128)(2,1)S(1)}, u32[]{:S(2)}, u32[]{:S(2)}) collective-permute-start(bf16[7,32,128]{2,1,0:T(8,128)(2,1)S(1)} %get-tuple-element.34), channel_id=1, source_target_pairs={{1,0},{3,2},{5,4},{7,6},{9,8},{11,10},{13,12},{15,14},{17,16},{19,... | collective-permute-start | bytes 172040 | tf_op jit(solution)/shard_map/ppermute | solution.py:22
  314.1 14.9 %collective-permute-start.36 = (bf16[7,32,128]{2,1,0:T(8,128)(2,1)S(1)}, bf16[7,32,128]{2,1,0:T(8,128)(2,1)S(1)}, u32[]{:S(2)}, u32[]{:S(2)}) collective-permute-start(bf16[7,32,128]{2,1,0:T(8,128)(2,1)S(1)} %get-tuple-element.33), channel_id=1, source_target_pairs={{0,1},{2,3},{4,5},{6,7},{8,9},{10,11},{12,13},{14,15},{16,17},{18,... | collective-permute-start | bytes 172040 | tf_op jit(solution)/shard_map/ppermute | solution.py:20
  317.1 13.2 %collective-permute-start.9 = (bf16[30,7,128]{2,1,0:T(8,128)(2,1)S(1)}, bf16[30,7,128]{2,1,0:T(8,128)(2,1)S(1)}, u32[]{:S(2)}, u32[]{:S(2)}) collective-permute-start(bf16[30,7,128]{2,1,0:T(8,128)(2,1)S(1)} %get-tuple-element.32), channel_id=1, source_target_pairs={{2,0},{3,1},{6,4},{7,5},{10,8},{11,9},{14,12},{15,13},{18,16},{19,... | collective-permute-start | bytes 161288 | tf_op jit(solution)/shard_map/ppermute | solution.py:22
  318.5 16.4 %collective-permute-start.8 = (bf16[30,7,128]{2,1,0:T(8,128)(2,1)S(1)}, bf16[30,7,128]{2,1,0:T(8,128)(2,1)S(1)}, u32[]{:S(2)}, u32[]{:S(2)}) collective-permute-start(bf16[30,7,128]{2,1,0:T(8,128)(2,1)S(1)} %get-tuple-element.31), channel_id=1, source_target_pairs={{0,2},{1,3},{4,6},{5,7},{8,10},{9,11},{12,14},{13,15},{16,18},{17,... | collective-permute-start | bytes 161288 | tf_op jit(solution)/shard_map/ppermute | solution.py:20
  323.1 13.5 %collective-permute-start.15 = (bf16[30,7,128]{2,1,0:T(8,128)(2,1)S(1)}, bf16[30,7,128]{2,1,0:T(8,128)(2,1)S(1)}, u32[]{:S(2)}, u32[]{:S(2)}) collective-permute-start(bf16[30,7,128]{2,1,0:T(8,128)(2,1)S(1)} %get-tuple-element.30), channel_id=1, source_target_pairs={{2,0},{3,1},{6,4},{7,5},{10,8},{11,9},{14,12},{15,13},{18,16},{19,... | collective-permute-start | bytes 161288 | tf_op jit(solution)/shard_map/ppermute | solution.py:22
  324.4 16.7 %collective-permute-start.14 = (bf16[30,7,128]{2,1,0:T(8,128)(2,1)S(1)}, bf16[30,7,128]{2,1,0:T(8,128)(2,1)S(1)}, u32[]{:S(2)}, u32[]{:S(2)}) collective-permute-start(bf16[30,7,128]{2,1,0:T(8,128)(2,1)S(1)} %get-tuple-element.29), channel_id=1, source_target_pairs={{0,2},{1,3},{4,6},{5,7},{8,10},{9,11},{12,14},{13,15},{16,18},{17,... | collective-permute-start | bytes 161288 | tf_op jit(solution)/shard_map/ppermute | solution.py:20
  329.0 13.7 %collective-permute-start.21 = (bf16[30,7,128]{2,1,0:T(8,128)(2,1)S(1)}, bf16[30,7,128]{2,1,0:T(8,128)(2,1)S(1)}, u32[]{:S(2)}, u32[]{:S(2)}) collective-permute-start(bf16[30,7,128]{2,1,0:T(8,128)(2,1)S(1)} %get-tuple-element.28), channel_id=1, source_target_pairs={{2,0},{3,1},{6,4},{7,5},{10,8},{11,9},{14,12},{15,13},{18,16},{19,... | collective-permute-start | bytes 161288 | tf_op jit(solution)/shard_map/ppermute | solution.py:22
  330.3 17.0 %collective-permute-start.20 = (bf16[30,7,128]{2,1,0:T(8,128)(2,1)S(1)}, bf16[30,7,128]{2,1,0:T(8,128)(2,1)S(1)}, u32[]{:S(2)}, u32[]{:S(2)}) collective-permute-start(bf16[30,7,128]{2,1,0:T(8,128)(2,1)S(1)} %get-tuple-element.27), channel_id=1, source_target_pairs={{0,2},{1,3},{4,6},{5,7},{8,10},{9,11},{12,14},{13,15},{16,18},{17,... | collective-permute-start | bytes 161288 | tf_op jit(solution)/shard_map/ppermute | solution.py:20
  334.9 14.0 %collective-permute-start.27 = (bf16[30,7,128]{2,1,0:T(8,128)(2,1)S(1)}, bf16[30,7,128]{2,1,0:T(8,128)(2,1)S(1)}, u32[]{:S(2)}, u32[]{:S(2)}) collective-permute-start(bf16[30,7,128]{2,1,0:T(8,128)(2,1)S(1)} %get-tuple-element.26), channel_id=1, source_target_pairs={{2,0},{3,1},{6,4},{7,5},{10,8},{11,9},{14,12},{15,13},{18,16},{19,... | collective-permute-start | bytes 161288 | tf_op jit(solution)/shard_map/ppermute | solution.py:22
  336.5 17.0 %collective-permute-start.26 = (bf16[30,7,128]{2,1,0:T(8,128)(2,1)S(1)}, bf16[30,7,128]{2,1,0:T(8,128)(2,1)S(1)}, u32[]{:S(2)}, u32[]{:S(2)}) collective-permute-start(bf16[30,7,128]{2,1,0:T(8,128)(2,1)S(1)} %get-tuple-element.25), channel_id=1, source_target_pairs={{0,2},{1,3},{4,6},{5,7},{8,10},{9,11},{12,14},{13,15},{16,18},{17,... | collective-permute-start | bytes 161288 | tf_op jit(solution)/shard_map/ppermute | solution.py:20
  341.1 14.0 %collective-permute-start.33 = (bf16[30,7,128]{2,1,0:T(8,128)(2,1)S(1)}, bf16[30,7,128]{2,1,0:T(8,128)(2,1)S(1)}, u32[]{:S(2)}, u32[]{:S(2)}) collective-permute-start(bf16[30,7,128]{2,1,0:T(8,128)(2,1)S(1)} %get-tuple-element.24), channel_id=1, source_target_pairs={{2,0},{3,1},{6,4},{7,5},{10,8},{11,9},{14,12},{15,13},{18,16},{19,... | collective-permute-start | bytes 161288 | tf_op jit(solution)/shard_map/ppermute | solution.py:22
  342.7 17.5 %collective-permute-start.32 = (bf16[30,7,128]{2,1,0:T(8,128)(2,1)S(1)}, bf16[30,7,128]{2,1,0:T(8,128)(2,1)S(1)}, u32[]{:S(2)}, u32[]{:S(2)}) collective-permute-start(bf16[30,7,128]{2,1,0:T(8,128)(2,1)S(1)} %get-tuple-element.23), channel_id=1, source_target_pairs={{0,2},{1,3},{4,6},{5,7},{8,10},{9,11},{12,14},{13,15},{16,18},{17,... | collective-permute-start | bytes 161288 | tf_op jit(solution)/shard_map/ppermute | solution.py:20
  347.3 14.5 %collective-permute-start.39 = (bf16[30,7,128]{2,1,0:T(8,128)(2,1)S(1)}, bf16[30,7,128]{2,1,0:T(8,128)(2,1)S(1)}, u32[]{:S(2)}, u32[]{:S(2)}) collective-permute-start(bf16[30,7,128]{2,1,0:T(8,128)(2,1)S(1)} %get-tuple-element.22), channel_id=1, source_target_pairs={{2,0},{3,1},{6,4},{7,5},{10,8},{11,9},{14,12},{15,13},{18,16},{19,... | collective-permute-start | bytes 161288 | tf_op jit(solution)/shard_map/ppermute | solution.py:22
  348.9 17.5 %collective-permute-start.38 = (bf16[30,7,128]{2,1,0:T(8,128)(2,1)S(1)}, bf16[30,7,128]{2,1,0:T(8,128)(2,1)S(1)}, u32[]{:S(2)}, u32[]{:S(2)}) collective-permute-start(bf16[30,7,128]{2,1,0:T(8,128)(2,1)S(1)} %get-tuple-element.21), channel_id=1, source_target_pairs={{0,2},{1,3},{4,6},{5,7},{8,10},{9,11},{12,14},{13,15},{16,18},{17,... | collective-permute-start | bytes 161288 | tf_op jit(solution)/shard_map/ppermute | solution.py:20
  353.5 14.5 %collective-permute-start.11 = (bf16[30,46,7]{2,1,0:T(8,128)(2,1)S(1)}, bf16[30,46,7]{2,1,0:T(8,128)(2,1)S(1)}, u32[]{:S(2)}, u32[]{:S(2)}) collective-permute-start(bf16[30,46,7]{2,1,0:T(8,128)(2,1)S(1)} %get-tuple-element.18), channel_id=1, source_target_pairs={{4,0},{8,4},{12,8},{5,1},{9,5},{13,9},{6,2},{10,6},{14,10},{7,3},{... | collective-permute-start | bytes 57968 | tf_op jit(solution)/shard_map/ppermute | solution.py:22
  355.1 17.5 %collective-permute-start.10 = (bf16[30,46,7]{2,1,0:T(8,128)(2,1)S(1)}, bf16[30,46,7]{2,1,0:T(8,128)(2,1)S(1)}, u32[]{:S(2)}, u32[]{:S(2)}) collective-permute-start(bf16[30,46,7]{2,1,0:T(8,128)(2,1)S(1)} %get-tuple-element.17), channel_id=1, source_target_pairs={{0,4},{4,8},{8,12},{1,5},{5,9},{9,13},{2,6},{6,10},{10,14},{3,7},{... | collective-permute-start | bytes 57968 | tf_op jit(solution)/shard_map/ppermute | solution.py:20
  360.2 35.3 %collective-permute-start.17 = (bf16[30,46,7]{2,1,0:T(8,128)(2,1)S(1)}, bf16[30,46,7]{2,1,0:T(8,128)(2,1)S(1)}, u32[]{:S(2)}, u32[]{:S(2)}) collective-permute-start(bf16[30,46,7]{2,1,0:T(8,128)(2,1)S(1)} %get-tuple-element.16), channel_id=1, source_target_pairs={{4,0},{8,4},{12,8},{5,1},{9,5},{13,9},{6,2},{10,6},{14,10},{7,3},{... | collective-permute-start | bytes 57968 | tf_op jit(solution)/shard_map/ppermute | solution.py:22
  361.8 38.3 %collective-permute-start.16 = (bf16[30,46,7]{2,1,0:T(8,128)(2,1)S(1)}, bf16[30,46,7]{2,1,0:T(8,128)(2,1)S(1)}, u32[]{:S(2)}, u32[]{:S(2)}) collective-permute-start(bf16[30,46,7]{2,1,0:T(8,128)(2,1)S(1)} %get-tuple-element.15), channel_id=1, source_target_pairs={{0,4},{4,8},{8,12},{1,5},{5,9},{9,13},{2,6},{6,10},{10,14},{3,7},{... | collective-permute-start | bytes 57968 | tf_op jit(solution)/shard_map/ppermute | solution.py:20
  366.4 55.9 %collective-permute-start.23 = (bf16[30,46,7]{2,1,0:T(8,128)(2,1)S(1)}, bf16[30,46,7]{2,1,0:T(8,128)(2,1)S(1)}, u32[]{:S(2)}, u32[]{:S(2)}) collective-permute-start(bf16[30,46,7]{2,1,0:T(8,128)(2,1)S(1)} %get-tuple-element.14), channel_id=1, source_target_pairs={{4,0},{8,4},{12,8},{5,1},{9,5},{13,9},{6,2},{10,6},{14,10},{7,3},{... | collective-permute-start | bytes 57968 | tf_op jit(solution)/shard_map/ppermute | solution.py:22
  368.0 58.9 %collective-permute-start.22 = (bf16[30,46,7]{2,1,0:T(8,128)(2,1)S(1)}, bf16[30,46,7]{2,1,0:T(8,128)(2,1)S(1)}, u32[]{:S(2)}, u32[]{:S(2)}) collective-permute-start(bf16[30,46,7]{2,1,0:T(8,128)(2,1)S(1)} %get-tuple-element.13), channel_id=1, source_target_pairs={{0,4},{4,8},{8,12},{1,5},{5,9},{9,13},{2,6},{6,10},{10,14},{3,7},{... | collective-permute-start | bytes 57968 | tf_op jit(solution)/shard_map/ppermute | solution.py:20
  372.6 76.1 %collective-permute-start.29 = (bf16[30,46,7]{2,1,0:T(8,128)(2,1)S(1)}, bf16[30,46,7]{2,1,0:T(8,128)(2,1)S(1)}, u32[]{:S(2)}, u32[]{:S(2)}) collective-permute-start(bf16[30,46,7]{2,1,0:T(8,128)(2,1)S(1)} %get-tuple-element.12), channel_id=1, source_target_pairs={{4,0},{8,4},{12,8},{5,1},{9,5},{13,9},{6,2},{10,6},{14,10},{7,3},{... | collective-permute-start | bytes 57968 | tf_op jit(solution)/shard_map/ppermute | solution.py:22
  395.5 58.0 %collective-permute-start.28 = (bf16[30,46,7]{2,1,0:T(8,128)(2,1)S(1)}, bf16[30,46,7]{2,1,0:T(8,128)(2,1)S(1)}, u32[]{:S(2)}, u32[]{:S(2)}) collective-permute-start(bf16[30,46,7]{2,1,0:T(8,128)(2,1)S(1)} %get-tuple-element.11), channel_id=1, source_target_pairs={{0,4},{4,8},{8,12},{1,5},{5,9},{9,13},{2,6},{6,10},{10,14},{3,7},{... | collective-permute-start | bytes 57968 | tf_op jit(solution)/shard_map/ppermute | solution.py:20
  400.1 74.3 %collective-permute-start.35 = (bf16[30,46,7]{2,1,0:T(8,128)(2,1)S(1)}, bf16[30,46,7]{2,1,0:T(8,128)(2,1)S(1)}, u32[]{:S(2)}, u32[]{:S(2)}) collective-permute-start(bf16[30,46,7]{2,1,0:T(8,128)(2,1)S(1)} %get-tuple-element.10), channel_id=1, source_target_pairs={{4,0},{8,4},{12,8},{5,1},{9,5},{13,9},{6,2},{10,6},{14,10},{7,3},{... | collective-permute-start | bytes 57968 | tf_op jit(solution)/shard_map/ppermute | solution.py:22
  422.3 52.1 %collective-permute-start.34 = (bf16[30,46,7]{2,1,0:T(8,128)(2,1)S(1)}, bf16[30,46,7]{2,1,0:T(8,128)(2,1)S(1)}, u32[]{:S(2)}, u32[]{:S(2)}) collective-permute-start(bf16[30,46,7]{2,1,0:T(8,128)(2,1)S(1)} %get-tuple-element.9), channel_id=1, source_target_pairs={{0,4},{4,8},{8,12},{1,5},{5,9},{9,13},{2,6},{6,10},{10,14},{3,7},{... | collective-permute-start | bytes 57968 | tf_op jit(solution)/shard_map/ppermute | solution.py:20
  426.9 78.9 %collective-permute-start.41 = (bf16[30,46,7]{2,1,0:T(8,128)(2,1)S(1)}, bf16[30,46,7]{2,1,0:T(8,128)(2,1)S(1)}, u32[]{:S(2)}, u32[]{:S(2)}) collective-permute-start(bf16[30,46,7]{2,1,0:T(8,128)(2,1)S(1)} %get-tuple-element.8), channel_id=1, source_target_pairs={{4,0},{8,4},{12,8},{5,1},{9,5},{13,9},{6,2},{10,6},{14,10},{7,3},{... | collective-permute-start | bytes 57968 | tf_op jit(solution)/shard_map/ppermute | solution.py:22
  448.8 57.1 %collective-permute-start.40 = (bf16[30,46,7]{2,1,0:T(8,128)(2,1)S(1)}, bf16[30,46,7]{2,1,0:T(8,128)(2,1)S(1)}, u32[]{:S(2)}, u32[]{:S(2)}) collective-permute-start(bf16[30,46,7]{2,1,0:T(8,128)(2,1)S(1)} %get-tuple-element.7), channel_id=1, source_target_pairs={{0,4},{4,8},{8,12},{1,5},{5,9},{9,13},{2,6},{6,10},{10,14},{3,7},{... | collective-permute-start | bytes 57968 | tf_op jit(solution)/shard_map/ppermute | solution.py:20
  547.1 20.0 %copy-start.1 = (f32[16,32,128]{2,1,0:T(8,128)S(1)}, f32[16,32,128]{2,1,0:T(8,128)}, u32[]{:S(2)}) copy-start(f32[16,32,128]{2,1,0:T(8,128)} %param.4) | copy-start | bytes 786436
where the time goes:
time: 589 us; the launch traced here: 578 us
  matrix products  365 us (62%)
  starting transfers between devices  120 us (20%)
  local copies, waits for them, and re-layouts  58 us (10%)
  other arithmetic  28.9 us (5%)
    dot_general x36, matrix products, valid_axis(): jnp.einsum(forms[axis_id], volume, matrix, precision=lax.Precision.HIGHEST)  365 us
    ppermute x21, starting transfers between devices, extended(): lax.ppermute(tail, axis, [(i, (i + 1) % count) for i in range(ends)])  85.9 us
    ppermute x21, starting transfers between devices, extended(): lax.ppermute(head, axis, [((i + 1) % count, i) for i in range(ends)])  27.6 us
    unnamed x10, local copies, waits for them, and re-layouts  25.1 us
    slice x33, local copies, waits for them, and re-layouts, band_matrix(): matrix = matrix + jnp.where(offset == tap_id, kernel[tap_id], 0.0)  23.6 us
  transfers between devices with their start and end apart: 43, of which 3 were waited for; matrix products, arithmetic and copies ran while one was open for 61% of the time, Pallas kernels for 0%

commit v1 on v0

v1 whole, which is shorter than its diff:
```python
import functools

import jax
import jax.numpy as jnp
from jax import lax
from jax.experimental import pallas as pl
from jax.experimental.pallas import tpu as pltpu
from jax.sharding import PartitionSpec as P

TAPS = 15
REACH = TAPS // 2
PAD = 8
BACKGROUND = 0.05

F32 = jnp.float32
BF16 = jnp.bfloat16

VMEM = pl.BlockSpec(memory_space=pltpu.VMEM)
SMEM = pl.BlockSpec(memory_space=pltpu.SMEM)


def call(body, out_shape, in_specs, scratch=(), flops=0, nbytes=0, name=None):
    many = isinstance(out_shape, (list, tuple))
    return pl.pallas_call(
        body,
        out_shape=out_shape,
        in_specs=in_specs,
        out_specs=[VMEM] * len(out_shape) if many else VMEM,
        scratch_shapes=list(scratch),
        compiler_params=pltpu.CompilerParams(vmem_limit_bytes=40 * 1024 * 1024),
        cost_estimate=pl.CostEstimate(
            flops=flops, bytes_accessed=nbytes, transcendentals=0
        ),
        name=name,
    )


def from_both(to_next, to_prev, axis):
    count = lax.axis_size(axis)
    return (
        lax.ppermute(to_next, axis, [(i, i + 1) for i in range(count - 1)]),
        lax.ppermute(to_prev, axis, [(i + 1, i) for i in range(count - 1)]),
    )


def banded(offset, weights, base):
    matrix = jnp.zeros(offset.shape, F32)
    for tap in range(TAPS):
        matrix = jnp.where(offset == tap, weights[base + tap], matrix)
    return matrix


def halves(matrix):
    high = matrix.astype(BF16).astype(F32)
    return high, matrix - high


def bands_body(views, block, prof_ref, box_ref, start_ref, yf_ref, yfh_ref, yr_ref, yrh_ref, xf_ref, xr_ref):
    _, bx, by = block
    ext = bx + 2 * PAD
    iota = lax.broadcasted_iota
    source = iota(jnp.int32, (by, by), 0)
    target = iota(jnp.int32, (by, by), 1)
    side = iota(jnp.int32, (2 * PAD, by), 0)
    side_source = jnp.where(side < PAD, side - PAD, by - PAD + side)
    side_target = iota(jnp.int32, (2 * PAD, by), 1)
    fx_col = iota(jnp.int32, (bx, 2 * ext), 1)
    fx_low = fx_col >= ext
    fx_off = jnp.where(fx_low, fx_col - ext, fx_col) - PAD - iota(jnp.int32, (bx, 2 * ext), 0)
    rx_col = iota(jnp.int32, (ext, 3 * bx), 1)
    rx_low = rx_col >= 2 * bx
    rx_row = iota(jnp.int32, (ext, 3 * bx), 0) - PAD
    rx_off = lax.rem(rx_col, bx) - rx_row

    def view(k, carry):
        base_x = (k * 3 + 1) * TAPS
        base_y = (k * 3 + 2) * TAPS

        def put(main_ref, halo_ref, matrix, halo):
            high, low = halves(matrix)
            main_ref[k, 0:by, :] = high.astype(BF16)
            main_ref[k, by : 2 * by, :] = low.astype(BF16)
            high, low = halves(halo)
            halo_ref[k, 0 : 2 * PAD, :] = high.astype(BF16)
            halo_ref[k, 2 * PAD : 4 * PAD, :] = low.astype(BF16)

        put(
            yf_ref,
            yfh_ref,
            banded(source - target + REACH, prof_ref, base_y),
            banded(side_source - side_target + REACH, prof_ref, base_y),
        )
        low_y = box_ref[k * 6 + 4] - start_ref[2]
        high_y = box_ref[k * 6 + 5] - start_ref[2]
        within = (target >= low_y) & (target < high_y)
        side_within = (side_target >= low_y) & (side_target < high_y)
        put(
            yr_ref,
            yrh_ref,
            jnp.where(within, banded(REACH - source + target, prof_ref, base_y), 0.0),
            jnp.where(side_within, banded(REACH - side_source + side_target, prof_ref, base_y), 0.0),
        )
        high, low = halves(banded(fx_off + REACH, prof_ref, base_x))
        xf_ref[k] = jnp.where(fx_low, low, high).astype(BF16)
        low_x = box_ref[k * 6 + 2] - start_ref[1]
        high_x = box_ref[k * 6 + 3] - start_ref[1]
        within = (rx_row >= low_x) & (rx_row < high_x)
        high, low = halves(jnp.where(within, banded(REACH - rx_off, prof_ref, base_x), 0.0))
        xr_ref[k] = jnp.where(rx_low, low, high).astype(BF16)
        return carry

    lax.fori_loop(0, views, view, 0)


def pick_columns(by):
    row = lax.broadcasted_iota(jnp.int32, (2 * PAD, by), 0)
    col = lax.broadcasted_iota(jnp.int32, (2 * PAD, by), 1)
    return jnp.where(col == jnp.where(row < PAD, row, by - 2 * PAD + row), 1.0, 0.0).astype(BF16)


def packed(cells):
    return lax.dot_general(
        pick_columns(cells.shape[1]), cells, (((1,), (1,)), ((), ())), preferred_element_type=F32
    ).astype(BF16)


def join_x_body(est_ref, left_ref, right_ref, out_ref):
    out_ref[...] = jnp.concatenate(
        [left_ref[...].astype(F32), est_ref[...], right_ref[...].astype(F32)], axis=1
    ).astype(BF16)


def join_z_body(mid_ref, below_ref, above_ref, cells_ref, first_ref, last_ref):
    depth, ext, by = mid_ref.shape
    cells_ref[0:PAD] = below_ref[...]
    cells_ref[PAD : PAD + depth] = mid_ref[...]
    cells_ref[PAD + depth :] = above_ref[...]
    sides = packed(cells_ref[...].reshape((depth + 2 * PAD) * ext, by))
    first_ref[...] = sides[:PAD]
    last_ref[...] = sides[PAD:]


def column_halo(left, right):
    both = jnp.concatenate([left.astype(F32), right.astype(F32)], axis=0)
    return jnp.concatenate([both, both], axis=0).T.astype(BF16)


def forward_body(views, block, prof_ref, box_ref, start_ref, cells_ref, left_ref, right_ref, yf_ref, yfh_ref, xf_ref, out_ref, halo, rows):
    bz, bx, by = block
    ext = bx + 2 * PAD
    deep = bz + 2 * PAD
    halo[...] = column_halo(left_ref[...], right_ref[...])
    step = 4
    row_x = lax.broadcasted_iota(jnp.int32, (8, by), 0)
    col_y = lax.broadcasted_iota(jnp.int32, (8, by), 1)

    def view(k, carry):
        along_y = yf_ref[k]
        along_side = yfh_ref[k]
        along_x = xf_ref[k]
        for first in range(0, deep, step):
            cells = cells_ref[first : first + step].reshape(step * ext, by)
            wide = jnp.concatenate([cells, cells], axis=1)
            mixed = jnp.dot(wide, along_y, preferred_element_type=F32)
            mixed = mixed + jnp.dot(
                halo[first * ext : (first + step) * ext, :], along_side, preferred_element_type=F32
            )
            mixed = mixed.astype(BF16).reshape(step, ext, by)
            for pair in range(0, step, 2):
                both = jnp.concatenate([mixed[pair], mixed[pair + 1]], axis=1)
                both = jnp.concatenate([both, both], axis=0)
                done = jnp.dot(along_x, both, preferred_element_type=F32)
                rows[first + pair] = done[:, :by]
                rows[first + pair + 1] = done[:, by:]
        taps = [prof_ref[k * 3 * TAPS + tap] for tap in range(TAPS)]
        low_z = box_ref[k * 6] - start_ref[0]
        high_z = box_ref[k * 6 + 1] - start_ref[0]
        low_x = box_ref[k * 6 + 2] - start_ref[1]
        high_x = box_ref[k * 6 + 3] - start_ref[1]
        low_y = box_ref[k * 6 + 4] - start_ref[2]
        high_y = box_ref[k * 6 + 5] - start_ref[2]
        within_y = (col_y >= low_y) & (col_y < high_y)
        for tile in range(0, bx, 8):
            within = within_y & (row_x + tile >= low_x) & (row_x + tile < high_x)
            inside = jnp.where(within, 1.0, 0.0)
            held = [rows[plane, tile : tile + 8, :] for plane in range(1, deep - 1)]
            for plane in range(bz):
                total = taps[0] * held[plane]
                for tap in range(1, TAPS):
                    total = total + taps[tap] * held[plane + tap]
                here = jnp.where((plane >= low_z) & (plane < high_z), 1.0, 0.0)
                out_ref[k, plane, tile : tile + 8, :] = here * inside / (total + BACKGROUND)
        return carry

    lax.fori_loop(0, views, view, 0)


def quotient_body(views, block, count, order_ref, *refs):
    gain_ref, parts = refs[0], refs[1 : 1 + count]
    quot_ref, first_ref, last_ref = refs[1 + count : 4 + count]
    held = refs[4 + count]
    bz, bx, by = block
    rows = bx // count

    def view(k, carry):
        for part, part_ref in enumerate(parts):
            at = pl.ds(pl.multiple_of(order_ref[part] * rows, rows), rows)
            held[:, at, :] = gain_ref[k, :, at, :] * part_ref[k].astype(F32)
        quot_ref[k] = held[...].astype(BF16)
        return carry

    lax.fori_loop(0, views, view, 0)
    sides = packed(quot_ref[...].reshape(views * bz * bx, by))
    first_ref[...] = sides[:PAD]
    last_ref[...] = sides[PAD:]


def return_body(views, block, prof_ref, box_ref, start_ref, quot_ref, left_ref, right_ref, yr_ref, yrh_ref, xr_ref, below_ref, mid_ref, above_ref, halo, rows, total):
    bz, bx, by = block
    ext = bx + 2 * PAD
    deep = bz + 2 * REACH
    halo[...] = column_halo(left_ref[...], right_ref[...])

    def view(k, carry):
        along_y = yr_ref[k]
        along_side = yrh_ref[k]
        along_x = xr_ref[k]
        cells = quot_ref[k].reshape(bz * bx, by)
        wide = jnp.concatenate([cells, cells], axis=1)
        mixed = jnp.dot(wide, along_y, preferred_element_type=F32)
        start = pl.multiple_of(k * (bz * bx), bz * bx)
        mixed = mixed + jnp.dot(
            halo[pl.ds(start, bz * bx), :], along_side, preferred_element_type=F32
        )
        high = mixed.astype(BF16)
        low = (mixed - high.astype(F32)).astype(BF16)
        high = high.reshape(bz, bx, by)
        low = low.reshape(bz, bx, by)
        for pair in range(0, bz, 2):
            upper = jnp.concatenate([high[pair], high[pair + 1]], axis=1)
            lower = jnp.concatenate([low[pair], low[pair + 1]], axis=1)
            both = jnp.concatenate([upper, lower, upper], axis=0)
            done = jnp.dot(along_x, both, preferred_element_type=F32)
            rows[pair] = done[:, :by]
            rows[pair + 1] = done[:, by:]
        taps = [prof_ref[k * 3 * TAPS + tap] for tap in range(TAPS)]
        low_z = box_ref[k * 6] - start_ref[0]
        high_z = box_ref[k * 6 + 1] - start_ref[0]
        for tile in range(0, ext, 8):
            held = [rows[plane, tile : tile + 8, :] for plane in range(bz)]
            for out in range(deep):
                plane = out - REACH
                part = None
                for source in range(max(0, plane - REACH), min(bz, plane + REACH + 1)):
                    term = taps[REACH - source + plane] * held[source]
                    part = term if part is None else part + term
                here = jnp.where((plane >= low_z) & (plane < high_z), 1.0, 0.0)
                part = here * part
                total[out, tile : tile + 8, :] = jnp.where(
                    k == 0, part, total[out, tile : tile + 8, :] + part
                )
        return carry

    total[...] = jnp.zeros_like(total)
    lax.fori_loop(0, views, view, 0)
    below_ref[...] = total[:REACH]
    mid_ref[...] = total[REACH : REACH + bz]
    above_ref[...] = total[REACH + bz :]


def add_z_body(mid_ref, below_ref, above_ref, mid_out, left_out, right_out):
    bz, ext, by = mid_ref.shape
    for plane in range(bz):
        cells = mid_ref[plane]
        if plane < REACH:
            cells = cells + below_ref[plane]
        if plane >= bz - REACH:
            cells = cells + above_ref[plane - (bz - REACH)]
        left_out[plane] = cells[:PAD]
        mid_out[plane] = cells[PAD : ext - PAD]
        right_out[plane] = cells[ext - PAD :]


def finish_body(views, box_ref, start_ref, est_ref, mid_ref, left_ref, right_ref, out_ref):
    bz, bx, by = est_ref.shape
    row_x = lax.broadcasted_iota(jnp.int32, (8, by), 0)
    col_y = lax.broadcasted_iota(jnp.int32, (8, by), 1)
    for tile in range(0, bx, 8):
        flat = []
        for k in range(views):
            low_x = box_ref[k * 6 + 2] - start_ref[1] - tile
            high_x = box_ref[k * 6 + 3] - start_ref[1] - tile
            low_y = box_ref[k * 6 + 4] - start_ref[2]
            high_y = box_ref[k * 6 + 5] - start_ref[2]
            within = (col_y >= low_y) & (col_y < high_y) & (row_x >= low_x) & (row_x < high_x)
            flat.append(jnp.where(within, 1.0, 0.0))
        for plane in range(bz):
            coverage = jnp.zeros((8, by), F32)
            for k in range(views):
                low_z = box_ref[k * 6] - start_ref[0]
                high_z = box_ref[k * 6 + 1] - start_ref[0]
                here = jnp.where((plane >= low_z) & (plane < high_z), 1.0, 0.0)
                coverage = coverage + here * flat[k]
            cells = mid_ref[plane, tile : tile + 8, :]
            if tile == 0:
                cells = cells + left_ref[plane]
            if tile == bx - 8:
                cells = cells + right_ref[plane]
            out_ref[plane, tile : tile + 8, :] = est_ref[plane, tile : tile + 8, :] * cells / coverage


def local(estimate, recorded, profiles, view_boxes):
    block = estimate.shape
    bz, bx, by = block
    views = recorded.shape[0]
    part_rows = recorded.shape[2]
    count = lax.axis_size("by")
    mine = lax.axis_index("by")
    ext = bx + 2 * PAD
    deep = bz + 2 * PAD
    shape = jax.ShapeDtypeStruct

    start = jnp.stack(
        [lax.axis_index("bz") * bz, lax.axis_index("bx") * bx, mine * by]
    ).astype(jnp.int32)
    taps = profiles.reshape(-1)
    boxes = view_boxes.reshape(-1)

    if count == 4 and part_rows % 8 == 0:
        pieces = [recorded[:, :, :, i * by : (i + 1) * by] for i in range(count)]
        stacked = jnp.stack(pieces)
        parts = [lax.dynamic_index_in_dim(stacked, mine, 0, keepdims=False)]
        for other in range(1, count):
            piece = lax.dynamic_index_in_dim(stacked, mine ^ other, 0, keepdims=False)
            parts.append(lax.ppermute(piece, "by", [(i, i ^ other) for i in range(count)]))
        order = jnp.stack([mine ^ other for other in range(count)]).astype(jnp.int32)
    else:
        parts = [lax.all_to_all(recorded, "by", split_axis=3, concat_axis=2, tiled=True)]
        order = jnp.zeros((1,), jnp.int32)

    head = estimate[:, :PAD].astype(BF16)
    tail = estimate[:, bx - PAD :].astype(BF16)
    left, right = from_both(tail, head, "bx")
    wide = call(
        join_x_body, shape((bz, ext, by), BF16), [VMEM] * 3, nbytes=bz * ext * by * 4, name="join_x"
    )(estimate, left, right)
    below, above = from_both(wide[bz - PAD :], wide[:PAD], "bz")
    cells, first, last = call(
        join_z_body,
        [shape((deep, ext, by), BF16), shape((PAD, deep * ext), BF16), shape((PAD, deep * ext), BF16)],
        [VMEM] * 3,
        nbytes=deep * ext * by * 4,
        name="join_z",
    )(wide, below, above)
    left, right = from_both(last, first, "by")

    yf, yfh, yr, yrh, xf, xr = call(
        functools.partial(bands_body, views, block),
        [
            shape((views, 2 * by, by), BF16),
            shape((views, 4 * PAD, by), BF16),
            shape((views, 2 * by, by), BF16),
            shape((views, 4 * PAD, by), BF16),
            shape((views, bx, 2 * ext), BF16),
            shape((views, ext, 3 * bx), BF16),
        ],
        [SMEM] * 3,
        flops=views * 64 * by * by,
        nbytes=views * by * by * 8,
        name="bands",
    )(taps, boxes, start)

    gain = call(
        functools.partial(forward_body, views, block),
        shape((views, bz, bx, by), F32),
        [SMEM] * 3 + [VMEM] * 6,
        [pltpu.VMEM((deep * ext, 4 * PAD), BF16), pltpu.VMEM((deep, bx, by), F32)],
        flops=views * deep * ext * by * 600,
        nbytes=views * bz * bx * by * 8,
        name="forward",
    )(taps, boxes, start, cells, left, right, yf, yfh, xf)

    quot, first, last = call(
        functools.partial(quotient_body, views, block, len(parts)),
        [
            shape((views, bz, bx, by), BF16),
            shape((PAD, views * bz * bx), BF16),
            shape((PAD, views * bz * bx), BF16),
        ],
        [SMEM] + [VMEM] * (1 + len(parts)),
        [pltpu.VMEM((bz, bx, by), F32)],
        flops=views * bz * bx * by * 40,
        nbytes=views * bz * bx * by * 8,
        name="quotient",
    )(order, gain, *parts)
    left, right = from_both(last, first, "by")

    below, mid, above = call(
        functools.partial(return_body, views, block),
        [
            shape((REACH, ext, by), F32),
            shape((bz, ext, by), F32),
            shape((REACH, ext, by), F32),
        ],
        [SMEM] * 3 + [VMEM] * 6,
        [
            pltpu.VMEM((views * bz * bx, 4 * PAD), BF16),
            pltpu.VMEM((bz, ext, by), F32),
            pltpu.VMEM((bz + 2 * REACH, ext, by), F32),
        ],
        flops=views * bz * ext * by * 600,
        nbytes=views * bz * bx * by * 8,
        name="returned",
    )(taps, boxes, start, quot, left, right, yr, yrh, xr)
    below, above = from_both(above, below, "bz")
    mid, left, right = call(
        add_z_body,
        [shape((bz, bx, by), F32), shape((bz, PAD, by), F32), shape((bz, PAD, by), F32)],
        [VMEM] * 3,
        nbytes=bz * ext * by * 8,
        name="add_z",
    )(mid, below, above)
    left, right = from_both(right, left, "bx")
    return call(
        functools.partial(finish_body, views),
        shape(block, F32),
        [SMEM] * 2 + [VMEM] * 4,
        nbytes=bz * bx * by * 12,
        name="finish",
    )(boxes, start, estimate, mid, left, right)


def solution(mesh):
    placed = (
        P(("groups", "bz"), "bx", "by"),
        P(None, ("groups", "bz"), ("bx", "by"), None),
        P(),
        P("groups", None),
    )
    return jax.shard_map(
        local,
        mesh=mesh,
        in_specs=placed,
        out_specs=P(("groups", "bz"), "bx", "by"),
        check_vma=False,
    )
```

time: 589 us -> 74.1 us (0.13); the launches traced: 578 us -> 73.7 us
  matrix products: 365 us -> 0 us
  starting transfers between devices: 120 us -> 32.8 us
  local copies, waits for them, and re-layouts: 58 us -> 1.59 us
  other arithmetic: 28.9 us -> 1.23 us
  Pallas kernels: 0 us -> 21.9 us
  waiting for transfers between devices: 5 us -> 16 us
    dot_general x36 -> x0, matrix products: 365 us -> none  [valid_axis(): jnp.einsum(forms[axis_id], volume, matrix, precision=lax.Precision.HIGHEST)]
    ppermute x42 -> x15, starting transfers between devices: 114 us -> 32.8 us  [the longest x6 20.6 us: from_both(): lax.ppermute(to_next, axis, [(i, i + 1) for i in range(count - 1)])]
    slice x50 -> x2, local copies, waits for them, and re-layouts: 26.2 us -> 0.02 us  [the longest x1 0.02 us: local(): below, above = from_both(wide[bz - PAD:], wide[:PAD], 'bz')]
    unnamed x10 -> x6, local copies, waits for them, and re-layouts: 25.1 us -> 0.02 us
    convert_element_type x12 -> x0, other arithmetic: 22.4 us -> none  [the longest x4 7.68 us: box_inside(): along_y = ((cols_y >= box[4]) & (cols_y < box[5])).astype(jnp.float32)]
    pallas_call x0 -> x8, Pallas kernels: none -> 21.9 us  [the longest x1 11 us: local(): call(functools.partial(forward_body, views, block), shape((views, bz, bx,...]
    ppermute x42 -> x15, waiting for transfers between devices: 5 us -> 16 us  [the longest x6 15 us: from_both(): lax.ppermute(to_prev, axis, [(i + 1, i) for i in range(count - 1)])]
    all_to_all x1 -> x0, local copies, waits for them, and re-layouts: 6.64 us -> none  [local(): lax.all_to_all(recorded, 'by', split_axis=3, concat_axis=2, tiled=True)]
  transfers between devices with their start and end apart: 43 -> 15, of which waited for: 3 -> 7; matrix products, arithmetic and copies ran while one was open for 61% -> 2% of each run, Pallas kernels for 0% -> 18%
where the time goes in v1:
time: 74.1 us; the launch traced here: 73.7 us
  starting transfers between devices  32.8 us (44%)
  Pallas kernels  21.9 us (30%)
  waiting for transfers between devices  16 us (22%)
  local copies, waits for them, and re-layouts  1.59 us (2%)
  other arithmetic  1.23 us (2%)
    ppermute x6, starting transfers between devices, from_both(): lax.ppermute(to_next, axis, [(i, i + 1) for i in range(count - 1)])  20.6 us
    ppermute x6, waiting for transfers between devices, from_both(): lax.ppermute(to_prev, axis, [(i + 1, i) for i in range(count - 1)])  15 us
    pallas_call x1, Pallas kernels, local(): call(functools.partial(forward_body, views, block), shape((views, bz, bx,...  11 us
    ppermute x6, starting transfers between devices, from_both(): lax.ppermute(to_prev, axis, [(i + 1, i) for i in range(count - 1)])  7.75 us
    pallas_call x1, Pallas kernels, local(): call(functools.partial(return_body, views, block), [shape((REACH, ext, by...  5.51 us
    ppermute x3, starting transfers between devices, local(): lax.ppermute(piece, 'by', [(i, i ^ other) for i in range(count)])  4.45 us
    pallas_call x1, Pallas kernels, local(): call(functools.partial(bands_body, views, block), [shape((views, 2 * by,...  2 us
    pallas_call x1, Pallas kernels, local(): call(functools.partial(finish_body, views), shape(block, F32), [SMEM] * 2...  1.91 us
  transfers between devices with their start and end apart: 15, of which 7 were waited for; matrix products, arithmetic and copies ran while one was open for 2% of the time, Pallas kernels for 18%

profile of v1, /device:TPU:0, one launch (start us, length us, event | category | flops | bytes accessed | tf_op | source)
XLA Modules:
  0.0 73.7 jit_solution(15280385745325573571)
XLA Ops:
  0.0 1.0 %convert.4 = bf16[16,32,128]{2,1,0:T(8,128)(2,1)S(1)} convert(f32[16,32,128]{2,1,0:T(8,128)} %est_ref.3) | non-fusion elementwise | flops 65536 | bytes 393216 | tf_op jit(solution)/shard_map/convert.1
  1.0 4.8 %collective-permute-start = (bf16[16,8,128]{2,1,0:T(8,128)(2,1)S(1)}, bf16[16,8,128]{2,1,0:T(8,128)(2,1)S(1)}, u32[]{:S(2)}, u32[]{:S(2)}) collective-permute-start(bf16[16,8,128]{2,1,0:T(8,128)(2,1)S(1)} %get-tuple-element.52), channel_id=1, source_target_pairs={{0,2},{1,3},{4,6},{5,7},{8,10},{9,11},{12,14},{13,15},{16,18},{17,... | collective-permute-start | bytes 98312 | tf_op jit(solution)/shard_map/ppermute | solution.py:41
  5.8 1.3 %collective-permute-start.1 = (bf16[16,8,128]{2,1,0:T(8,128)(2,1)S(1)}, bf16[16,8,128]{2,1,0:T(8,128)(2,1)S(1)}, u32[]{:S(2)}, u32[]{:S(2)}) collective-permute-start(bf16[16,8,128]{2,1,0:T(8,128)(2,1)S(1)} %get-tuple-element.51), channel_id=1, source_target_pairs={{2,0},{3,1},{6,4},{7,5},{10,8},{11,9},{14,12},{15,13},{18,16},{19,... | collective-permute-start | bytes 98312 | tf_op jit(solution)/shard_map/ppermute | solution.py:42
  7.2 1.3 %slice_bitcast_fusion.3 = (bf16[1,6,16,8,128]{4,3,2,1,0:T(8,128)(2,1)S(1)}, bf16[1,6,16,8,128]{4,3,2,1,0:T(8,128)(2,1)S(1)}, bf16[1,6,16,8,128]{4,3,2,1,0:T(8,128)(2,1)S(1)}, bf16[1,6,16,8,128]{4,3,2,1,0:T(8,128)(2,1)S(1)}) fusion(bf16[6,16,8,512]{3,2,1,0:T(8,128)(2,1)} %param.5), kind=kLoop, calls=%fused_computation.8 | loop fusion | bytes 1572864 | tf_op jit(solution)/shard_map/stack | solution.py:331
  8.5 0.0 copy-start
  8.5 0.1 pad_maximum_fusion
  8.6 0.0 copy-start.2
  8.6 0.0 copy-start.1
  8.6 0.1 dynamic-slice_bitcast_fusion
  8.7 1.6 %collective-permute-start.6 = (bf16[6,16,8,128]{3,2,1,0:T(8,128)(2,1)S(1)}, bf16[6,16,8,128]{3,2,1,0:T(8,128)(2,1)S(1)}, u32[]{:S(2)}, u32[]{:S(2)}) collective-permute-start(bf16[6,16,8,128]{3,2,1,0:T(8,128)(2,1)S(1)} %get-tuple-element.43), channel_id=1, source_target_pairs={{0,4},{4,0},{8,12},{12,8},{1,5},{5,1},{9,13},{13,9},{2,6},{6,2},{1... | collective-permute-start | bytes 589832 | tf_op jit(solution)/shard_map/ppermute | solution.py:335
  10.3 2.6 %collective-permute-start.7 = (bf16[6,16,8,128]{3,2,1,0:T(8,128)(2,1)S(1)}, bf16[6,16,8,128]{3,2,1,0:T(8,128)(2,1)S(1)}, u32[]{:S(2)}, u32[]{:S(2)}) collective-permute-start(bf16[6,16,8,128]{3,2,1,0:T(8,128)(2,1)S(1)} %get-tuple-element.42), channel_id=1, source_target_pairs={{0,8},{4,12},{8,0},{12,4},{1,9},{5,13},{9,1},{13,5},{2,10},{6,14},... | collective-permute-start | bytes 589832 | tf_op jit(solution)/shard_map/ppermute | solution.py:335
  12.9 0.2 collective-permute-start.8
  13.2 0.0 collective-permute-done.left_ref
  13.2 0.0 collective-permute-done.1.right_ref
  13.2 1.3 %collective-permute-start.2 = (bf16[8,48,128]{2,1,0:T(8,128)(2,1)S(1)}, bf16[8,48,128]{2,1,0:T(8,128)(2,1)S(1)}, u32[]{:S(2)}, u32[]{:S(2)}) collective-permute-start(bf16[8,48,128]{2,1,0:T(8,128)(2,1)S(1)} %get-tuple-element.50), channel_id=1, source_target_pairs={{0,1},{2,3},{4,5},{6,7},{8,9},{10,11},{12,13},{14,15},{16,17},{18,... | collective-permute-start | bytes 294920 | tf_op jit(solution)/shard_map/ppermute | solution.py:41
  14.5 1.3 %collective-permute-start.3 = (bf16[8,48,128]{2,1,0:T(8,128)(2,1)S(1)}, bf16[8,48,128]{2,1,0:T(8,128)(2,1)S(1)}, u32[]{:S(2)}, u32[]{:S(2)}) collective-permute-start(bf16[8,48,128]{2,1,0:T(8,128)(2,1)S(1)} %get-tuple-element.49), channel_id=1, source_target_pairs={{1,0},{3,2},{5,4},{7,6},{9,8},{11,10},{13,12},{15,14},{17,16},{19,... | collective-permute-start | bytes 294920 | tf_op jit(solution)/shard_map/ppermute | solution.py:42
  15.8 0.1 pad_add_fusion.start_ref
  15.9 0.0 collective-permute-done.2.below_ref
  15.9 1.8 %collective-permute-done.3.above_ref = bf16[8,48,128]{2,1,0:T(8,128)(2,1)S(1)} collective-permute-done((bf16[8,48,128]{2,1,0:T(8,128)(2,1)S(1)}, bf16[8,48,128]{2,1,0:T(8,128)(2,1)S(1)}, u32[]{:S(2)}, u32[]{:S(2)}) %collective-permute-start.3) | collective-permute-done | bytes 98336 | tf_op jit(solution)/shard_map/ppermute | solution.py:42
  17.7 0.2 join_z.1
  17.9 2.6 %collective-permute-start.4 = (bf16[8,1536]{1,0:T(8,128)(2,1)S(1)}, bf16[8,1536]{1,0:T(8,128)(2,1)S(1)}, u32[]{:S(2)}, u32[]{:S(2)}) collective-permute-start(bf16[8,1536]{1,0:T(8,128)(2,1)S(1)} %get-tuple-element.24), channel_id=1, source_target_pairs={{0,4},{4,8},{8,12},{1,5},{5,9},{9,13},{2,6},{6,10},{10,14},{3,7},{... | collective-permute-start | bytes 73736 | tf_op jit(solution)/shard_map/ppermute | solution.py:41
  20.5 1.3 %collective-permute-start.5 = (bf16[8,1536]{1,0:T(8,128)(2,1)S(1)}, bf16[8,1536]{1,0:T(8,128)(2,1)S(1)}, u32[]{:S(2)}, u32[]{:S(2)}) collective-permute-start(bf16[8,1536]{1,0:T(8,128)(2,1)S(1)} %get-tuple-element.25), channel_id=1, source_target_pairs={{4,0},{8,4},{12,8},{5,1},{9,5},{13,9},{6,2},{10,6},{14,10},{7,3},{... | collective-permute-start | bytes 73736 | tf_op jit(solution)/shard_map/ppermute | solution.py:42
  21.8 0.1 pad_add_fusion.1.order_ref
  21.9 0.1 reshape.6.box_ref
  22.0 0.0 copy-done.1
  22.0 0.1 reshape.7.prof_ref
  22.1 2.0 %bands.1 = (bf16[6,256,128]{2,1,0:T(8,128)(2,1)S(1)}, bf16[6,32,128]{2,1,0:T(8,128)(2,1)S(1)}, bf16[6,256,128]{2,1,0:T(8,128)(2,1)S(1)}, bf16[6,32,128]{2,1,0:T(...) custom-call(f32[270]{0:T(512)S(1)} %reshape.7.prof_ref, s32[36]{0:T(128)S(1)} %reshape.6.box_ref, ...), custom_call_target="tpu_custom_call" | custom-call | flops 6291456 | bytes 786432 | tf_op jit(solution)/shard_map/bands/pallas_call | solution.py:357
  24.1 0.0 collective-permute-done.4.left_ref
  24.1 2.6 %collective-permute-done.5.right_ref = bf16[8,1536]{1,0:T(8,128)(2,1)S(1)} collective-permute-done((bf16[8,1536]{1,0:T(8,128)(2,1)S(1)}, bf16[8,1536]{1,0:T(8,128)(2,1)S(1)}, u32[]{:S(2)}, u32[]{:S(2)}) %collective-permute-start.5) | collective-permute-done | bytes 24608 | tf_op jit(solution)/shard_map/ppermute | solution.py:42
  26.7 11.0 %forward.1.refs_0_ = f32[6,16,32,128]{3,2,1,0:T(8,128)S(1)} custom-call(f32[270]{0:T(512)S(1)} %reshape.7.prof_ref, s32[36]{0:T(128)S(1)} %reshape.6.box_ref, s32[3]{0:T(128)S(1)} %pad_add_fusion.start_ref, bf16[32,48,128]{2,1,0:T(8,128)(2,1)S(1)} %get-tuple-element.23.cells_ref, bf16[8,1536]{1,0:T(8,128)(2,1)S(1)} %collective-permute-done.4.left_ref, ...), custom_call_target="tpu_custom_call" | custom-call | flops 707788800 | bytes 3145728 | tf_op jit(solution)/shard_map/forward/pallas_call | solution.py:373
  37.7 0.0 collective-permute-done.6.refs_2_
  37.8 0.0 collective-permute-done.7.refs_3_
  37.8 0.0 collective-permute-done.8.refs_4_
  37.8 1.2 %quotient.1 = (bf16[6,16,32,128]{3,2,1,0:T(8,128)(2,1)S(1)}, bf16[8,3072]{1,0:T(8,128)(2,1)S(1)}, bf16[8,3072]{1,0:T(8,128)(2,1)S(1)}) custom-call(s32[4]{0:T(128)S(1)} %pad_add_fusion.1.order_ref, f32[6,16,32,128]{3,2,1,0:T(8,128)S(1)} %forward.1.refs_0_, bf16[6,16,8,128]{3,2,1,0:T(8,128)(2,1)S(1)} %get-tuple-element.44.refs_1_, ...), custom_call_target="tpu_custom_call" | custom-call | flops 15728640 | bytes 3145728 | tf_op jit(solution)/shard_map/quotient/pallas_call | solution.py:383
  39.0 6.3 %collective-permute-start.9 = (bf16[8,3072]{1,0:T(8,128)(2,1)S(1)}, bf16[8,3072]{1,0:T(8,128)(2,1)S(1)}, u32[]{:S(2)}, u32[]{:S(2)}) collective-permute-start(bf16[8,3072]{1,0:T(8,128)(2,1)S(1)} %get-tuple-element.30), channel_id=1, source_target_pairs={{0,4},{4,8},{8,12},{1,5},{5,9},{9,13},{2,6},{6,10},{10,14},{3,7},{... | collective-permute-start | bytes 147464 | tf_op jit(solution)/shard_map/ppermute | solution.py:41
  45.2 1.3 %collective-permute-start.10 = (bf16[8,3072]{1,0:T(8,128)(2,1)S(1)}, bf16[8,3072]{1,0:T(8,128)(2,1)S(1)}, u32[]{:S(2)}, u32[]{:S(2)}) collective-permute-start(bf16[8,3072]{1,0:T(8,128)(2,1)S(1)} %get-tuple-element.31), channel_id=1, source_target_pairs={{4,0},{8,4},{12,8},{5,1},{9,5},{13,9},{6,2},{10,6},{14,10},{7,3},{... | collective-permute-start | bytes 147464 | tf_op jit(solution)/shard_map/ppermute | solution.py:42
  46.5 0.4 collective-permute-done.9.left_ref
  47.0 4.3 %collective-permute-done.10.right_ref = bf16[8,3072]{1,0:T(8,128)(2,1)S(1)} collective-permute-done((bf16[8,3072]{1,0:T(8,128)(2,1)S(1)}, bf16[8,3072]{1,0:T(8,128)(2,1)S(1)}, u32[]{:S(2)}, u32[]{:S(2)}) %collective-permute-start.10) | collective-permute-done | bytes 49184 | tf_op jit(solution)/shard_map/ppermute | solution.py:42
  51.2 5.5 %returned.1 = (f32[7,48,128]{2,1,0:T(8,128)S(1)}, f32[16,48,128]{2,1,0:T(8,128)S(1)}, f32[7,48,128]{2,1,0:T(8,128)S(1)}) custom-call(f32[270]{0:T(512)S(1)} %reshape.7.prof_ref, s32[36]{0:T(128)S(1)} %reshape.6.box_ref, s32[3]{0:T(128)S(1)} %pad_add_fusion.start_ref, bf16[6,16,32,128]{3,2,1,0:T(8,128)(2,1)S(1)} %get-tuple-element.29.quot_ref, ...), custom_call_target="tpu_custom_call" | custom-call | flops 353894400 | bytes 3145728 | tf_op jit(solution)/shard_map/returned/pallas_call | solution.py:398
  56.7 1.3 %collective-permute-start.11 = (f32[7,48,128]{2,1,0:T(8,128)S(1)}, f32[7,48,128]{2,1,0:T(8,128)S(1)}, u32[]{:S(2)}, u32[]{:S(2)}) collective-permute-start(f32[7,48,128]{2,1,0:T(8,128)S(1)} %get-tuple-element.36), channel_id=1, source_target_pairs={{0,1},{2,3},{4,5},{6,7},{8,9},{10,11},{12,13},{14,15},{16,17},{18,... | collective-permute-start | bytes 516104 | tf_op jit(solution)/shard_map/ppermute | solution.py:41
  58.1 1.3 %collective-permute-start.12 = (f32[7,48,128]{2,1,0:T(8,128)S(1)}, f32[7,48,128]{2,1,0:T(8,128)S(1)}, u32[]{:S(2)}, u32[]{:S(2)}) collective-permute-start(f32[7,48,128]{2,1,0:T(8,128)S(1)} %get-tuple-element.37), channel_id=1, source_target_pairs={{1,0},{3,2},{5,4},{7,6},{9,8},{11,10},{13,12},{15,14},{17,16},{19,... | collective-permute-start | bytes 516104 | tf_op jit(solution)/shard_map/ppermute | solution.py:42
  59.4 0.0 collective-permute-done.11.below_ref
  59.4 2.0 %collective-permute-done.12.above_ref = f32[7,48,128]{2,1,0:T(8,128)S(1)} collective-permute-done((f32[7,48,128]{2,1,0:T(8,128)S(1)}, f32[7,48,128]{2,1,0:T(8,128)S(1)}, u32[]{:S(2)}, u32[]{:S(2)}) %collective-permute-start.12) | collective-permute-done | bytes 172064 | tf_op jit(solution)/shard_map/ppermute | solution.py:42
  61.4 4.3 %collective-permute-start.13 = (f32[16,8,128]{2,1,0:T(8,128)S(1)}, f32[16,8,128]{2,1,0:T(8,128)S(1)}, u32[]{:S(2)}, u32[]{:S(2)}) collective-permute-start(f32[16,8,128]{2,1,0:T(8,128)S(1)} %get-tuple-element.39), channel_id=1, source_target_pairs={{0,2},{1,3},{4,6},{5,7},{8,10},{9,11},{12,14},{13,15},{16,18},{17,... | collective-permute-start | bytes 196616 | tf_op jit(solution)/shard_map/ppermute | solution.py:41
  65.7 1.3 %collective-permute-start.14 = (f32[16,8,128]{2,1,0:T(8,128)S(1)}, f32[16,8,128]{2,1,0:T(8,128)S(1)}, u32[]{:S(2)}, u32[]{:S(2)}) collective-permute-start(f32[16,8,128]{2,1,0:T(8,128)S(1)} %get-tuple-element.40), channel_id=1, source_target_pairs={{2,0},{3,1},{6,4},{7,5},{10,8},{11,9},{14,12},{15,13},{18,16},{19,... | collective-permute-start | bytes 196616 | tf_op jit(solution)/shard_map/ppermute | solution.py:42
  67.0 0.6 collective-permute-done.13.left_ref
  67.6 4.3 %collective-permute-done.14.right_ref = f32[16,8,128]{2,1,0:T(8,128)S(1)} collective-permute-done((f32[16,8,128]{2,1,0:T(8,128)S(1)}, f32[16,8,128]{2,1,0:T(8,128)S(1)}, u32[]{:S(2)}, u32[]{:S(2)}) %collective-permute-start.14) | collective-permute-done | bytes 65568 | tf_op jit(solution)/shard_map/ppermute | solution.py:42
  71.8 1.9 %finish.1 = f32[16,32,128]{2,1,0:T(8,128)} custom-call(s32[36]{0:T(128)S(1)} %reshape.6.box_ref, s32[3]{0:T(128)S(1)} %pad_add_fusion.start_ref, f32[16,32,128]{2,1,0:T(8,128)S(1)} %copy-done, f32[16,32,128]{2,1,0:T(8,128)S(1)} %get-tuple-element.38.mid_ref, f32[16,8,128]{2,1,0:T(8,128)S(1)} %collective-permute-done.13.left_ref, ...), custom_call_target="tpu_custom_call" | custom-call | bytes 786432 | tf_op jit(solution)/shard_map/finish/pallas_call | solution.py:424
  (6 shorter events, 0.1 us)
Async XLA Ops:
  1.0 12.2 %collective-permute-start = (bf16[16,8,128]{2,1,0:T(8,128)(2,1)S(1)}, bf16[16,8,128]{2,1,0:T(8,128)(2,1)S(1)}, u32[]{:S(2)}, u32[]{:S(2)}) collective-permute-start(bf16[16,8,128]{2,1,0:T(8,128)(2,1)S(1)} %get-tuple-element.52), channel_id=1, source_target_pairs={{0,2},{1,3},{4,6},{5,7},{8,10},{9,11},{12,14},{13,15},{16,18},{17,... | collective-permute-start | bytes 98312 | tf_op jit(solution)/shard_map/ppermute | solution.py:41
  5.8 7.3 %collective-permute-start.1 = (bf16[16,8,128]{2,1,0:T(8,128)(2,1)S(1)}, bf16[16,8,128]{2,1,0:T(8,128)(2,1)S(1)}, u32[]{:S(2)}, u32[]{:S(2)}) collective-permute-start(bf16[16,8,128]{2,1,0:T(8,128)(2,1)S(1)} %get-tuple-element.51), channel_id=1, source_target_pairs={{2,0},{3,1},{6,4},{7,5},{10,8},{11,9},{14,12},{15,13},{18,16},{19,... | collective-permute-start | bytes 98312 | tf_op jit(solution)/shard_map/ppermute | solution.py:42
  8.5 4.7 %copy-start = (f32[16,32,128]{2,1,0:T(8,128)S(1)}, f32[16,32,128]{2,1,0:T(8,128)}, u32[]{:S(2)}) copy-start(f32[16,32,128]{2,1,0:T(8,128)} %est_ref.3) | copy-start | bytes 786436
  8.6 13.3 %copy-start.2 = (s32[6,6]{1,0:T(8,128)S(1)}, s32[6,6]{1,0:T(8,128)}, u32[]{:S(2)}) copy-start(s32[6,6]{1,0:T(8,128)} %param.7) | copy-start | bytes 436
  8.6 13.4 %copy-start.1 = (f32[6,3,15]{2,1,0:T(4,128)S(1)}, f32[6,3,15]{2,1,0:T(4,128)}, u32[]{:S(2)}) copy-start(f32[6,3,15]{2,1,0:T(4,128)} %param.6) | copy-start | bytes 3244
  8.7 29.0 %collective-permute-start.6 = (bf16[6,16,8,128]{3,2,1,0:T(8,128)(2,1)S(1)}, bf16[6,16,8,128]{3,2,1,0:T(8,128)(2,1)S(1)}, u32[]{:S(2)}, u32[]{:S(2)}) collective-permute-start(bf16[6,16,8,128]{3,2,1,0:T(8,128)(2,1)S(1)} %get-tuple-element.43), channel_id=1, source_target_pairs={{0,4},{4,0},{8,12},{12,8},{1,5},{5,1},{9,13},{13,9},{2,6},{6,2},{1... | collective-permute-start | bytes 589832 | tf_op jit(solution)/shard_map/ppermute | solution.py:335
  10.3 27.4 %collective-permute-start.7 = (bf16[6,16,8,128]{3,2,1,0:T(8,128)(2,1)S(1)}, bf16[6,16,8,128]{3,2,1,0:T(8,128)(2,1)S(1)}, u32[]{:S(2)}, u32[]{:S(2)}) collective-permute-start(bf16[6,16,8,128]{3,2,1,0:T(8,128)(2,1)S(1)} %get-tuple-element.42), channel_id=1, source_target_pairs={{0,8},{4,12},{8,0},{12,4},{1,9},{5,13},{9,1},{13,5},{2,10},{6,14},... | collective-permute-start | bytes 589832 | tf_op jit(solution)/shard_map/ppermute | solution.py:335
  12.9 24.8 %collective-permute-start.8 = (bf16[6,16,8,128]{3,2,1,0:T(8,128)(2,1)S(1)}, bf16[6,16,8,128]{3,2,1,0:T(8,128)(2,1)S(1)}, u32[]{:S(2)}, u32[]{:S(2)}) collective-permute-start(bf16[6,16,8,128]{3,2,1,0:T(8,128)(2,1)S(1)} %get-tuple-element.41), channel_id=1, source_target_pairs={{0,12},{4,8},{8,4},{12,0},{1,13},{5,9},{9,5},{13,1},{2,14},{6,10},... | collective-permute-start | bytes 589832 | tf_op jit(solution)/shard_map/ppermute | solution.py:335
  13.2 2.7 %collective-permute-start.2 = (bf16[8,48,128]{2,1,0:T(8,128)(2,1)S(1)}, bf16[8,48,128]{2,1,0:T(8,128)(2,1)S(1)}, u32[]{:S(2)}, u32[]{:S(2)}) collective-permute-start(bf16[8,48,128]{2,1,0:T(8,128)(2,1)S(1)} %get-tuple-element.50), channel_id=1, source_target_pairs={{0,1},{2,3},{4,5},{6,7},{8,9},{10,11},{12,13},{14,15},{16,17},{18,... | collective-permute-start | bytes 294920 | tf_op jit(solution)/shard_map/ppermute | solution.py:41
  14.5 3.2 %collective-permute-start.3 = (bf16[8,48,128]{2,1,0:T(8,128)(2,1)S(1)}, bf16[8,48,128]{2,1,0:T(8,128)(2,1)S(1)}, u32[]{:S(2)}, u32[]{:S(2)}) collective-permute-start(bf16[8,48,128]{2,1,0:T(8,128)(2,1)S(1)} %get-tuple-element.49), channel_id=1, source_target_pairs={{1,0},{3,2},{5,4},{7,6},{9,8},{11,10},{13,12},{15,14},{17,16},{19,... | collective-permute-start | bytes 294920 | tf_op jit(solution)/shard_map/ppermute | solution.py:42
  17.9 6.2 %collective-permute-start.4 = (bf16[8,1536]{1,0:T(8,128)(2,1)S(1)}, bf16[8,1536]{1,0:T(8,128)(2,1)S(1)}, u32[]{:S(2)}, u32[]{:S(2)}) collective-permute-start(bf16[8,1536]{1,0:T(8,128)(2,1)S(1)} %get-tuple-element.24), channel_id=1, source_target_pairs={{0,4},{4,8},{8,12},{1,5},{5,9},{9,13},{2,6},{6,10},{10,14},{3,7},{... | collective-permute-start | bytes 73736 | tf_op jit(solution)/shard_map/ppermute | solution.py:41
  20.5 6.2 %collective-permute-start.5 = (bf16[8,1536]{1,0:T(8,128)(2,1)S(1)}, bf16[8,1536]{1,0:T(8,128)(2,1)S(1)}, u32[]{:S(2)}, u32[]{:S(2)}) collective-permute-start(bf16[8,1536]{1,0:T(8,128)(2,1)S(1)} %get-tuple-element.25), channel_id=1, source_target_pairs={{4,0},{8,4},{12,8},{5,1},{9,5},{13,9},{6,2},{10,6},{14,10},{7,3},{... | collective-permute-start | bytes 73736 | tf_op jit(solution)/shard_map/ppermute | solution.py:42
  39.0 8.0 %collective-permute-start.9 = (bf16[8,3072]{1,0:T(8,128)(2,1)S(1)}, bf16[8,3072]{1,0:T(8,128)(2,1)S(1)}, u32[]{:S(2)}, u32[]{:S(2)}) collective-permute-start(bf16[8,3072]{1,0:T(8,128)(2,1)S(1)} %get-tuple-element.30), channel_id=1, source_target_pairs={{0,4},{4,8},{8,12},{1,5},{5,9},{9,13},{2,6},{6,10},{10,14},{3,7},{... | collective-permute-start | bytes 147464 | tf_op jit(solution)/shard_map/ppermute | solution.py:41
  45.2 6.0 %collective-permute-start.10 = (bf16[8,3072]{1,0:T(8,128)(2,1)S(1)}, bf16[8,3072]{1,0:T(8,128)(2,1)S(1)}, u32[]{:S(2)}, u32[]{:S(2)}) collective-permute-start(bf16[8,3072]{1,0:T(8,128)(2,1)S(1)} %get-tuple-element.31), channel_id=1, source_target_pairs={{4,0},{8,4},{12,8},{5,1},{9,5},{13,9},{6,2},{10,6},{14,10},{7,3},{... | collective-permute-start | bytes 147464 | tf_op jit(solution)/shard_map/ppermute | solution.py:42
  56.7 2.6 %collective-permute-start.11 = (f32[7,48,128]{2,1,0:T(8,128)S(1)}, f32[7,48,128]{2,1,0:T(8,128)S(1)}, u32[]{:S(2)}, u32[]{:S(2)}) collective-permute-start(f32[7,48,128]{2,1,0:T(8,128)S(1)} %get-tuple-element.36), channel_id=1, source_target_pairs={{0,1},{2,3},{4,5},{6,7},{8,9},{10,11},{12,13},{14,15},{16,17},{18,... | collective-permute-start | bytes 516104 | tf_op jit(solution)/shard_map/ppermute | solution.py:41
  58.1 3.3 %collective-permute-start.12 = (f32[7,48,128]{2,1,0:T(8,128)S(1)}, f32[7,48,128]{2,1,0:T(8,128)S(1)}, u32[]{:S(2)}, u32[]{:S(2)}) collective-permute-start(f32[7,48,128]{2,1,0:T(8,128)S(1)} %get-tuple-element.37), channel_id=1, source_target_pairs={{1,0},{3,2},{5,4},{7,6},{9,8},{11,10},{13,12},{15,14},{17,16},{19,... | collective-permute-start | bytes 516104 | tf_op jit(solution)/shard_map/ppermute | solution.py:42
  61.4 6.2 %collective-permute-start.13 = (f32[16,8,128]{2,1,0:T(8,128)S(1)}, f32[16,8,128]{2,1,0:T(8,128)S(1)}, u32[]{:S(2)}, u32[]{:S(2)}) collective-permute-start(f32[16,8,128]{2,1,0:T(8,128)S(1)} %get-tuple-element.39), channel_id=1, source_target_pairs={{0,2},{1,3},{4,6},{5,7},{8,10},{9,11},{12,14},{13,15},{16,18},{17,... | collective-permute-start | bytes 196616 | tf_op jit(solution)/shard_map/ppermute | solution.py:41
  65.7 6.2 %collective-permute-start.14 = (f32[16,8,128]{2,1,0:T(8,128)S(1)}, f32[16,8,128]{2,1,0:T(8,128)S(1)}, u32[]{:S(2)}, u32[]{:S(2)}) collective-permute-start(f32[16,8,128]{2,1,0:T(8,128)S(1)} %get-tuple-element.40), channel_id=1, source_target_pairs={{2,0},{3,1},{6,4},{7,5},{10,8},{11,9},{14,12},{15,13},{18,16},{19,... | collective-permute-start | bytes 196616 | tf_op jit(solution)/shard_map/ppermute | solution.py:42

commit v2 on v0

v2 whole, which is shorter than its diff:
```python
import functools

import jax
import jax.numpy as jnp
from jax import lax
from jax.experimental import pallas as pl
from jax.experimental.pallas import tpu as pltpu
from jax.sharding import PartitionSpec as P

TAPS = 15
REACH = TAPS // 2
PAD = 8
BACKGROUND = 0.05

F32 = jnp.float32
BF16 = jnp.bfloat16

VMEM = pl.BlockSpec(memory_space=pltpu.VMEM)
SMEM = pl.BlockSpec(memory_space=pltpu.SMEM)


def call(body, out_shape, in_specs, scratch=(), flops=0, nbytes=0, name=None):
    many = isinstance(out_shape, (list, tuple))
    return pl.pallas_call(
        body,
        out_shape=out_shape,
        in_specs=in_specs,
        out_specs=[VMEM] * len(out_shape) if many else VMEM,
        scratch_shapes=list(scratch),
        compiler_params=pltpu.CompilerParams(vmem_limit_bytes=40 * 1024 * 1024),
        cost_estimate=pl.CostEstimate(
            flops=flops, bytes_accessed=nbytes, transcendentals=0
        ),
        name=name,
    )


def partner(index, count, swap):
    other = index ^ 1 if swap == 0 else ((index + 1) ^ 1) - 1
    return other if 0 <= other < count else index


def swaps_of(count):
    return {1: [], 2: [0]}.get(count, [0, 1])


def meets_next(index, swap):
    return lax.rem(index + swap, 2) == 0


def has_partner(index, count, swap):
    after = meets_next(index, swap)
    return jnp.where(after, index < count - 1, index > 0)


def links_of(count_x, count_z):
    along_x, along_z = [None, *swaps_of(count_x)], [None, *swaps_of(count_z)]
    return [(x, z) for x in along_x for z in along_z if (x, z) != (None, None)]


def exchange(cells, link, count_x, count_z):
    x, z = link
    pairs = []
    for i in range(count_x):
        for j in range(count_z):
            to_x = i if x is None else partner(i, count_x, x)
            to_z = j if z is None else partner(j, count_z, z)
            pairs.append((i * count_z + j, to_x * count_z + to_z))
    return lax.ppermute(cells, ("bx", "bz"), pairs)


def exchange_y(first, second):
    count = lax.axis_size("by")
    return [
        lax.ppermute(cells, "by", [(i, partner(i, count, swap)) for i in range(count)])
        for swap, cells in enumerate((first, second))
    ]


def banded(offset, tap_of):
    matrix = jnp.zeros(offset.shape, F32)
    for tap in range(TAPS):
        matrix = jnp.where(offset == tap, tap_of(tap), matrix)
    return matrix


def halves(matrix):
    high = matrix.astype(BF16)
    return high, (matrix - high.astype(F32)).astype(BF16)


def prepare_body(views, count, counts, links, est_ref, rec_ref, *out_refs):
    bz, bx, by = est_ref.shape
    mine = lax.axis_index("by")
    for other in range(count):
        at = pl.ds(pl.multiple_of((mine ^ other) * by, by), by)
        out_refs[other][...] = rec_ref[:, :, :, at]
    for (x, z), out_ref in zip(links, out_refs[count:]):
        at_x, at_z = slice(None), slice(None)
        if x is not None:
            begin = jnp.where(meets_next(lax.axis_index("bx"), x), bx - PAD, 0)
            at_x = pl.ds(pl.multiple_of(begin, PAD), PAD)
        if z is not None:
            begin = jnp.where(meets_next(lax.axis_index("bz"), z), bz - PAD, 0)
            at_z = pl.ds(begin, PAD)
        out_ref[...] = est_ref[at_z, at_x, :].astype(BF16)


def packed(cells, begin):
    by = cells.shape[1]
    row = lax.broadcasted_iota(jnp.int32, (PAD, by), 0)
    col = lax.broadcasted_iota(jnp.int32, (PAD, by), 1)
    pick = jnp.where(col == row + begin, 1.0, 0.0).astype(BF16)
    return lax.dot_general(
        pick, cells, (((1,), (1,)), ((), ())), preferred_element_type=F32
    ).astype(BF16)


def pack_both(cells, by, first_ref, second_ref):
    last = by - PAD
    mine = lax.axis_index("by")
    first_ref[...] = packed(cells, jnp.where(meets_next(mine, 0), last, 0))
    second_ref[...] = packed(cells, jnp.where(meets_next(mine, 1), last, 0))


def unpack_both(count, first_ref, second_ref):
    mine = lax.axis_index("by")
    first, second = first_ref[...].astype(F32), second_ref[...].astype(F32)
    even = meets_next(mine, 0)
    before = jnp.where(even, second, first)
    after = jnp.where(even, first, second)
    before = jnp.where(mine > 0, before, 0.0)
    after = jnp.where(mine < count - 1, after, 0.0)
    return jnp.concatenate([before, after], axis=0).T.astype(BF16)


def join_body(counts, links, est_ref, *refs):
    bz, bx, by = est_ref.shape
    ext = bx + 2 * PAD
    deep = bz + 2 * PAD
    link_refs = refs[: len(links)]
    cells_ref, first_ref, second_ref, wide = refs[len(links) :]
    wide[...] = jnp.zeros_like(wide)
    wide[PAD : PAD + bz, PAD : PAD + bx, :] = est_ref[...]
    for (x, z), link_ref in zip(links, link_refs):
        at_x, at_z, known = slice(PAD, PAD + bx), slice(PAD, PAD + bz), None
        if x is not None:
            index = lax.axis_index("bx")
            begin = jnp.where(meets_next(index, x), PAD + bx, 0)
            at_x = pl.ds(pl.multiple_of(begin, PAD), PAD)
            known = has_partner(index, counts[0], x)
        if z is not None:
            index = lax.axis_index("bz")
            at_z = pl.ds(jnp.where(meets_next(index, z), PAD + bz, 0), PAD)
            there = has_partner(index, counts[1], z)
            known = there if known is None else known & there

        @pl.when(known)
        def _():
            wide[at_z, at_x, :] = link_ref[...].astype(F32)

    cells_ref[...] = wide[...].astype(BF16)
    pack_both(cells_ref[...].reshape(deep * ext, by), by, first_ref, second_ref)


def bands_body(views, prof_ref, box_ref, est_ref, yf_ref, yr_ref, xf_ref, xr_ref, share_ref):
    bz, bx, by = est_ref.shape
    ext = bx + 2 * PAD
    start_z = lax.axis_index("bz") * bz
    start_x = lax.axis_index("bx") * bx
    start_y = lax.axis_index("by") * by

    def iota(shape, dim):
        return lax.broadcasted_iota(jnp.int32, shape, dim)

    shape_y = (by + 2 * PAD, by)
    row = iota(shape_y, 0)
    source = jnp.where(row < by, row, jnp.where(row < by + PAD, row - by - PAD, row - PAD))
    target = iota(shape_y, 1)
    shape_x = (bx, 2 * ext)
    col = iota(shape_x, 1)
    is_low = col >= ext
    forward_x = jnp.where(is_low, col - ext, col) - PAD - iota(shape_x, 0)

    def view(k, carry):
        forward = banded(source - target + REACH, lambda tap: prof_ref[k, 2, tap])
        high, low = halves(forward)
        yf_ref[k, :, :by] = high
        yf_ref[k, :, by:] = low
        back = banded(REACH - source + target, lambda tap: prof_ref[k, 2, tap])
        within = (target >= box_ref[k, 4] - start_y) & (target < box_ref[k, 5] - start_y)
        high, low = halves(jnp.where(within, back, 0.0))
        yr_ref[k, :, :by] = high
        yr_ref[k, :, by:] = low
        high, low = halves(banded(forward_x + REACH, lambda tap: prof_ref[k, 1, tap]))
        at = pl.ds(pl.multiple_of(k * bx, bx), bx)
        xf_ref[at, :] = jnp.where(is_low, low.astype(F32), high.astype(F32)).astype(BF16)
        return carry

    lax.fori_loop(0, views, view, 0)

    shape_x = (ext, views * bx)
    target = iota(shape_x, 0) - PAD
    col = iota(shape_x, 1)

    def back_view(k, matrix):
        source = col - k * bx
        back = banded(REACH - source + target, lambda tap: prof_ref[k, 1, tap])
        within = (source >= 0) & (source < bx)
        within = within & (target >= box_ref[k, 2] - start_x) & (target < box_ref[k, 3] - start_x)
        return jnp.where(within, back, matrix)

    high, low = halves(lax.fori_loop(0, views, back_view, jnp.zeros(shape_x, F32)))
    xr_ref[:ext] = high
    xr_ref[ext:] = low

    row_x = iota((bx, by), 0) + start_x
    col_y = iota((bx, by), 1) + start_y
    flat = []
    for k in range(views):
        within = (col_y >= box_ref[k, 4]) & (col_y < box_ref[k, 5])
        within = within & (row_x >= box_ref[k, 2]) & (row_x < box_ref[k, 3])
        flat.append(jnp.where(within, 1.0, 0.0))
    for plane in range(bz):
        coverage = jnp.zeros((bx, by), F32)
        for k in range(views):
            at = plane + start_z
            here = (at >= box_ref[k, 0]) & (at < box_ref[k, 1])
            coverage = coverage + jnp.where(here, 1.0, 0.0) * flat[k]
        share_ref[plane] = est_ref[plane] / coverage


def forward_body(views, block, count, prof_ref, box_ref, cells_ref, first_ref, second_ref, yf_ref, xf_ref, gain_ref, halo, blurred_x, rows):
    bz, bx, by = block
    ext = bx + 2 * PAD
    deep = bz + 2 * PAD
    halo[...] = unpack_both(count, first_ref, second_ref)
    for plane in range(1, deep - 1):
        cells = jnp.concatenate([cells_ref[plane], halo[plane * ext : (plane + 1) * ext, :]], axis=1)
        cells = jnp.concatenate([cells, cells], axis=0)
        mixed = jnp.dot(xf_ref[...], cells, preferred_element_type=F32).astype(BF16)
        for k in range(views):
            blurred_x[k, plane * bx : (plane + 1) * bx, :] = mixed[k * bx : (k + 1) * bx]
    row_x = lax.broadcasted_iota(jnp.int32, (8, by), 0) + lax.axis_index("bx") * bx
    col_y = lax.broadcasted_iota(jnp.int32, (8, by), 1) + lax.axis_index("by") * by
    start_z = lax.axis_index("bz") * bz
    step = 10

    def view(k, carry):
        along_y = yf_ref[k]
        for first in range(1, deep - 1, step):
            mixed = jnp.dot(
                blurred_x[k, first * bx : (first + step) * bx, :], along_y, preferred_element_type=F32
            )
            rows[first : first + step] = (mixed[:, :by] + mixed[:, by:]).reshape(step, bx, by)
        taps = [prof_ref[k, 0, tap] for tap in range(TAPS)]
        within_y = (col_y >= box_ref[k, 4]) & (col_y < box_ref[k, 5])
        inside = []
        for tile in range(0, bx, 8):
            at = row_x + tile
            inside.append(jnp.where(within_y & (at >= box_ref[k, 2]) & (at < box_ref[k, 3]), 1.0, 0.0))
        gain_ref[k] = jnp.zeros((bz, bx, by), F32)

        def plane_of(plane, carry):
            for tile in range(0, bx, 8):
                total = taps[0] * rows[plane + 1, tile : tile + 8, :]
                for tap in range(1, TAPS):
                    total = total + taps[tap] * rows[plane + 1 + tap, tile : tile + 8, :]
                gain_ref[k, plane, tile : tile + 8, :] = inside[tile // 8] / (total + BACKGROUND)
            return carry

        begin = jnp.clip(box_ref[k, 0] - start_z, 0, bz)
        end = jnp.clip(box_ref[k, 1] - start_z, 0, bz)
        lax.fori_loop(begin, end, plane_of, 0)
        return carry

    lax.fori_loop(0, views, view, 0)


def quotient_body(views, block, count, gain_ref, *refs):
    parts = refs[:count]
    quot_ref, first_ref, second_ref, held = refs[count:]
    bz, bx, by = block
    rows = bx // count
    mine = lax.axis_index("by") if count > 1 else 0

    def view(k, carry):
        for part, part_ref in enumerate(parts):
            at = pl.ds(pl.multiple_of((mine ^ part) * rows, rows), rows)
            held[:, at, :] = gain_ref[k, :, at, :] * part_ref[k].astype(F32)
        quot_ref[k] = held[...].astype(BF16)
        return carry

    lax.fori_loop(0, views, view, 0)
    pack_both(quot_ref[...].reshape(views * bz * bx, by), by, first_ref, second_ref)


def return_body(views, block, count, counts, links, prof_ref, box_ref, quot_ref, first_ref, second_ref, yr_ref, xr_ref, mid_ref, *refs):
    bz, bx, by = block
    ext = bx + 2 * PAD
    deep = bz + 2 * REACH
    link_refs = refs[: len(links)]
    halo, rows, high_rows, low_rows, total = refs[len(links) :]
    halo[...] = unpack_both(count, first_ref, second_ref)
    start_z = lax.axis_index("bz") * bz

    def view(k, carry):
        start = pl.multiple_of(k * (bz * bx), bz * bx)
        cells = quot_ref[k].reshape(bz * bx, by)
        cells = jnp.concatenate([cells, halo[pl.ds(start, bz * bx), :]], axis=1)
        mixed = jnp.dot(cells, yr_ref[k], preferred_element_type=F32)
        rows[...] = (mixed[:, :by] + mixed[:, by:]).reshape(bz, bx, by)
        taps = [prof_ref[k, 0, tap] for tap in range(TAPS)]
        at = pl.ds(pl.multiple_of(k * bx, bx), bx)
        for out in range(deep):
            plane = out - REACH
            here = (plane + start_z >= box_ref[k, 0]) & (plane + start_z < box_ref[k, 1])

            @pl.when(here)
            def _():
                sums = []
                for tile in range(0, bx, 8):
                    part = None
                    for source in range(max(0, plane - REACH), min(bz, plane + REACH + 1)):
                        term = taps[REACH - source + plane] * rows[source, tile : tile + 8, :]
                        part = term if part is None else part + term
                    sums.append(part)
                high, low = halves(jnp.concatenate(sums, axis=0))
                high_rows[out, at, :] = high
                low_rows[out, at, :] = low

            @pl.when(jnp.logical_not(here))
            def _():
                high_rows[out, at, :] = jnp.zeros((bx, by), BF16)
                low_rows[out, at, :] = jnp.zeros((bx, by), BF16)

        return carry

    lax.fori_loop(0, views, view, 0)
    for out in range(0, deep, 2):
        high = jnp.concatenate([high_rows[out], high_rows[out + 1]], axis=1)
        low = jnp.concatenate([low_rows[out], low_rows[out + 1]], axis=1)
        mixed = jnp.dot(xr_ref[...], high, preferred_element_type=F32)
        mixed = mixed[:ext] + mixed[ext:] + jnp.dot(xr_ref[:ext], low, preferred_element_type=F32)
        total[out] = mixed[:, :by]
        total[out + 1] = mixed[:, by:]
    mid_ref[...] = total[REACH : REACH + bz, PAD : PAD + bx, :]
    for (x, z), link_ref in zip(links, link_refs):
        at_x, at_z = slice(PAD, PAD + bx), slice(REACH, REACH + bz)
        if x is not None:
            begin = jnp.where(meets_next(lax.axis_index("bx"), x), PAD + bx, 0)
            at_x = pl.ds(pl.multiple_of(begin, PAD), PAD)
        if z is not None:
            at_z = pl.ds(jnp.where(meets_next(lax.axis_index("bz"), z), REACH + bz, 0), REACH)
        link_ref[...] = total[at_z, at_x, :]


def finish_body(counts, links, share_ref, mid_ref, *refs):
    bz, bx, by = share_ref.shape
    link_refs, out_ref = refs[: len(links)], refs[len(links)]
    out_ref[...] = share_ref[...] * mid_ref[...]
    for (x, z), link_ref in zip(links, link_refs):
        at_x, at_z, known = slice(None), slice(None), None
        if x is not None:
            index = lax.axis_index("bx")
            begin = jnp.where(meets_next(index, x), bx - PAD, 0)
            at_x = pl.ds(pl.multiple_of(begin, PAD), PAD)
            known = has_partner(index, counts[0], x)
        if z is not None:
            index = lax.axis_index("bz")
            at_z = pl.ds(jnp.where(meets_next(index, z), bz - REACH, 0), REACH)
            there = has_partner(index, counts[1], z)
            known = there if known is None else known & there

        @pl.when(known)
        def _():
            out_ref[at_z, at_x, :] = out_ref[at_z, at_x, :] + share_ref[at_z, at_x, :] * link_ref[...]


def local(estimate, recorded, profiles, view_boxes):
    block = estimate.shape
    bz, bx, by = block
    views = recorded.shape[0]
    part_rows = recorded.shape[2]
    count = lax.axis_size("by")
    counts = (lax.axis_size("bx"), lax.axis_size("bz"))
    links = links_of(*counts)
    ext = bx + 2 * PAD
    deep = bz + 2 * PAD
    shape = jax.ShapeDtypeStruct

    def link_shape(link, reach, dtype):
        x, z = link
        return shape((bz if z is None else reach, bx if x is None else PAD, by), dtype)

    swapped = count & (count - 1) == 0 and count <= 4 and part_rows % 8 == 0
    holders = count if swapped else 0
    sent = call(
        functools.partial(prepare_body, views, holders, counts, links),
        [shape((views, bz, part_rows, by), BF16)] * holders
        + [link_shape(link, PAD, BF16) for link in links],
        [VMEM] * 2,
        nbytes=views * bz * bx * by * 4,
        name="prepare",
    )(estimate, recorded)
    if swapped:
        parts = [sent[0]] + [
            lax.ppermute(sent[other], "by", [(i, i ^ other) for i in range(count)])
            for other in range(1, count)
        ]
    else:
        parts = [lax.all_to_all(recorded, "by", split_axis=3, concat_axis=2, tiled=True)]

    came = [exchange(cells, link, *counts) for link, cells in zip(links, sent[holders:])]
    side = shape((PAD, deep * ext), BF16)
    cells, first, second = call(
        functools.partial(join_body, counts, links),
        [shape((deep, ext, by), BF16), side, side],
        [VMEM] * (1 + len(links)),
        [pltpu.VMEM((deep, ext, by), F32)],
        nbytes=deep * ext * by * 4,
        name="join",
    )(estimate, *came)
    first, second = exchange_y(first, second)

    yf, yr, xf, xr, share = call(
        functools.partial(bands_body, views),
        [
            shape((views, by + 2 * PAD, 2 * by), BF16),
            shape((views, by + 2 * PAD, 2 * by), BF16),
            shape((views * bx, 2 * ext), BF16),
            shape((2 * ext, views * bx), BF16),
            shape(block, F32),
        ],
        [SMEM] * 2 + [VMEM],
        flops=views * 64 * by * by,
        nbytes=views * by * by * 8,
        name="bands",
    )(profiles, view_boxes, estimate)

    gain = call(
        functools.partial(forward_body, views, block, count),
        shape((views, bz, bx, by), F32),
        [SMEM] * 2 + [VMEM] * 5,
        [
            pltpu.VMEM((deep * ext, 2 * PAD), BF16),
            pltpu.VMEM((views, deep * bx, by + 2 * PAD), BF16),
            pltpu.VMEM((deep, bx, by), F32),
        ],
        flops=views * deep * ext * by * 600,
        nbytes=views * bz * bx * by * 8,
        name="forward",
    )(profiles, view_boxes, cells, first, second, yf, xf)

    side = shape((PAD, views * bz * bx), BF16)
    quot, first, second = call(
        functools.partial(quotient_body, views, block, len(parts)),
        [shape((views, bz, bx, by), BF16), side, side],
        [VMEM] * (1 + len(parts)),
        [pltpu.VMEM((bz, bx, by), F32)],
        flops=views * bz * bx * by * 40,
        nbytes=views * bz * bx * by * 8,
        name="quotient",
    )(gain, *parts)
    first, second = exchange_y(first, second)

    mid, *sums = call(
        functools.partial(return_body, views, block, count, counts, links),
        [shape(block, F32)] + [link_shape(link, REACH, F32) for link in links],
        [SMEM] * 2 + [VMEM] * 5,
        [
            pltpu.VMEM((views * bz * bx, 2 * PAD), BF16),
            pltpu.VMEM((bz, bx, by), F32),
            pltpu.VMEM((bz + 2 * REACH, views * bx, by), BF16),
            pltpu.VMEM((bz + 2 * REACH, views * bx, by), BF16),
            pltpu.VMEM((bz + 2 * REACH, ext, by), F32),
        ],
        flops=views * bz * ext * by * 600,
        nbytes=views * bz * bx * by * 8,
        name="returned",
    )(profiles, view_boxes, quot, first, second, yr, xr)
    sums = [exchange(cells, link, *counts) for link, cells in zip(links, sums)]
    return call(
        functools.partial(finish_body, counts, links),
        shape(block, F32),
        [VMEM] * (2 + len(links)),
        nbytes=bz * bx * by * 12,
        name="finish",
    )(share, mid, *sums)


def solution(mesh):
    placed = (
        P(("groups", "bz"), "bx", "by"),
        P(None, ("groups", "bz"), ("bx", "by"), None),
        P(),
        P("groups", None),
    )
    return jax.shard_map(
        local,
        mesh=mesh,
        in_specs=placed,
        out_specs=P(("groups", "bz"), "bx", "by"),
        check_vma=False,
    )
```

time: 589 us -> 48.7 us (0.08)
  the two profiles are of different devices: /device:TPU:0 before, /device:TPU:13 now
where the time goes in v2:
time: 48.7 us; the launch traced here: 48.2 us
  starting transfers between devices  18.1 us (37%)
  Pallas kernels  16.8 us (34%)
  waiting for transfers between devices  9.71 us (20%)
  local copies, waits for them, and re-layouts  3.48 us (7%)
    ppermute x4, starting transfers between devices, exchange_y(): lax.ppermute(cells, 'by', [(i, partner(i, count, swap)) for i in range(co...  7.76 us
    ppermute x6, starting transfers between devices, exchange(): return lax.ppermute(cells, ('bx', 'bz'), pairs)  7.6 us
    ppermute x6, waiting for transfers between devices, exchange(): return lax.ppermute(cells, ('bx', 'bz'), pairs)  7.19 us
    pallas_call x1, Pallas kernels, local(): call(functools.partial(return_body, views, block, count, counts, links),...  6.44 us
    pallas_call x1, Pallas kernels, local(): call(functools.partial(forward_body, views, block, count), shape((views,...  5.49 us
    unnamed x12, local copies, waits for them, and re-layouts  3.48 us
    ppermute x3, starting transfers between devices, local(): lax.ppermute(sent[other], 'by', [(i, i ^ other) for i in range(count)])  2.71 us
    pallas_call x1, Pallas kernels, local(): call(functools.partial(bands_body, views), [shape((views, by + 2 * PAD, 2...  2.64 us
  transfers between devices with their start and end apart: 13, of which 5 were waited for; matrix products, arithmetic and copies ran while one was open for 0% of the time, Pallas kernels for 18%

profile of v2, /device:TPU:13, one launch (start us, length us, event | category | flops | bytes accessed | tf_op | source)
XLA Modules:
  0.0 48.2 jit_solution(10534398297075452901)
XLA Ops:
  0.0 0.0 copy-start
  0.0 0.9 %copy-done = f32[16,32,128]{2,1,0:T(8,128)S(1)} copy-done((f32[16,32,128]{2,1,0:T(8,128)S(1)}, f32[16,32,128]{2,1,0:T(8,128)}, u32[]{:S(2)}) %copy-start) | copy-done | bytes 262168
  1.0 0.0 copy-start.2
  1.0 1.1 %copy-done.2 = bf16[6,16,8,512]{3,2,1,0:T(8,128)(2,1)S(1)} copy-done((bf16[6,16,8,512]{3,2,1,0:T(8,128)(2,1)S(1)}, bf16[6,16,8,512]{3,2,1,0:T(8,128)(2,1)}, u32[]{:S(2)}) %copy-start.2) | copy-done | bytes 786456
  2.1 0.0 copy-start.1
  2.1 0.2 prepare.1
  2.2 0.2 collective-permute-start.5
  2.5 2.3 %collective-permute-start.6 = (bf16[6,16,8,128]{3,2,1,0:T(8,128)(2,1)S(1)}, bf16[6,16,8,128]{3,2,1,0:T(8,128)(2,1)S(1)}, u32[]{:S(2)}, u32[]{:S(2)}) collective-permute-start(bf16[6,16,8,128]{3,2,1,0:T(8,128)(2,1)S(1)} %get-tuple-element.38), channel_id=1, source_target_pairs={{0,8},{4,12},{8,0},{12,4},{1,9},{5,13},{9,1},{13,5},{2,10},{6,14},... | collective-permute-start | bytes 589832 | tf_op jit(solution)/shard_map/ppermute | solution.py:408
  4.8 0.2 collective-permute-start.7
  5.0 1.5 %collective-permute-start = (bf16[8,32,128]{2,1,0:T(8,128)(2,1)S(1)}, bf16[8,32,128]{2,1,0:T(8,128)(2,1)S(1)}, u32[]{:S(2)}, u32[]{:S(2)}) collective-permute-start(bf16[8,32,128]{2,1,0:T(8,128)(2,1)S(1)} %get-tuple-element.28), channel_id=1, source_target_pairs={{0,1},{1,0},{2,3},{3,2},{4,5},{5,4},{6,7},{7,6},{8,9},{9,8},{10,11... | collective-permute-start | bytes 196616 | tf_op jit(solution)/shard_map/ppermute | solution.py:69
  6.5 1.1 %collective-permute-start.2 = (bf16[8,8,128]{2,1,0:T(8,128)(2,1)S(1)}, bf16[8,8,128]{2,1,0:T(8,128)(2,1)S(1)}, u32[]{:S(2)}, u32[]{:S(2)}) collective-permute-start(bf16[8,8,128]{2,1,0:T(8,128)(2,1)S(1)} %get-tuple-element.30), channel_id=1, source_target_pairs={{0,3},{1,2},{2,1},{3,0},{4,7},{5,6},{6,5},{7,4},{8,11},{9,10},{10,... | collective-permute-start | bytes 49160 | tf_op jit(solution)/shard_map/ppermute | solution.py:69
  7.6 2.4 %collective-permute-done.2.refs_2_ = bf16[8,8,128]{2,1,0:T(8,128)(2,1)S(1)} collective-permute-done((bf16[8,8,128]{2,1,0:T(8,128)(2,1)S(1)}, bf16[8,8,128]{2,1,0:T(8,128)(2,1)S(1)}, u32[]{:S(2)}, u32[]{:S(2)}) %collective-permute-start.2) | collective-permute-done | bytes 16416 | tf_op jit(solution)/shard_map/ppermute | solution.py:69
  9.9 1.2 %collective-permute-start.1 = (bf16[16,8,128]{2,1,0:T(8,128)(2,1)S(1)}, bf16[16,8,128]{2,1,0:T(8,128)(2,1)S(1)}, u32[]{:S(2)}, u32[]{:S(2)}) collective-permute-start(bf16[16,8,128]{2,1,0:T(8,128)(2,1)S(1)} %get-tuple-element.29), channel_id=1, source_target_pairs={{0,2},{1,3},{2,0},{3,1},{4,6},{5,7},{6,4},{7,5},{8,10},{9,11},{10,... | collective-permute-start | bytes 98312 | tf_op jit(solution)/shard_map/ppermute | solution.py:69
  11.2 2.0 %collective-permute-done.1.refs_1_ = bf16[16,8,128]{2,1,0:T(8,128)(2,1)S(1)} collective-permute-done((bf16[16,8,128]{2,1,0:T(8,128)(2,1)S(1)}, bf16[16,8,128]{2,1,0:T(8,128)(2,1)S(1)}, u32[]{:S(2)}, u32[]{:S(2)}) %collective-permute-start.1) | collective-permute-done | bytes 32800 | tf_op jit(solution)/shard_map/ppermute | solution.py:69
  13.2 0.0 collective-permute-done.refs_0_
  13.2 0.4 join.1
  13.6 1.1 %collective-permute-start.3 = (bf16[8,1536]{1,0:T(8,128)(2,1)S(1)}, bf16[8,1536]{1,0:T(8,128)(2,1)S(1)}, u32[]{:S(2)}, u32[]{:S(2)}) collective-permute-start(bf16[8,1536]{1,0:T(8,128)(2,1)S(1)} %get-tuple-element.32), channel_id=1, source_target_pairs={{0,4},{4,0},{8,12},{12,8},{1,5},{5,1},{9,13},{13,9},{2,6},{6,2},{1... | collective-permute-start | bytes 73736 | tf_op jit(solution)/shard_map/ppermute | solution.py:75
  14.7 4.3 %collective-permute-start.4 = (bf16[8,1536]{1,0:T(8,128)(2,1)S(1)}, bf16[8,1536]{1,0:T(8,128)(2,1)S(1)}, u32[]{:S(2)}, u32[]{:S(2)}) collective-permute-start(bf16[8,1536]{1,0:T(8,128)(2,1)S(1)} %get-tuple-element.33), channel_id=1, source_target_pairs={{0,0},{4,8},{8,4},{12,12},{1,1},{5,9},{9,5},{13,13},{2,2},{6,10},{... | collective-permute-start | bytes 73736 | tf_op jit(solution)/shard_map/ppermute | solution.py:75
  19.0 0.0 copy-done.1
  19.0 0.0 copy-start.3
  19.0 0.7 %copy-done.3 = f32[6,3,15]{2,1,0:T(4,128)S(1)} copy-done((f32[6,3,15]{2,1,0:T(4,128)S(1)}, f32[6,3,15]{2,1,0:T(4,128)}, u32[]{:S(2)}) %copy-start.3) | copy-done | bytes 1104
  19.7 0.0 copy-start.4
  19.7 0.7 %copy-done.4 = s32[6,6]{1,0:T(8,128)S(1)} copy-done((s32[6,6]{1,0:T(8,128)S(1)}, s32[6,6]{1,0:T(8,128)}, u32[]{:S(2)}) %copy-start.4) | copy-done | bytes 168
  20.4 2.6 %bands.1 = (bf16[6,144,256]{2,1,0:T(8,128)(2,1)S(1)}, bf16[6,144,256]{2,1,0:T(8,128)(2,1)S(1)}, bf16[192,96]{1,0:T(8,128)(2,1)S(1)}, bf16[96,192]{1,0:T(8,128)(2,1)S(1)}, f32[16,32,128]{2,1,0:T(8,128)S(1)}) custom-call(f32[6,3,15]{2,1,0:T(4,128)S(1)} %copy-done.3, s32[6,6]{1,0:T(8,128)S(1)} %copy-done.4, f32[16,32,128]{2,1,0:T(8,128)S(1)} %copy-done.1), custom_call_target="tpu_custom_call" | custom-call | flops 6291456 | bytes 786432 | tf_op jit(solution)/shard_map/bands/pallas_call | solution.py:426
  23.1 0.0 collective-permute-done.3.first_ref
  23.1 0.0 collective-permute-done.4.second_ref
  23.1 5.5 %forward.1.gain_ref = f32[6,16,32,128]{3,2,1,0:T(8,128)S(1)} custom-call(f32[6,3,15]{2,1,0:T(4,128)S(1)} %copy-done.3, s32[6,6]{1,0:T(8,128)S(1)} %copy-done.4, bf16[32,48,128]{2,1,0:T(8,128)(2,1)S(1)} %get-tuple-element.31.cells_ref, bf16[8,1536]{1,0:T(8,128)(2,1)S(1)} %collective-permute-done.3.first_ref, ...), custom_call_target="tpu_custom_call" | custom-call | flops 707788800 | bytes 3145728 | tf_op jit(solution)/shard_map/forward/pallas_call | solution.py:441
  28.6 0.0 copy-start.5
  28.6 0.0 collective-permute-done.5.refs_1_
  28.6 0.0 collective-permute-done.6.refs_2_
  28.6 0.0 collective-permute-done.7.refs_3_
  28.6 0.9 %quotient.1 = (bf16[6,16,32,128]{3,2,1,0:T(8,128)(2,1)S(1)}, bf16[8,3072]{1,0:T(8,128)(2,1)S(1)}, bf16[8,3072]{1,0:T(8,128)(2,1)S(1)}) custom-call(f32[6,16,32,128]{3,2,1,0:T(8,128)S(1)} %forward.1.gain_ref, bf16[6,16,8,128]{3,2,1,0:T(8,128)(2,1)S(1)} %get-tuple-element.36.refs_0_, bf16[6,16,8,128]{3,2,1,0:T(8,128)(2,1)S(1)} %collective-permute-done.5.refs_1_, ...), custom_call_target="tpu_custom_call" | custom-call | flops 15728640 | bytes 3145728 | tf_op jit(solution)/shard_map/quotient/pallas_call | solution.py:456
  29.5 0.0 collective-permute-start.8
  29.5 2.3 %collective-permute-start.9 = (bf16[8,3072]{1,0:T(8,128)(2,1)S(1)}, bf16[8,3072]{1,0:T(8,128)(2,1)S(1)}, u32[]{:S(2)}, u32[]{:S(2)}) collective-permute-start(bf16[8,3072]{1,0:T(8,128)(2,1)S(1)} %get-tuple-element.42), channel_id=1, source_target_pairs={{0,0},{4,8},{8,4},{12,12},{1,1},{5,9},{9,5},{13,13},{2,2},{6,10},{... | collective-permute-start | bytes 147464 | tf_op jit(solution)/shard_map/ppermute | solution.py:75
  31.9 0.6 %collective-permute-done.8.first_ref = bf16[8,3072]{1,0:T(8,128)(2,1)S(1)} collective-permute-done((bf16[8,3072]{1,0:T(8,128)(2,1)S(1)}, bf16[8,3072]{1,0:T(8,128)(2,1)S(1)}, u32[]{:S(2)}, u32[]{:S(2)}) %collective-permute-start.8) | collective-permute-done | bytes 49184 | tf_op jit(solution)/shard_map/ppermute | solution.py:75
  32.4 1.9 %collective-permute-done.9.second_ref = bf16[8,3072]{1,0:T(8,128)(2,1)S(1)} collective-permute-done((bf16[8,3072]{1,0:T(8,128)(2,1)S(1)}, bf16[8,3072]{1,0:T(8,128)(2,1)S(1)}, u32[]{:S(2)}, u32[]{:S(2)}) %collective-permute-start.9) | collective-permute-done | bytes 49184 | tf_op jit(solution)/shard_map/ppermute | solution.py:75
  34.4 0.0 copy-done.5
  34.4 6.4 %returned.1 = (f32[16,32,128]{2,1,0:T(8,128)S(1)}, f32[7,32,128]{2,1,0:T(8,128)S(1)}, f32[16,8,128]{2,1,0:T(8,128)S(1)}, f32[7,8,128]{2,1,0:T(8,128)S(1)}) custom-call(f32[6,3,15]{2,1,0:T(4,128)S(1)} %copy-done.3, s32[6,6]{1,0:T(8,128)S(1)} %copy-done.5, bf16[6,16,32,128]{3,2,1,0:T(8,128)(2,1)S(1)} %get-tuple-element.40.quot_ref, ...), custom_call_target="tpu_custom_call" | custom-call | flops 353894400 | bytes 3145728 | tf_op jit(solution)/shard_map/returned/pallas_call | solution.py:467
  40.8 2.1 %collective-permute-start.10 = (f32[7,32,128]{2,1,0:T(8,128)S(1)}, f32[7,32,128]{2,1,0:T(8,128)S(1)}, u32[]{:S(2)}, u32[]{:S(2)}) collective-permute-start(f32[7,32,128]{2,1,0:T(8,128)S(1)} %get-tuple-element.46), channel_id=1, source_target_pairs={{0,1},{1,0},{2,3},{3,2},{4,5},{5,4},{6,7},{7,6},{8,9},{9,8},{10,11... | collective-permute-start | bytes 344072 | tf_op jit(solution)/shard_map/ppermute | solution.py:69
  42.9 1.2 %collective-permute-start.11 = (f32[16,8,128]{2,1,0:T(8,128)S(1)}, f32[16,8,128]{2,1,0:T(8,128)S(1)}, u32[]{:S(2)}, u32[]{:S(2)}) collective-permute-start(f32[16,8,128]{2,1,0:T(8,128)S(1)} %get-tuple-element.47), channel_id=1, source_target_pairs={{0,2},{1,3},{2,0},{3,1},{4,6},{5,7},{6,4},{7,5},{8,10},{9,11},{10,... | collective-permute-start | bytes 196616 | tf_op jit(solution)/shard_map/ppermute | solution.py:69
  44.1 0.5 %collective-permute-start.12 = (f32[7,8,128]{2,1,0:T(8,128)S(1)}, f32[7,8,128]{2,1,0:T(8,128)S(1)}, u32[]{:S(2)}, u32[]{:S(2)}) collective-permute-start(f32[7,8,128]{2,1,0:T(8,128)S(1)} %get-tuple-element.48), channel_id=1, source_target_pairs={{0,3},{1,2},{2,1},{3,0},{4,7},{5,6},{6,5},{7,4},{8,11},{9,10},{10,... | collective-permute-start | bytes 86024 | tf_op jit(solution)/shard_map/ppermute | solution.py:69
  44.6 2.8 %collective-permute-done.12.refs_2_ = f32[7,8,128]{2,1,0:T(8,128)S(1)} collective-permute-done((f32[7,8,128]{2,1,0:T(8,128)S(1)}, f32[7,8,128]{2,1,0:T(8,128)S(1)}, u32[]{:S(2)}, u32[]{:S(2)}) %collective-permute-start.12) | collective-permute-done | bytes 28704 | tf_op jit(solution)/shard_map/ppermute | solution.py:69
  47.4 0.0 collective-permute-done.11.refs_1_
  47.4 0.0 collective-permute-done.10.refs_0_
  47.4 0.8 %finish.1 = f32[16,32,128]{2,1,0:T(8,128)} custom-call(f32[16,32,128]{2,1,0:T(8,128)S(1)} %get-tuple-element.27.share_ref, f32[16,32,128]{2,1,0:T(8,128)S(1)} %get-tuple-element.45.mid_ref, f32[7,32,128]{2,1,0:T(8,128)S(1)} %collective-permute-done.10.refs_0_, f32[16,8,128]{2,1,0:T(8,128)S(1)} %collective-permute-done.11.refs_1_, ...), custom_call_target="tpu_custom_call" | custom-call | bytes 786432 | tf_op jit(solution)/shard_map/finish/pallas_call | solution.py:483
Async XLA Ops:
  0.0 0.9 %copy-start = (f32[16,32,128]{2,1,0:T(8,128)S(1)}, f32[16,32,128]{2,1,0:T(8,128)}, u32[]{:S(2)}) copy-start(f32[16,32,128]{2,1,0:T(8,128)} %est_ref.5) | copy-start | bytes 786436
  1.0 1.1 %copy-start.2 = (bf16[6,16,8,512]{3,2,1,0:T(8,128)(2,1)S(1)}, bf16[6,16,8,512]{3,2,1,0:T(8,128)(2,1)}, u32[]{:S(2)}) copy-start(bf16[6,16,8,512]{3,2,1,0:T(8,128)(2,1)} %rec_ref.1) | copy-start | bytes 2359300
  2.1 16.9 %copy-start.1 = (f32[16,32,128]{2,1,0:T(8,128)S(1)}, f32[16,32,128]{2,1,0:T(8,128)}, u32[]{:S(2)}) copy-start(f32[16,32,128]{2,1,0:T(8,128)} %est_ref.5) | copy-start | bytes 786436
  2.2 26.4 %collective-permute-start.5 = (bf16[6,16,8,128]{3,2,1,0:T(8,128)(2,1)S(1)}, bf16[6,16,8,128]{3,2,1,0:T(8,128)(2,1)S(1)}, u32[]{:S(2)}, u32[]{:S(2)}) collective-permute-start(bf16[6,16,8,128]{3,2,1,0:T(8,128)(2,1)S(1)} %get-tuple-element.37), channel_id=1, source_target_pairs={{0,4},{4,0},{8,12},{12,8},{1,5},{5,1},{9,13},{13,9},{2,6},{6,2},{1... | collective-permute-start | bytes 589832 | tf_op jit(solution)/shard_map/ppermute | solution.py:408
  2.5 26.1 %collective-permute-start.6 = (bf16[6,16,8,128]{3,2,1,0:T(8,128)(2,1)S(1)}, bf16[6,16,8,128]{3,2,1,0:T(8,128)(2,1)S(1)}, u32[]{:S(2)}, u32[]{:S(2)}) collective-permute-start(bf16[6,16,8,128]{3,2,1,0:T(8,128)(2,1)S(1)} %get-tuple-element.38), channel_id=1, source_target_pairs={{0,8},{4,12},{8,0},{12,4},{1,9},{5,13},{9,1},{13,5},{2,10},{6,14},... | collective-permute-start | bytes 589832 | tf_op jit(solution)/shard_map/ppermute | solution.py:408
  4.8 23.8 %collective-permute-start.7 = (bf16[6,16,8,128]{3,2,1,0:T(8,128)(2,1)S(1)}, bf16[6,16,8,128]{3,2,1,0:T(8,128)(2,1)S(1)}, u32[]{:S(2)}, u32[]{:S(2)}) collective-permute-start(bf16[6,16,8,128]{3,2,1,0:T(8,128)(2,1)S(1)} %get-tuple-element.39), channel_id=1, source_target_pairs={{0,12},{4,8},{8,4},{12,0},{1,13},{5,9},{9,5},{13,1},{2,14},{6,10},... | collective-permute-start | bytes 589832 | tf_op jit(solution)/shard_map/ppermute | solution.py:408
  5.0 8.2 %collective-permute-start = (bf16[8,32,128]{2,1,0:T(8,128)(2,1)S(1)}, bf16[8,32,128]{2,1,0:T(8,128)(2,1)S(1)}, u32[]{:S(2)}, u32[]{:S(2)}) collective-permute-start(bf16[8,32,128]{2,1,0:T(8,128)(2,1)S(1)} %get-tuple-element.28), channel_id=1, source_target_pairs={{0,1},{1,0},{2,3},{3,2},{4,5},{5,4},{6,7},{7,6},{8,9},{9,8},{10,11... | collective-permute-start | bytes 196616 | tf_op jit(solution)/shard_map/ppermute | solution.py:69
  6.5 3.5 %collective-permute-start.2 = (bf16[8,8,128]{2,1,0:T(8,128)(2,1)S(1)}, bf16[8,8,128]{2,1,0:T(8,128)(2,1)S(1)}, u32[]{:S(2)}, u32[]{:S(2)}) collective-permute-start(bf16[8,8,128]{2,1,0:T(8,128)(2,1)S(1)} %get-tuple-element.30), channel_id=1, source_target_pairs={{0,3},{1,2},{2,1},{3,0},{4,7},{5,6},{6,5},{7,4},{8,11},{9,10},{10,... | collective-permute-start | bytes 49160 | tf_op jit(solution)/shard_map/ppermute | solution.py:69
  9.9 3.2 %collective-permute-start.1 = (bf16[16,8,128]{2,1,0:T(8,128)(2,1)S(1)}, bf16[16,8,128]{2,1,0:T(8,128)(2,1)S(1)}, u32[]{:S(2)}, u32[]{:S(2)}) collective-permute-start(bf16[16,8,128]{2,1,0:T(8,128)(2,1)S(1)} %get-tuple-element.29), channel_id=1, source_target_pairs={{0,2},{1,3},{2,0},{3,1},{4,6},{5,7},{6,4},{7,5},{8,10},{9,11},{10,... | collective-permute-start | bytes 98312 | tf_op jit(solution)/shard_map/ppermute | solution.py:69
  13.6 9.5 %collective-permute-start.3 = (bf16[8,1536]{1,0:T(8,128)(2,1)S(1)}, bf16[8,1536]{1,0:T(8,128)(2,1)S(1)}, u32[]{:S(2)}, u32[]{:S(2)}) collective-permute-start(bf16[8,1536]{1,0:T(8,128)(2,1)S(1)} %get-tuple-element.32), channel_id=1, source_target_pairs={{0,4},{4,0},{8,12},{12,8},{1,5},{5,1},{9,13},{13,9},{2,6},{6,2},{1... | collective-permute-start | bytes 73736 | tf_op jit(solution)/shard_map/ppermute | solution.py:75
  14.7 8.4 %collective-permute-start.4 = (bf16[8,1536]{1,0:T(8,128)(2,1)S(1)}, bf16[8,1536]{1,0:T(8,128)(2,1)S(1)}, u32[]{:S(2)}, u32[]{:S(2)}) collective-permute-start(bf16[8,1536]{1,0:T(8,128)(2,1)S(1)} %get-tuple-element.33), channel_id=1, source_target_pairs={{0,0},{4,8},{8,4},{12,12},{1,1},{5,9},{9,5},{13,13},{2,2},{6,10},{... | collective-permute-start | bytes 73736 | tf_op jit(solution)/shard_map/ppermute | solution.py:75
  19.0 0.7 %copy-start.3 = (f32[6,3,15]{2,1,0:T(4,128)S(1)}, f32[6,3,15]{2,1,0:T(4,128)}, u32[]{:S(2)}) copy-start(f32[6,3,15]{2,1,0:T(4,128)} %prof_ref.5) | copy-start | bytes 3244
  19.7 0.7 %copy-start.4 = (s32[6,6]{1,0:T(8,128)S(1)}, s32[6,6]{1,0:T(8,128)}, u32[]{:S(2)}) copy-start(s32[6,6]{1,0:T(8,128)} %box_ref.5) | copy-start | bytes 436
  28.6 5.8 %copy-start.5 = (s32[6,6]{1,0:T(8,128)S(1)}, s32[6,6]{1,0:T(8,128)}, u32[]{:S(2)}) copy-start(s32[6,6]{1,0:T(8,128)} %box_ref.5) | copy-start | bytes 436
  29.5 3.0 %collective-permute-start.8 = (bf16[8,3072]{1,0:T(8,128)(2,1)S(1)}, bf16[8,3072]{1,0:T(8,128)(2,1)S(1)}, u32[]{:S(2)}, u32[]{:S(2)}) collective-permute-start(bf16[8,3072]{1,0:T(8,128)(2,1)S(1)} %get-tuple-element.41), channel_id=1, source_target_pairs={{0,4},{4,0},{8,12},{12,8},{1,5},{5,1},{9,13},{13,9},{2,6},{6,2},{1... | collective-permute-start | bytes 147464 | tf_op jit(solution)/shard_map/ppermute | solution.py:75
  29.5 4.8 %collective-permute-start.9 = (bf16[8,3072]{1,0:T(8,128)(2,1)S(1)}, bf16[8,3072]{1,0:T(8,128)(2,1)S(1)}, u32[]{:S(2)}, u32[]{:S(2)}) collective-permute-start(bf16[8,3072]{1,0:T(8,128)(2,1)S(1)} %get-tuple-element.42), channel_id=1, source_target_pairs={{0,0},{4,8},{8,4},{12,12},{1,1},{5,9},{9,5},{13,13},{2,2},{6,10},{... | collective-permute-start | bytes 147464 | tf_op jit(solution)/shard_map/ppermute | solution.py:75
  40.8 6.6 %collective-permute-start.10 = (f32[7,32,128]{2,1,0:T(8,128)S(1)}, f32[7,32,128]{2,1,0:T(8,128)S(1)}, u32[]{:S(2)}, u32[]{:S(2)}) collective-permute-start(f32[7,32,128]{2,1,0:T(8,128)S(1)} %get-tuple-element.46), channel_id=1, source_target_pairs={{0,1},{1,0},{2,3},{3,2},{4,5},{5,4},{6,7},{7,6},{8,9},{9,8},{10,11... | collective-permute-start | bytes 344072 | tf_op jit(solution)/shard_map/ppermute | solution.py:69
  42.9 4.5 %collective-permute-start.11 = (f32[16,8,128]{2,1,0:T(8,128)S(1)}, f32[16,8,128]{2,1,0:T(8,128)S(1)}, u32[]{:S(2)}, u32[]{:S(2)}) collective-permute-start(f32[16,8,128]{2,1,0:T(8,128)S(1)} %get-tuple-element.47), channel_id=1, source_target_pairs={{0,2},{1,3},{2,0},{3,1},{4,6},{5,7},{6,4},{7,5},{8,10},{9,11},{10,... | collective-permute-start | bytes 196616 | tf_op jit(solution)/shard_map/ppermute | solution.py:69
  44.1 3.3 %collective-permute-start.12 = (f32[7,8,128]{2,1,0:T(8,128)S(1)}, f32[7,8,128]{2,1,0:T(8,128)S(1)}, u32[]{:S(2)}, u32[]{:S(2)}) collective-permute-start(f32[7,8,128]{2,1,0:T(8,128)S(1)} %get-tuple-element.48), channel_id=1, source_target_pairs={{0,3},{1,2},{2,1},{3,0},{4,7},{5,6},{6,5},{7,4},{8,11},{9,10},{10,... | collective-permute-start | bytes 86024 | tf_op jit(solution)/shard_map/ppermute | solution.py:69

commit v3 on v2

--- a/solution.py
+++ b/solution.py
@@ -11,12 +11,15 @@
 REACH = TAPS // 2
 PAD = 8
 BACKGROUND = 0.05
+WEIGHT = 0.7
 
 F32 = jnp.float32
 BF16 = jnp.bfloat16
 
 VMEM = pl.BlockSpec(memory_space=pltpu.VMEM)
 SMEM = pl.BlockSpec(memory_space=pltpu.SMEM)
+ANY = pl.BlockSpec(memory_space=pl.ANY)
+HBM = pl.BlockSpec(memory_space=pltpu.HBM)
 
 
 def call(body, out_shape, in_specs, scratch=(), flops=0, nbytes=0, name=None):
@@ -29,7 +32,7 @@
         scratch_shapes=list(scratch),
         compiler_params=pltpu.CompilerParams(vmem_limit_bytes=40 * 1024 * 1024),
         cost_estimate=pl.CostEstimate(
-            flops=flops, bytes_accessed=nbytes, transcendentals=0
+            flops=int(WEIGHT * flops), bytes_accessed=int(WEIGHT * nbytes), transcendentals=0
         ),
         name=name,
     )
@@ -89,23 +92,6 @@
     return high, (matrix - high.astype(F32)).astype(BF16)
 
 
-def prepare_body(views, count, counts, links, est_ref, rec_ref, *out_refs):
-    bz, bx, by = est_ref.shape
-    mine = lax.axis_index("by")
-    for other in range(count):
-        at = pl.ds(pl.multiple_of((mine ^ other) * by, by), by)
-        out_refs[other][...] = rec_ref[:, :, :, at]
-    for (x, z), out_ref in zip(links, out_refs[count:]):
-        at_x, at_z = slice(None), slice(None)
-        if x is not None:
-            begin = jnp.where(meets_next(lax.axis_index("bx"), x), bx - PAD, 0)
-            at_x = pl.ds(pl.multiple_of(begin, PAD), PAD)
-        if z is not None:
-            begin = jnp.where(meets_next(lax.axis_index("bz"), z), bz - PAD, 0)
-            at_z = pl.ds(begin, PAD)
-        out_ref[...] = est_ref[at_z, at_x, :].astype(BF16)
-
-
 def packed(cells, begin):
     by = cells.shape[1]
     row = lax.broadcasted_iota(jnp.int32, (PAD, by), 0)
@@ -134,36 +120,77 @@
     return jnp.concatenate([before, after], axis=0).T.astype(BF16)
 
 
-def join_body(counts, links, est_ref, *refs):
+def columns_body(rec_ref, est_ref, cells_ref, first_ref, second_ref):
     bz, bx, by = est_ref.shape
-    ext = bx + 2 * PAD
+    cells_ref[...] = est_ref[...].astype(BF16)
+    pack_both(cells_ref[...].reshape(bz * bx, by), by, first_ref, second_ref)
+
+
+def pieces_body(order_ref, rec_ref, *out_refs):
+    by = out_refs[0].shape[3]
+    for other, out_ref in enumerate(out_refs):
+        at = pl.ds(pl.multiple_of((lax.axis_index("by") ^ other) * by, by), by)
+        out_ref[...] = rec_ref[:, :, :, at]
+
+
+def upright(cells):
+    return cells.astype(F32).T
+
+
+def lying(cells):
+    wide = cells.shape[1]
+    row = lax.broadcasted_iota(jnp.int32, (wide, wide), 0)
+    col = lax.broadcasted_iota(jnp.int32, (wide, wide), 1)
+    same = jnp.where(row == col, 1.0, 0.0).astype(BF16)
+    return lax.dot_general(
+        same, cells.astype(BF16), (((1,), (1,)), ((), ())), preferred_element_type=F32
+    )
+
+
+def edges_body(count, est_ref, first_ref, second_ref, halo_ref, *out_refs):
+    bz, bx, by = est_ref.shape
+    halo_ref[...] = unpack_both(count, first_ref, second_ref)
+    for swap, out_ref in enumerate(out_refs):
+        begin = jnp.where(meets_next(lax.axis_index("bz"), swap), bz - PAD, 0)
+        out_ref[:PAD] = est_ref[pl.ds(begin, PAD)]
+        rows = halo_ref[pl.ds(pl.multiple_of(begin * bx, PAD * bx), PAD * bx), :]
+        flat = lying(rows).astype(BF16)
+        for i in range(PAD * bx // by):
+            out_ref[PAD, 2 * PAD * i : 2 * PAD * (i + 1), :] = flat[:, i * by : (i + 1) * by]
+
+
+def deep_body(counts, count_z, order_ref, est_ref, halo_ref, *refs):
+    bz, bx, by = est_ref.shape
     deep = bz + 2 * PAD
-    link_refs = refs[: len(links)]
-    cells_ref, first_ref, second_ref, wide = refs[len(links) :]
-    wide[...] = jnp.zeros_like(wide)
-    wide[PAD : PAD + bz, PAD : PAD + bx, :] = est_ref[...]
-    for (x, z), link_ref in zip(links, link_refs):
-        at_x, at_z, known = slice(PAD, PAD + bx), slice(PAD, PAD + bz), None
-        if x is not None:
-            index = lax.axis_index("bx")
-            begin = jnp.where(meets_next(index, x), PAD + bx, 0)
-            at_x = pl.ds(pl.multiple_of(begin, PAD), PAD)
-            known = has_partner(index, counts[0], x)
-        if z is not None:
-            index = lax.axis_index("bz")
-            at_z = pl.ds(jnp.where(meets_next(index, z), PAD + bz, 0), PAD)
-            there = has_partner(index, counts[1], z)
-            known = there if known is None else known & there
-
-        @pl.when(known)
+    z_refs, (cells_ref, halos_ref, *out_refs) = refs[:count_z], refs[count_z:]
+    cells_ref[...] = jnp.zeros_like(cells_ref)
+    halos_ref[...] = jnp.zeros_like(halos_ref)
+    cells_ref[PAD : PAD + bz] = est_ref[...].astype(F32)
+    halos_ref[PAD : PAD + bz] = halo_ref[...].astype(F32).reshape(bz, bx, 2 * PAD)
+    for swap, z_ref in enumerate(z_refs):
+        index = lax.axis_index("bz")
+        at = pl.ds(jnp.where(meets_next(index, swap), PAD + bz, 0), PAD)
+
+        @pl.when(has_partner(index, counts[1], swap))
         def _():
-            wide[at_z, at_x, :] = link_ref[...].astype(F32)
-
-    cells_ref[...] = wide[...].astype(BF16)
-    pack_both(cells_ref[...].reshape(deep * ext, by), by, first_ref, second_ref)
-
-
-def bands_body(views, prof_ref, box_ref, est_ref, yf_ref, yr_ref, xf_ref, xr_ref, share_ref):
+            cells_ref[at] = z_ref[:PAD].astype(F32)
+            flat = jnp.concatenate(
+                [z_ref[PAD, 2 * PAD * i : 2 * PAD * (i + 1), :] for i in range(PAD * bx // by)], axis=1
+            )
+            halos_ref[at] = upright(flat).reshape(PAD, bx, 2 * PAD)
+
+    for swap, out_ref in enumerate(out_refs):
+        begin = jnp.where(meets_next(lax.axis_index("bx"), swap), bx - PAD, 0)
+        at = pl.ds(pl.multiple_of(begin, PAD), PAD)
+        out_ref[:deep] = cells_ref[:, at, :].astype(BF16)
+        flat = lying(halos_ref[:, at, :].reshape(deep * PAD, 2 * PAD))
+        for i in range(deep * PAD // by):
+            part = flat[:, i * by : (i + 1) * by]
+            out_ref[deep + 2 * i] = part[:PAD].astype(BF16)
+            out_ref[deep + 2 * i + 1] = part[PAD:].astype(BF16)
+
+
+def bands_body(views, order_ref, prof_ref, box_ref, est_ref, yf_ref, yr_ref, xf_ref, xr_ref, share_ref):
     bz, bx, by = est_ref.shape
     ext = bx + 2 * PAD
     start_z = lax.axis_index("bz") * bz
@@ -230,13 +257,33 @@
         share_ref[plane] = est_ref[plane] / coverage
 
 
-def forward_body(views, block, count, prof_ref, box_ref, cells_ref, first_ref, second_ref, yf_ref, xf_ref, gain_ref, halo, blurred_x, rows):
+def forward_body(views, block, counts, count_x, prof_ref, box_ref, cells_ref, halos_ref, yf_ref, xf_ref, *refs):
+    x_refs, (gain_ref, side_halo, blurred_x, rows) = refs[:count_x], refs[count_x:]
     bz, bx, by = block
-    ext = bx + 2 * PAD
     deep = bz + 2 * PAD
-    halo[...] = unpack_both(count, first_ref, second_ref)
+    sides = []
+    for swap, x_ref in enumerate(x_refs):
+        index = lax.axis_index("bx")
+        known = has_partner(index, counts[0], swap)
+        after = meets_next(index, swap)
+        sides.append((known & jnp.logical_not(after), known & after))
+        flat = [
+            jnp.concatenate([x_ref[deep + 2 * i].astype(F32), x_ref[deep + 2 * i + 1].astype(F32)], axis=0)
+            for i in range(deep * PAD // by)
+        ]
+        side_halo[swap] = jnp.concatenate(flat, axis=1).T.reshape(deep, PAD, 2 * PAD)
     for plane in range(1, deep - 1):
-        cells = jnp.concatenate([cells_ref[plane], halo[plane * ext : (plane + 1) * ext, :]], axis=1)
+        left = right = jnp.zeros((PAD, by), F32)
+        left_halo = right_halo = jnp.zeros((PAD, 2 * PAD), F32)
+        for swap, (is_left, is_right) in enumerate(sides):
+            came, came_halo = x_refs[swap][plane].astype(F32), side_halo[swap, plane]
+            left = jnp.where(is_left, came, left)
+            right = jnp.where(is_right, came, right)
+            left_halo = jnp.where(is_left, came_halo, left_halo)
+            right_halo = jnp.where(is_right, came_halo, right_halo)
+        cells = jnp.concatenate([left, cells_ref[plane], right], axis=0).astype(BF16)
+        halo = jnp.concatenate([left_halo, halos_ref[plane], right_halo], axis=0).astype(BF16)
+        cells = jnp.concatenate([cells, halo], axis=1)
         cells = jnp.concatenate([cells, cells], axis=0)
         mixed = jnp.dot(xf_ref[...], cells, preferred_element_type=F32).astype(BF16)
         for k in range(views):
@@ -393,35 +440,48 @@
         x, z = link
         return shape((bz if z is None else reach, bx if x is None else PAD, by), dtype)
 
-    swapped = count & (count - 1) == 0 and count <= 4 and part_rows % 8 == 0
-    holders = count if swapped else 0
-    sent = call(
-        functools.partial(prepare_body, views, holders, counts, links),
-        [shape((views, bz, part_rows, by), BF16)] * holders
-        + [link_shape(link, PAD, BF16) for link in links],
-        [VMEM] * 2,
-        nbytes=views * bz * bx * by * 4,
-        name="prepare",
-    )(estimate, recorded)
-    if swapped:
-        parts = [sent[0]] + [
-            lax.ppermute(sent[other], "by", [(i, i ^ other) for i in range(count)])
-            for other in range(1, count)
-        ]
+    side = shape((PAD, bz * bx), BF16)
+    own, order, second = call(
+        columns_body,
+        [shape(block, BF16), side, side],
+        [ANY, VMEM],
+        nbytes=bz * bx * by * 4,
+        name="columns",
+    )(recorded, estimate)
+    first, second = exchange_y(order, second)
+
+    if count & (count - 1) == 0 and count <= 4 and part_rows % 8 == 0:
+        parts = [*call(
+            pieces_body,
+            [shape((views, bz, part_rows, by), BF16)] * count,
+            [ANY, VMEM],
+            nbytes=views * bz * bx * by * 4,
+            name="pieces",
+        )(order, recorded)]
+        for other in range(1, count):
+            parts[other] = lax.ppermute(parts[other], "by", [(i, i ^ other) for i in range(count)])
     else:
         parts = [lax.all_to_all(recorded, "by", split_axis=3, concat_axis=2, tiled=True)]
 
-    came = [exchange(cells, link, *counts) for link, cells in zip(links, sent[holders:])]
-    side = shape((PAD, deep * ext), BF16)
-    cells, first, second = call(
-        functools.partial(join_body, counts, links),
-        [shape((deep, ext, by), BF16), side, side],
-        [VMEM] * (1 + len(links)),
-        [pltpu.VMEM((deep, ext, by), F32)],
-        nbytes=deep * ext * by * 4,
-        name="join",
-    )(estimate, *came)
-    first, second = exchange_y(first, second)
+    along_x, along_z = swaps_of(counts[0]), swaps_of(counts[1])
+    halo, *edges = call(
+        functools.partial(edges_body, count),
+        [shape((bz * bx, 2 * PAD), BF16)] + [shape((PAD + 1, bx, by), BF16)] * len(along_z),
+        [VMEM] * 3,
+        nbytes=bz * bx * by * 4,
+        name="edges",
+    )(own, first, second)
+    edges = [exchange(cells, (None, swap), *counts) for swap, cells in zip(along_z, edges)]
+
+    cells, halos, *edges = call(
+        functools.partial(deep_body, counts, len(along_z)),
+        [shape((deep, bx, by), F32), shape((deep, bx, 2 * PAD), F32)]
+        + [shape((deep + 2 * deep * PAD // by, PAD, by), BF16)] * len(along_x),
+        [ANY] + [VMEM] * (2 + len(along_z)),
+        nbytes=deep * bx * by * 4,
+        name="deep",
+    )(own, own, halo, *edges)
+    edges = [exchange(cells, (swap, None), *counts) for swap, cells in zip(along_x, edges)]
 
     yf, yr, xf, xr, share = call(
         functools.partial(bands_body, views),
@@ -432,25 +492,25 @@
             shape((2 * ext, views * bx), BF16),
             shape(block, F32),
         ],
-        [SMEM] * 2 + [VMEM],
+        [ANY] + [SMEM] * 2 + [VMEM],
         flops=views * 64 * by * by,
         nbytes=views * by * by * 8,
         name="bands",
-    )(profiles, view_boxes, estimate)
+    )(order, profiles, view_boxes, estimate)
 
     gain = call(
-        functools.partial(forward_body, views, block, count),
+        functools.partial(forward_body, views, block, counts, len(along_x)),
         shape((views, bz, bx, by), F32),
-        [SMEM] * 2 + [VMEM] * 5,
+        [SMEM] * 2 + [VMEM] * (4 + len(along_x)),
         [
-            pltpu.VMEM((deep * ext, 2 * PAD), BF16),
+            pltpu.VMEM((max(1, len(along_x)), deep, PAD, 2 * PAD), F32),
             pltpu.VMEM((views, deep * bx, by + 2 * PAD), BF16),
             pltpu.VMEM((deep, bx, by), F32),
         ],
         flops=views * deep * ext * by * 600,
         nbytes=views * bz * bx * by * 8,
         name="forward",
-    )(profiles, view_boxes, cells, first, second, yf, xf)
+    )(profiles, view_boxes, cells, halos, yf, xf, *edges)
 
     side = shape((PAD, views * bz * bx), BF16)
     quot, first, second = call(

time: 48.7 us -> 47.4 us (0.973)
  local copies, waits for them, and re-layouts: 3.48 us -> 2.09 us
  waiting for transfers between devices: 9.71 us -> 10.3 us
    ppermute x3, waiting for transfers between devices: 0.01 us -> 3.73 us  [local(): lax.ppermute(parts[other], 'by', [(i, i ^ other) for i in range(count)])]
    ppermute x6 -> x5, waiting for transfers between devices: 7.19 us -> 3.73 us  [exchange(): return lax.ppermute(cells, ('bx', 'bz'), pairs)]
    unnamed x12 -> x10, local copies, waits for them, and re-layouts: 3.48 us -> 2.09 us
    ppermute x4, starting transfers between devices: 7.76 us -> 6.52 us  [exchange_y(): lax.ppermute(cells, 'by', [(i, partner(i, count, swap)) for i in range(co...]
    ppermute x6 -> x5, starting transfers between devices: 7.6 us -> 8.45 us  [exchange(): return lax.ppermute(cells, ('bx', 'bz'), pairs)]
    pallas_call x3 -> x5, Pallas kernels: 6.06 us -> 6.17 us  [the longest x1 5.24 us: local(): call(functools.partial(forward_body, views, block, counts, len(along_x)),...]
  transfers between devices with their start and end apart: 13 -> 12, of which waited for: 5 -> 5; matrix products, arithmetic and copies ran while one was open for 0% -> 0% of each run, Pallas kernels for 18% -> 18%
where the time goes in v3:
time: 47.4 us; the launch traced here: 47 us
  starting transfers between devices  17.7 us (37%)
  Pallas kernels  16.8 us (35%)
  waiting for transfers between devices  10.3 us (22%)
  local copies, waits for them, and re-layouts  2.09 us (4%)
    ppermute x5, starting transfers between devices, exchange(): return lax.ppermute(cells, ('bx', 'bz'), pairs)  8.45 us
    ppermute x4, starting transfers between devices, exchange_y(): lax.ppermute(cells, 'by', [(i, partner(i, count, swap)) for i in range(co...  6.52 us
    pallas_call x1, Pallas kernels, local(): call(functools.partial(return_body, views, block, count, counts, links),...  6.4 us
    pallas_call x1, Pallas kernels, local(): call(functools.partial(forward_body, views, block, counts, len(along_x)),...  5.24 us
    ppermute x3, waiting for transfers between devices, local(): lax.ppermute(parts[other], 'by', [(i, i ^ other) for i in range(count)])  3.73 us
    ppermute x5, waiting for transfers between devices, exchange(): return lax.ppermute(cells, ('bx', 'bz'), pairs)  3.73 us
    ppermute x4, waiting for transfers between devices, exchange_y(): lax.ppermute(cells, 'by', [(i, partner(i, count, swap)) for i in range(co...  2.84 us
    ppermute x3, starting transfers between devices, local(): lax.ppermute(parts[other], 'by', [(i, i ^ other) for i in range(count)])  2.71 us
  transfers between devices with their start and end apart: 12, of which 5 were waited for; matrix products, arithmetic and copies ran while one was open for 0% of the time, Pallas kernels for 18%

profile of v3, /device:TPU:13, one launch (start us, length us, event | category | flops | bytes accessed | tf_op | source)
XLA Modules:
  0.0 47.0 jit_solution(11866016334560461846)
XLA Ops:
  0.0 0.0 copy-start
  0.0 1.1 %copy-done = bf16[6,16,8,512]{3,2,1,0:T(8,128)(2,1)S(1)} copy-done((bf16[6,16,8,512]{3,2,1,0:T(8,128)(2,1)S(1)}, bf16[6,16,8,512]{3,2,1,0:T(8,128)(2,1)}, u32[]{:S(2)}) %copy-start) | copy-done | bytes 786456
  1.1 0.0 copy-start.1
  1.1 0.9 %copy-done.1 = f32[16,32,128]{2,1,0:T(8,128)S(1)} copy-done((f32[16,32,128]{2,1,0:T(8,128)S(1)}, f32[16,32,128]{2,1,0:T(8,128)}, u32[]{:S(2)}) %copy-start.1) | copy-done | bytes 262168
  2.1 0.0 copy-start.2
  2.1 0.0 copy-start.3
  2.1 0.0 copy-start.4
  2.1 0.2 columns.1
  2.3 0.2 collective-permute-start
  2.5 4.3 %collective-permute-start.1 = (bf16[8,512]{1,0:T(8,128)(2,1)S(1)}, bf16[8,512]{1,0:T(8,128)(2,1)S(1)}, u32[]{:S(2)}, u32[]{:S(2)}) collective-permute-start(bf16[8,512]{1,0:T(8,128)(2,1)S(1)} %get-tuple-element.32), channel_id=1, source_target_pairs={{0,0},{4,8},{8,4},{12,12},{1,1},{5,9},{9,5},{13,13},{2,2},{6,10},{... | collective-permute-start | bytes 24584 | tf_op jit(solution)/shard_map/ppermute | solution.py:78
  6.8 0.2 pieces.1
  6.9 0.1 collective-permute-start.4
  7.0 1.2 %collective-permute-start.5 = (bf16[6,16,8,128]{3,2,1,0:T(8,128)(2,1)S(1)}, bf16[6,16,8,128]{3,2,1,0:T(8,128)(2,1)S(1)}, u32[]{:S(2)}, u32[]{:S(2)}) collective-permute-start(bf16[6,16,8,128]{3,2,1,0:T(8,128)(2,1)S(1)} %get-tuple-element.42), channel_id=1, source_target_pairs={{0,8},{4,12},{8,0},{12,4},{1,9},{5,13},{9,1},{13,5},{2,10},{6,14},... | collective-permute-start | bytes 589832 | tf_op jit(solution)/shard_map/ppermute | solution.py:462
  8.2 1.5 %collective-permute-start.6 = (bf16[6,16,8,128]{3,2,1,0:T(8,128)(2,1)S(1)}, bf16[6,16,8,128]{3,2,1,0:T(8,128)(2,1)S(1)}, u32[]{:S(2)}, u32[]{:S(2)}) collective-permute-start(bf16[6,16,8,128]{3,2,1,0:T(8,128)(2,1)S(1)} %get-tuple-element.43), channel_id=1, source_target_pairs={{0,12},{4,8},{8,4},{12,0},{1,13},{5,9},{9,5},{13,1},{2,14},{6,10},... | collective-permute-start | bytes 589832 | tf_op jit(solution)/shard_map/ppermute | solution.py:462
  9.7 0.0 collective-permute-done.first_ref
  9.7 0.0 collective-permute-done.1.second_ref
  9.7 0.3 edges.1
  9.9 2.1 %collective-permute-start.2 = (bf16[9,32,128]{2,1,0:T(8,128)(2,1)S(1)}, bf16[9,32,128]{2,1,0:T(8,128)(2,1)S(1)}, u32[]{:S(2)}, u32[]{:S(2)}) collective-permute-start(bf16[9,32,128]{2,1,0:T(8,128)(2,1)S(1)} %get-tuple-element.34), channel_id=1, source_target_pairs={{0,1},{1,0},{2,3},{3,2},{4,5},{5,4},{6,7},{7,6},{8,9},{9,8},{10,11... | collective-permute-start | bytes 221192 | tf_op jit(solution)/shard_map/ppermute | solution.py:72
  12.0 0.9 %collective-permute-done.2.refs_0_ = bf16[9,32,128]{2,1,0:T(8,128)(2,1)S(1)} collective-permute-done((bf16[9,32,128]{2,1,0:T(8,128)(2,1)S(1)}, bf16[9,32,128]{2,1,0:T(8,128)(2,1)S(1)}, u32[]{:S(2)}, u32[]{:S(2)}) %collective-permute-start.2) | collective-permute-done | bytes 73760 | tf_op jit(solution)/shard_map/ppermute | solution.py:72
  12.9 0.3 deep.1
  13.3 1.2 %collective-permute-start.3 = (bf16[36,8,128]{2,1,0:T(8,128)(2,1)S(1)}, bf16[36,8,128]{2,1,0:T(8,128)(2,1)S(1)}, u32[]{:S(2)}, u32[]{:S(2)}) collective-permute-start(bf16[36,8,128]{2,1,0:T(8,128)(2,1)S(1)} %get-tuple-element.39), channel_id=1, source_target_pairs={{0,2},{1,3},{2,0},{3,1},{4,6},{5,7},{6,4},{7,5},{8,10},{9,11},{10,... | collective-permute-start | bytes 221192 | tf_op jit(solution)/shard_map/ppermute | solution.py:72
  14.5 0.0 copy-done.2
  14.5 0.0 copy-done.3
  14.5 0.0 copy-done.4
  14.5 2.6 %bands.1 = (bf16[6,144,256]{2,1,0:T(8,128)(2,1)S(1)}, bf16[6,144,256]{2,1,0:T(8,128)(2,1)S(1)}, bf16[192,96]{1,0:T(8,128)(2,1)S(1)}, bf16[96,192]{1,0:T(8,128)(2,1)S(1)}, f32[16,32,128]{2,1,0:T(8,128)S(1)}) custom-call(bf16[8,512]{1,0:T(8,128)(2,1)S(1)} %get-tuple-element.29.order_ref, f32[6,3,15]{2,1,0:T(4,128)S(1)} %copy-done.3, s32[6,6]{1,0:T(8,128)S(1)} %copy-done.4, ...), custom_call_target="tpu_custom_call" | custom-call | flops 4404019 | bytes 550502 | tf_op jit(solution)/shard_map/bands/pallas_call | solution.py:486
  17.1 0.0 collective-permute-done.3.refs_0_
  17.1 5.2 %forward.1.gain_ref = f32[6,16,32,128]{3,2,1,0:T(8,128)S(1)} custom-call(f32[6,3,15]{2,1,0:T(4,128)S(1)} %copy-done.3, s32[6,6]{1,0:T(8,128)S(1)} %copy-done.4, f32[32,32,128]{2,1,0:T(8,128)S(1)} %get-tuple-element.35.cells_ref, f32[32,32,16]{2,1,0:T(8,128)S(1)} %get-tuple-element.36.halos_ref, bf16[6,144,256]{2,1,0:T(8,128)(2,1)S(1)} %get-tuple-element.37.yf_ref, ...), custom_call_target="tpu_custom_call" | custom-call | flops 495452160 | bytes 2202009 | tf_op jit(solution)/shard_map/forward/pallas_call | solution.py:501
  22.4 0.0 collective-permute-done.4.refs_1_
  22.4 0.0 collective-permute-done.5.refs_2_
  22.4 3.7 %collective-permute-done.6.refs_3_ = bf16[6,16,8,128]{3,2,1,0:T(8,128)(2,1)S(1)} collective-permute-done((bf16[6,16,8,128]{3,2,1,0:T(8,128)(2,1)S(1)}, bf16[6,16,8,128]{3,2,1,0:T(8,128)(2,1)S(1)}, u32[]{:S(2)}, u32[]{:S(2)}) %collective-permute-start.6) | collective-permute-done | bytes 196640 | tf_op jit(solution)/shard_map/ppermute | solution.py:462
  26.2 0.8 %quotient.1 = (bf16[6,16,32,128]{3,2,1,0:T(8,128)(2,1)S(1)}, bf16[8,3072]{1,0:T(8,128)(2,1)S(1)}, bf16[8,3072]{1,0:T(8,128)(2,1)S(1)}) custom-call(f32[6,16,32,128]{3,2,1,0:T(8,128)S(1)} %forward.1.gain_ref, bf16[6,16,8,128]{3,2,1,0:T(8,128)(2,1)S(1)} %get-tuple-element.40.refs_0_, bf16[6,16,8,128]{3,2,1,0:T(8,128)(2,1)S(1)} %collective-permute-done.4.refs_1_, ...), custom_call_target="tpu_custom_call" | custom-call | flops 11010048 | bytes 2202009 | tf_op jit(solution)/shard_map/quotient/pallas_call | solution.py:516
  27.0 0.0 collective-permute-start.7
  27.0 2.0 %collective-permute-start.8 = (bf16[8,3072]{1,0:T(8,128)(2,1)S(1)}, bf16[8,3072]{1,0:T(8,128)(2,1)S(1)}, u32[]{:S(2)}, u32[]{:S(2)}) collective-permute-start(bf16[8,3072]{1,0:T(8,128)(2,1)S(1)} %get-tuple-element.46), channel_id=1, source_target_pairs={{0,0},{4,8},{8,4},{12,12},{1,1},{5,9},{9,5},{13,13},{2,2},{6,10},{... | collective-permute-start | bytes 147464 | tf_op jit(solution)/shard_map/ppermute | solution.py:78
  29.0 0.9 %collective-permute-done.7.first_ref = bf16[8,3072]{1,0:T(8,128)(2,1)S(1)} collective-permute-done((bf16[8,3072]{1,0:T(8,128)(2,1)S(1)}, bf16[8,3072]{1,0:T(8,128)(2,1)S(1)}, u32[]{:S(2)}, u32[]{:S(2)}) %collective-permute-start.7) | collective-permute-done | bytes 49184 | tf_op jit(solution)/shard_map/ppermute | solution.py:78
  30.0 1.9 %collective-permute-done.8.second_ref = bf16[8,3072]{1,0:T(8,128)(2,1)S(1)} collective-permute-done((bf16[8,3072]{1,0:T(8,128)(2,1)S(1)}, bf16[8,3072]{1,0:T(8,128)(2,1)S(1)}, u32[]{:S(2)}, u32[]{:S(2)}) %collective-permute-start.8) | collective-permute-done | bytes 49184 | tf_op jit(solution)/shard_map/ppermute | solution.py:78
  31.9 6.4 %returned.1 = (f32[16,32,128]{2,1,0:T(8,128)S(1)}, f32[7,32,128]{2,1,0:T(8,128)S(1)}, f32[16,8,128]{2,1,0:T(8,128)S(1)}, f32[7,8,128]{2,1,0:T(8,128)S(1)}) custom-call(f32[6,3,15]{2,1,0:T(4,128)S(1)} %copy-done.3, s32[6,6]{1,0:T(8,128)S(1)} %copy-done.4, bf16[6,16,32,128]{3,2,1,0:T(8,128)(2,1)S(1)} %get-tuple-element.44.quot_ref, ...), custom_call_target="tpu_custom_call" | custom-call | flops 247726080 | bytes 2202009 | tf_op jit(solution)/shard_map/returned/pallas_call | solution.py:527
  38.3 3.4 %collective-permute-start.9 = (f32[7,32,128]{2,1,0:T(8,128)S(1)}, f32[7,32,128]{2,1,0:T(8,128)S(1)}, u32[]{:S(2)}, u32[]{:S(2)}) collective-permute-start(f32[7,32,128]{2,1,0:T(8,128)S(1)} %get-tuple-element.50), channel_id=1, source_target_pairs={{0,1},{1,0},{2,3},{3,2},{4,5},{5,4},{6,7},{7,6},{8,9},{9,8},{10,11... | collective-permute-start | bytes 344072 | tf_op jit(solution)/shard_map/ppermute | solution.py:72
  41.7 1.2 %collective-permute-start.10 = (f32[16,8,128]{2,1,0:T(8,128)S(1)}, f32[16,8,128]{2,1,0:T(8,128)S(1)}, u32[]{:S(2)}, u32[]{:S(2)}) collective-permute-start(f32[16,8,128]{2,1,0:T(8,128)S(1)} %get-tuple-element.51), channel_id=1, source_target_pairs={{0,2},{1,3},{2,0},{3,1},{4,6},{5,7},{6,4},{7,5},{8,10},{9,11},{10,... | collective-permute-start | bytes 196616 | tf_op jit(solution)/shard_map/ppermute | solution.py:72
  42.9 0.5 %collective-permute-start.11 = (f32[7,8,128]{2,1,0:T(8,128)S(1)}, f32[7,8,128]{2,1,0:T(8,128)S(1)}, u32[]{:S(2)}, u32[]{:S(2)}) collective-permute-start(f32[7,8,128]{2,1,0:T(8,128)S(1)} %get-tuple-element.52), channel_id=1, source_target_pairs={{0,3},{1,2},{2,1},{3,0},{4,7},{5,6},{6,5},{7,4},{8,11},{9,10},{10,... | collective-permute-start | bytes 86024 | tf_op jit(solution)/shard_map/ppermute | solution.py:72
  43.4 2.8 %collective-permute-done.11.refs_2_ = f32[7,8,128]{2,1,0:T(8,128)S(1)} collective-permute-done((f32[7,8,128]{2,1,0:T(8,128)S(1)}, f32[7,8,128]{2,1,0:T(8,128)S(1)}, u32[]{:S(2)}, u32[]{:S(2)}) %collective-permute-start.11) | collective-permute-done | bytes 28704 | tf_op jit(solution)/shard_map/ppermute | solution.py:72
  46.2 0.0 collective-permute-done.10.refs_1_
  46.2 0.0 collective-permute-done.9.refs_0_
  46.2 0.8 %finish.1 = f32[16,32,128]{2,1,0:T(8,128)} custom-call(f32[16,32,128]{2,1,0:T(8,128)S(1)} %get-tuple-element.30.share_ref, f32[16,32,128]{2,1,0:T(8,128)S(1)} %get-tuple-element.49.mid_ref, f32[7,32,128]{2,1,0:T(8,128)S(1)} %collective-permute-done.9.refs_0_, f32[16,8,128]{2,1,0:T(8,128)S(1)} %collective-permute-done.10.refs_1_, ...), custom_call_target="tpu_custom_call" | custom-call | bytes 550502 | tf_op jit(solution)/shard_map/finish/pallas_call | solution.py:543
Async XLA Ops:
  0.0 1.1 %copy-start = (bf16[6,16,8,512]{3,2,1,0:T(8,128)(2,1)S(1)}, bf16[6,16,8,512]{3,2,1,0:T(8,128)(2,1)}, u32[]{:S(2)}) copy-start(bf16[6,16,8,512]{3,2,1,0:T(8,128)(2,1)} %rec_ref.3) | copy-start | bytes 2359300
  1.1 0.9 %copy-start.1 = (f32[16,32,128]{2,1,0:T(8,128)S(1)}, f32[16,32,128]{2,1,0:T(8,128)}, u32[]{:S(2)}) copy-start(f32[16,32,128]{2,1,0:T(8,128)} %est_ref.3) | copy-start | bytes 786436
  2.1 12.4 %copy-start.2 = (f32[16,32,128]{2,1,0:T(8,128)S(1)}, f32[16,32,128]{2,1,0:T(8,128)}, u32[]{:S(2)}) copy-start(f32[16,32,128]{2,1,0:T(8,128)} %est_ref.3) | copy-start | bytes 786436
  2.1 12.4 %copy-start.3 = (f32[6,3,15]{2,1,0:T(4,128)S(1)}, f32[6,3,15]{2,1,0:T(4,128)}, u32[]{:S(2)}) copy-start(f32[6,3,15]{2,1,0:T(4,128)} %prof_ref.5) | copy-start | bytes 3244
  2.1 12.4 %copy-start.4 = (s32[6,6]{1,0:T(8,128)S(1)}, s32[6,6]{1,0:T(8,128)}, u32[]{:S(2)}) copy-start(s32[6,6]{1,0:T(8,128)} %box_ref.5) | copy-start | bytes 436
  2.3 7.4 %collective-permute-start = (bf16[8,512]{1,0:T(8,128)(2,1)S(1)}, bf16[8,512]{1,0:T(8,128)(2,1)S(1)}, u32[]{:S(2)}, u32[]{:S(2)}) collective-permute-start(bf16[8,512]{1,0:T(8,128)(2,1)S(1)} %get-tuple-element.29.order_ref), channel_id=1, source_target_pairs={{0,4},{4,0},{8,12},{12,8},{1,5},{5,1},{9,13},{13,9},{2,6},{6,2},{1... | collective-permute-start | bytes 24584 | tf_op jit(solution)/shard_map/ppermute | solution.py:78
  2.5 7.2 %collective-permute-start.1 = (bf16[8,512]{1,0:T(8,128)(2,1)S(1)}, bf16[8,512]{1,0:T(8,128)(2,1)S(1)}, u32[]{:S(2)}, u32[]{:S(2)}) collective-permute-start(bf16[8,512]{1,0:T(8,128)(2,1)S(1)} %get-tuple-element.32), channel_id=1, source_target_pairs={{0,0},{4,8},{8,4},{12,12},{1,1},{5,9},{9,5},{13,13},{2,2},{6,10},{... | collective-permute-start | bytes 24584 | tf_op jit(solution)/shard_map/ppermute | solution.py:78
  6.9 15.5 %collective-permute-start.4 = (bf16[6,16,8,128]{3,2,1,0:T(8,128)(2,1)S(1)}, bf16[6,16,8,128]{3,2,1,0:T(8,128)(2,1)S(1)}, u32[]{:S(2)}, u32[]{:S(2)}) collective-permute-start(bf16[6,16,8,128]{3,2,1,0:T(8,128)(2,1)S(1)} %get-tuple-element.41), channel_id=1, source_target_pairs={{0,4},{4,0},{8,12},{12,8},{1,5},{5,1},{9,13},{13,9},{2,6},{6,2},{1... | collective-permute-start | bytes 589832 | tf_op jit(solution)/shard_map/ppermute | solution.py:462
  7.0 15.4 %collective-permute-start.5 = (bf16[6,16,8,128]{3,2,1,0:T(8,128)(2,1)S(1)}, bf16[6,16,8,128]{3,2,1,0:T(8,128)(2,1)S(1)}, u32[]{:S(2)}, u32[]{:S(2)}) collective-permute-start(bf16[6,16,8,128]{3,2,1,0:T(8,128)(2,1)S(1)} %get-tuple-element.42), channel_id=1, source_target_pairs={{0,8},{4,12},{8,0},{12,4},{1,9},{5,13},{9,1},{13,5},{2,10},{6,14},... | collective-permute-start | bytes 589832 | tf_op jit(solution)/shard_map/ppermute | solution.py:462
  8.2 17.9 %collective-permute-start.6 = (bf16[6,16,8,128]{3,2,1,0:T(8,128)(2,1)S(1)}, bf16[6,16,8,128]{3,2,1,0:T(8,128)(2,1)S(1)}, u32[]{:S(2)}, u32[]{:S(2)}) collective-permute-start(bf16[6,16,8,128]{3,2,1,0:T(8,128)(2,1)S(1)} %get-tuple-element.43), channel_id=1, source_target_pairs={{0,12},{4,8},{8,4},{12,0},{1,13},{5,9},{9,5},{13,1},{2,14},{6,10},... | collective-permute-start | bytes 589832 | tf_op jit(solution)/shard_map/ppermute | solution.py:462
  9.9 3.0 %collective-permute-start.2 = (bf16[9,32,128]{2,1,0:T(8,128)(2,1)S(1)}, bf16[9,32,128]{2,1,0:T(8,128)(2,1)S(1)}, u32[]{:S(2)}, u32[]{:S(2)}) collective-permute-start(bf16[9,32,128]{2,1,0:T(8,128)(2,1)S(1)} %get-tuple-element.34), channel_id=1, source_target_pairs={{0,1},{1,0},{2,3},{3,2},{4,5},{5,4},{6,7},{7,6},{8,9},{9,8},{10,11... | collective-permute-start | bytes 221192 | tf_op jit(solution)/shard_map/ppermute | solution.py:72
  13.3 3.9 %collective-permute-start.3 = (bf16[36,8,128]{2,1,0:T(8,128)(2,1)S(1)}, bf16[36,8,128]{2,1,0:T(8,128)(2,1)S(1)}, u32[]{:S(2)}, u32[]{:S(2)}) collective-permute-start(bf16[36,8,128]{2,1,0:T(8,128)(2,1)S(1)} %get-tuple-element.39), channel_id=1, source_target_pairs={{0,2},{1,3},{2,0},{3,1},{4,6},{5,7},{6,4},{7,5},{8,10},{9,11},{10,... | collective-permute-start | bytes 221192 | tf_op jit(solution)/shard_map/ppermute | solution.py:72
  27.0 3.0 %collective-permute-start.7 = (bf16[8,3072]{1,0:T(8,128)(2,1)S(1)}, bf16[8,3072]{1,0:T(8,128)(2,1)S(1)}, u32[]{:S(2)}, u32[]{:S(2)}) collective-permute-start(bf16[8,3072]{1,0:T(8,128)(2,1)S(1)} %get-tuple-element.45), channel_id=1, source_target_pairs={{0,4},{4,0},{8,12},{12,8},{1,5},{5,1},{9,13},{13,9},{2,6},{6,2},{1... | collective-permute-start | bytes 147464 | tf_op jit(solution)/shard_map/ppermute | solution.py:78
  27.0 4.8 %collective-permute-start.8 = (bf16[8,3072]{1,0:T(8,128)(2,1)S(1)}, bf16[8,3072]{1,0:T(8,128)(2,1)S(1)}, u32[]{:S(2)}, u32[]{:S(2)}) collective-permute-start(bf16[8,3072]{1,0:T(8,128)(2,1)S(1)} %get-tuple-element.46), channel_id=1, source_target_pairs={{0,0},{4,8},{8,4},{12,12},{1,1},{5,9},{9,5},{13,13},{2,2},{6,10},{... | collective-permute-start | bytes 147464 | tf_op jit(solution)/shard_map/ppermute | solution.py:78
  38.3 8.0 %collective-permute-start.9 = (f32[7,32,128]{2,1,0:T(8,128)S(1)}, f32[7,32,128]{2,1,0:T(8,128)S(1)}, u32[]{:S(2)}, u32[]{:S(2)}) collective-permute-start(f32[7,32,128]{2,1,0:T(8,128)S(1)} %get-tuple-element.50), channel_id=1, source_target_pairs={{0,1},{1,0},{2,3},{3,2},{4,5},{5,4},{6,7},{7,6},{8,9},{9,8},{10,11... | collective-permute-start | bytes 344072 | tf_op jit(solution)/shard_map/ppermute | solution.py:72
  41.7 4.5 %collective-permute-start.10 = (f32[16,8,128]{2,1,0:T(8,128)S(1)}, f32[16,8,128]{2,1,0:T(8,128)S(1)}, u32[]{:S(2)}, u32[]{:S(2)}) collective-permute-start(f32[16,8,128]{2,1,0:T(8,128)S(1)} %get-tuple-element.51), channel_id=1, source_target_pairs={{0,2},{1,3},{2,0},{3,1},{4,6},{5,7},{6,4},{7,5},{8,10},{9,11},{10,... | collective-permute-start | bytes 196616 | tf_op jit(solution)/shard_map/ppermute | solution.py:72
  42.9 3.3 %collective-permute-start.11 = (f32[7,8,128]{2,1,0:T(8,128)S(1)}, f32[7,8,128]{2,1,0:T(8,128)S(1)}, u32[]{:S(2)}, u32[]{:S(2)}) collective-permute-start(f32[7,8,128]{2,1,0:T(8,128)S(1)} %get-tuple-element.52), channel_id=1, source_target_pairs={{0,3},{1,2},{2,1},{3,0},{4,7},{5,6},{6,5},{7,4},{8,11},{9,10},{10,... | collective-permute-start | bytes 86024 | tf_op jit(solution)/shard_map/ppermute | solution.py:72

commit v4 on v3

--- a/solution.py
+++ b/solution.py
@@ -10,8 +10,9 @@
 TAPS = 15
 REACH = TAPS // 2
 PAD = 8
+SIDE = 2 * PAD
 BACKGROUND = 0.05
-WEIGHT = 0.7
+WEIGHT = 0.8
 
 F32 = jnp.float32
 BF16 = jnp.bfloat16
@@ -94,19 +95,12 @@
 
 def packed(cells, begin):
     by = cells.shape[1]
-    row = lax.broadcasted_iota(jnp.int32, (PAD, by), 0)
-    col = lax.broadcasted_iota(jnp.int32, (PAD, by), 1)
+    row = lax.broadcasted_iota(jnp.int32, (SIDE, by), 0)
+    col = lax.broadcasted_iota(jnp.int32, (SIDE, by), 1)
     pick = jnp.where(col == row + begin, 1.0, 0.0).astype(BF16)
     return lax.dot_general(
         pick, cells, (((1,), (1,)), ((), ())), preferred_element_type=F32
     ).astype(BF16)
-
-
-def pack_both(cells, by, first_ref, second_ref):
-    last = by - PAD
-    mine = lax.axis_index("by")
-    first_ref[...] = packed(cells, jnp.where(meets_next(mine, 0), last, 0))
-    second_ref[...] = packed(cells, jnp.where(meets_next(mine, 1), last, 0))
 
 
 def unpack_both(count, first_ref, second_ref):
@@ -123,14 +117,38 @@
 def columns_body(rec_ref, est_ref, cells_ref, first_ref, second_ref):
     bz, bx, by = est_ref.shape
     cells_ref[...] = est_ref[...].astype(BF16)
-    pack_both(cells_ref[...].reshape(bz * bx, by), by, first_ref, second_ref)
+    cells = cells_ref[...].reshape(bz * bx, by)
+    mine = lax.axis_index("by")
+    first_ref[...] = packed(cells, jnp.where(meets_next(mine, 0), by - SIDE, 0))
+    second_ref[...] = packed(cells, jnp.where(meets_next(mine, 1), by - SIDE, 0))
 
 
 def pieces_body(order_ref, rec_ref, *out_refs):
-    by = out_refs[0].shape[3]
+    views, bz, rows, width = rec_ref.shape
+    count = len(out_refs)
+    by = width // count
+    row = lax.broadcasted_iota(jnp.int32, (by, by), 0)
+    col = lax.broadcasted_iota(jnp.int32, (by, by), 1)
+    picks = []
+    for k in range(views):
+        lane = col - 2 * PAD * k
+        picks.append((lane >= 0) & (lane < PAD) & (row == by - PAD + lane))
+        picks.append((lane >= PAD) & (lane < 2 * PAD) & (row == lane - PAD))
+    picks = jnp.concatenate([jnp.where(pick, 1.0, 0.0).astype(BF16) for pick in picks], axis=0)
     for other, out_ref in enumerate(out_refs):
-        at = pl.ds(pl.multiple_of((lax.axis_index("by") ^ other) * by, by), by)
-        out_ref[...] = rec_ref[:, :, :, at]
+        target = lax.axis_index("by") ^ other
+
+        def columns(tile):
+            return pl.ds(pl.multiple_of(jnp.clip(tile, 0, count - 1) * by, by), by)
+
+        out_ref[:views] = rec_ref[:, :, :, columns(target)]
+        beside = []
+        for k in range(views):
+            for tile in (target - 1, target + 1):
+                cells = rec_ref[k, :, :, columns(tile)]
+                beside.append(cells.astype(F32).reshape(bz * rows, by).astype(BF16))
+        beside = jnp.dot(jnp.concatenate(beside, axis=1), picks, preferred_element_type=F32)
+        out_ref[views] = beside.reshape(bz, rows, by).astype(BF16)
 
 
 def upright(cells):
@@ -156,7 +174,7 @@
         rows = halo_ref[pl.ds(pl.multiple_of(begin * bx, PAD * bx), PAD * bx), :]
         flat = lying(rows).astype(BF16)
         for i in range(PAD * bx // by):
-            out_ref[PAD, 2 * PAD * i : 2 * PAD * (i + 1), :] = flat[:, i * by : (i + 1) * by]
+            out_ref[PAD + i, : 2 * SIDE, :] = flat[:, i * by : (i + 1) * by]
 
 
 def deep_body(counts, count_z, order_ref, est_ref, halo_ref, *refs):
@@ -166,7 +184,7 @@
     cells_ref[...] = jnp.zeros_like(cells_ref)
     halos_ref[...] = jnp.zeros_like(halos_ref)
     cells_ref[PAD : PAD + bz] = est_ref[...].astype(F32)
-    halos_ref[PAD : PAD + bz] = halo_ref[...].astype(F32).reshape(bz, bx, 2 * PAD)
+    halos_ref[PAD : PAD + bz] = halo_ref[...].astype(F32).reshape(bz, bx, 2 * SIDE)
     for swap, z_ref in enumerate(z_refs):
         index = lax.axis_index("bz")
         at = pl.ds(jnp.where(meets_next(index, swap), PAD + bz, 0), PAD)
@@ -175,22 +193,23 @@
         def _():
             cells_ref[at] = z_ref[:PAD].astype(F32)
             flat = jnp.concatenate(
-                [z_ref[PAD, 2 * PAD * i : 2 * PAD * (i + 1), :] for i in range(PAD * bx // by)], axis=1
+                [z_ref[PAD + i, : 2 * SIDE, :] for i in range(PAD * bx // by)], axis=1
             )
-            halos_ref[at] = upright(flat).reshape(PAD, bx, 2 * PAD)
+            halos_ref[at] = upright(flat).reshape(PAD, bx, 2 * SIDE)
 
     for swap, out_ref in enumerate(out_refs):
         begin = jnp.where(meets_next(lax.axis_index("bx"), swap), bx - PAD, 0)
         at = pl.ds(pl.multiple_of(begin, PAD), PAD)
         out_ref[:deep] = cells_ref[:, at, :].astype(BF16)
-        flat = lying(halos_ref[:, at, :].reshape(deep * PAD, 2 * PAD))
+        flat = lying(halos_ref[:, at, :].reshape(deep * PAD, 2 * SIDE))
+        groups = 2 * SIDE // PAD
         for i in range(deep * PAD // by):
-            part = flat[:, i * by : (i + 1) * by]
-            out_ref[deep + 2 * i] = part[:PAD].astype(BF16)
-            out_ref[deep + 2 * i + 1] = part[PAD:].astype(BF16)
-
-
-def bands_body(views, order_ref, prof_ref, box_ref, est_ref, yf_ref, yr_ref, xf_ref, xr_ref, share_ref):
+            for j in range(groups):
+                part = flat[j * PAD : (j + 1) * PAD, i * by : (i + 1) * by]
+                out_ref[deep + groups * i + j] = part.astype(BF16)
+
+
+def bands_body(views, order_ref, prof_ref, box_ref, est_ref, yf_ref, yh_ref, yr_ref, xf_ref, xr_ref, share_ref):
     bz, bx, by = est_ref.shape
     ext = bx + 2 * PAD
     start_z = lax.axis_index("bz") * bz
@@ -200,10 +219,16 @@
     def iota(shape, dim):
         return lax.broadcasted_iota(jnp.int32, shape, dim)
 
-    shape_y = (by + 2 * PAD, by)
+    shape_y = (by + 2 * SIDE, by)
     row = iota(shape_y, 0)
-    source = jnp.where(row < by, row, jnp.where(row < by + PAD, row - by - PAD, row - PAD))
+    source = jnp.where(row < by, row, jnp.where(row < by + SIDE, row - by - SIDE, row - SIDE))
     target = iota(shape_y, 1)
+    beside_view = lax.div(target, 2 * PAD)
+    beside = lax.rem(target, 2 * PAD)
+    beside = jnp.where(beside < PAD, beside - PAD, by + beside - PAD)
+    back_row, back_target = iota((by, by), 0), iota((by, by), 1)
+    side_row, side_target = iota((2 * PAD, by), 0), iota((2 * PAD, by), 1)
+    side_row = jnp.where(side_row < PAD, side_row - PAD, by + side_row - PAD)
     shape_x = (bx, 2 * ext)
     col = iota(shape_x, 1)
     is_low = col >= ext
@@ -214,11 +239,24 @@
         high, low = halves(forward)
         yf_ref[k, :, :by] = high
         yf_ref[k, :, by:] = low
-        back = banded(REACH - source + target, lambda tap: prof_ref[k, 2, tap])
-        within = (target >= box_ref[k, 4] - start_y) & (target < box_ref[k, 5] - start_y)
-        high, low = halves(jnp.where(within, back, 0.0))
-        yr_ref[k, :, :by] = high
-        yr_ref[k, :, by:] = low
+        forward = banded(source - beside + REACH, lambda tap: prof_ref[k, 2, tap])
+        high, low = halves(jnp.where(beside_view == k, forward, 0.0))
+        yh_ref[k, :, :by] = high
+        yh_ref[k, :, by:] = low
+
+        def back(row, target):
+            within = (target >= box_ref[k, 4] - start_y) & (target < box_ref[k, 5] - start_y)
+            matrix = banded(REACH - row + target, lambda tap: prof_ref[k, 2, tap])
+            return halves(jnp.where(within, matrix, 0.0))
+
+        high, low = back(back_row, back_target)
+        yr_ref[k, :by, :by] = high
+        yr_ref[k, :by, by:] = low
+        yr_ref[k, by:, :] = jnp.zeros((by, 2 * by), BF16)
+        at = pl.ds(pl.multiple_of(by + 2 * PAD * k, 2 * PAD), 2 * PAD)
+        high, low = back(side_row, side_target)
+        yr_ref[k, at, :by] = high
+        yr_ref[k, at, by:] = low
         high, low = halves(banded(forward_x + REACH, lambda tap: prof_ref[k, 1, tap]))
         at = pl.ds(pl.multiple_of(k * bx, bx), bx)
         xf_ref[at, :] = jnp.where(is_low, low.astype(F32), high.astype(F32)).astype(BF16)
@@ -257,7 +295,7 @@
         share_ref[plane] = est_ref[plane] / coverage
 
 
-def forward_body(views, block, counts, count_x, prof_ref, box_ref, cells_ref, halos_ref, yf_ref, xf_ref, *refs):
+def forward_body(views, block, counts, count_x, prof_ref, box_ref, cells_ref, halos_ref, yf_ref, yh_ref, xf_ref, *refs):
     x_refs, (gain_ref, side_halo, blurred_x, rows) = refs[:count_x], refs[count_x:]
     bz, bx, by = block
     deep = bz + 2 * PAD
@@ -267,14 +305,15 @@
         known = has_partner(index, counts[0], swap)
         after = meets_next(index, swap)
         sides.append((known & jnp.logical_not(after), known & after))
+        groups = 2 * SIDE // PAD
         flat = [
-            jnp.concatenate([x_ref[deep + 2 * i].astype(F32), x_ref[deep + 2 * i + 1].astype(F32)], axis=0)
+            jnp.concatenate([x_ref[deep + groups * i + j].astype(F32) for j in range(groups)], axis=0)
             for i in range(deep * PAD // by)
         ]
-        side_halo[swap] = jnp.concatenate(flat, axis=1).T.reshape(deep, PAD, 2 * PAD)
+        side_halo[swap] = jnp.concatenate(flat, axis=1).T.reshape(deep, PAD, 2 * SIDE)
     for plane in range(1, deep - 1):
         left = right = jnp.zeros((PAD, by), F32)
-        left_halo = right_halo = jnp.zeros((PAD, 2 * PAD), F32)
+        left_halo = right_halo = jnp.zeros((PAD, 2 * SIDE), F32)
         for swap, (is_left, is_right) in enumerate(sides):
             came, came_halo = x_refs[swap][plane].astype(F32), side_halo[swap, plane]
             left = jnp.where(is_left, came, left)
@@ -323,10 +362,45 @@
 
     lax.fori_loop(0, views, view, 0)
 
+    lane = lax.broadcasted_iota(jnp.int32, (8, by), 1)
+    owner = lax.div(lane, 2 * PAD)
+    col_y = lax.rem(lane, 2 * PAD)
+    col_y = jnp.where(col_y < PAD, col_y - PAD, by + col_y - PAD) + lax.axis_index("by") * by
+
+    def by_lane(value, start):
+        for k in range(views):
+            start = jnp.where(owner == k, value(k), start)
+        return start
+
+    taps = [by_lane(lambda k: prof_ref[k, 0, tap], jnp.zeros((8, by), F32)) for tap in range(TAPS)]
+    box = [by_lane(lambda k: box_ref[k, i], jnp.zeros((8, by), jnp.int32)) for i in range(6)]
+    within_y = (col_y >= box[4]) & (col_y < box[5])
+    step = 5
+    for first in range(1, deep - 1, step):
+        at = slice(first * bx, (first + step) * bx)
+        mixed = jnp.dot(blurred_x[0, at, :], yh_ref[0], preferred_element_type=F32)
+        for k in range(1, views):
+            mixed = mixed + jnp.dot(blurred_x[k, at, :], yh_ref[k], preferred_element_type=F32)
+        rows[first : first + step] = (mixed[:, :by] + mixed[:, by:]).reshape(step, bx, by)
+
+    def beside_plane(plane, carry):
+        at_z = plane + start_z
+        within_z = within_y & (at_z >= box[0]) & (at_z < box[1])
+        for tile in range(0, bx, 8):
+            at_x = row_x + tile
+            total = taps[0] * rows[plane + 1, tile : tile + 8, :]
+            for tap in range(1, TAPS):
+                total = total + taps[tap] * rows[plane + 1 + tap, tile : tile + 8, :]
+            within = within_z & (at_x >= box[2]) & (at_x < box[3])
+            gain_ref[views, plane, tile : tile + 8, :] = jnp.where(within, 1.0, 0.0) / (total + BACKGROUND)
+        return carry
+
+    lax.fori_loop(0, bz, beside_plane, 0)
+
 
 def quotient_body(views, block, count, gain_ref, *refs):
     parts = refs[:count]
-    quot_ref, first_ref, second_ref, held = refs[count:]
+    quot_ref, held = refs[count:]
     bz, bx, by = block
     rows = bx // count
     mine = lax.axis_index("by") if count > 1 else 0
@@ -338,23 +412,20 @@
         quot_ref[k] = held[...].astype(BF16)
         return carry
 
-    lax.fori_loop(0, views, view, 0)
-    pack_both(quot_ref[...].reshape(views * bz * bx, by), by, first_ref, second_ref)
-
-
-def return_body(views, block, count, counts, links, prof_ref, box_ref, quot_ref, first_ref, second_ref, yr_ref, xr_ref, mid_ref, *refs):
+    lax.fori_loop(0, views + 1, view, 0)
+
+
+def return_body(views, block, links, prof_ref, box_ref, quot_ref, yr_ref, xr_ref, mid_ref, *refs):
     bz, bx, by = block
     ext = bx + 2 * PAD
     deep = bz + 2 * REACH
     link_refs = refs[: len(links)]
-    halo, rows, high_rows, low_rows, total = refs[len(links) :]
-    halo[...] = unpack_both(count, first_ref, second_ref)
+    rows, high_rows, low_rows, total = refs[len(links) :]
     start_z = lax.axis_index("bz") * bz
 
     def view(k, carry):
-        start = pl.multiple_of(k * (bz * bx), bz * bx)
-        cells = quot_ref[k].reshape(bz * bx, by)
-        cells = jnp.concatenate([cells, halo[pl.ds(start, bz * bx), :]], axis=1)
+        cells = [quot_ref[i].reshape(bz * bx, by) for i in (k, views)]
+        cells = jnp.concatenate(cells, axis=1)
         mixed = jnp.dot(cells, yr_ref[k], preferred_element_type=F32)
         rows[...] = (mixed[:, :by] + mixed[:, by:]).reshape(bz, bx, by)
         taps = [prof_ref[k, 0, tap] for tap in range(TAPS)]
@@ -440,7 +511,7 @@
         x, z = link
         return shape((bz if z is None else reach, bx if x is None else PAD, by), dtype)
 
-    side = shape((PAD, bz * bx), BF16)
+    side = shape((SIDE, bz * bx), BF16)
     own, order, second = call(
         columns_body,
         [shape(block, BF16), side, side],
@@ -453,7 +524,7 @@
     if count & (count - 1) == 0 and count <= 4 and part_rows % 8 == 0:
         parts = [*call(
             pieces_body,
-            [shape((views, bz, part_rows, by), BF16)] * count,
+            [shape((views + 1, bz, part_rows, by), BF16)] * count,
             [ANY, VMEM],
             nbytes=views * bz * bx * by * 4,
             name="pieces",
@@ -461,12 +532,21 @@
         for other in range(1, count):
             parts[other] = lax.ppermute(parts[other], "by", [(i, i ^ other) for i in range(count)])
     else:
-        parts = [lax.all_to_all(recorded, "by", split_axis=3, concat_axis=2, tiled=True)]
+        tiles = jnp.moveaxis(recorded.reshape(views, bz, part_rows, count, by), 3, 0)
+        before = jnp.roll(tiles[..., by - PAD :], 1, axis=0)
+        after = jnp.roll(tiles[..., :PAD], -1, axis=0)
+        beside = jnp.moveaxis(jnp.concatenate([before, after], axis=-1), 1, 3)
+        beside = beside.reshape(count, 1, bz, part_rows, views * 2 * PAD)
+        beside = jnp.pad(beside, [(0, 0)] * 4 + [(0, by - views * 2 * PAD)])
+        tiles = jnp.concatenate([tiles, beside], axis=1)
+        tiles = lax.all_to_all(tiles, "by", split_axis=0, concat_axis=0, tiled=True)
+        parts = [jnp.moveaxis(tiles, 0, 2).reshape(views + 1, bz, bx, by)]
 
     along_x, along_z = swaps_of(counts[0]), swaps_of(counts[1])
     halo, *edges = call(
         functools.partial(edges_body, count),
-        [shape((bz * bx, 2 * PAD), BF16)] + [shape((PAD + 1, bx, by), BF16)] * len(along_z),
+        [shape((bz * bx, 2 * SIDE), BF16)]
+        + [shape((PAD + PAD * bx // by, bx, by), BF16)] * len(along_z),
         [VMEM] * 3,
         nbytes=bz * bx * by * 4,
         name="edges",
@@ -475,19 +555,20 @@
 
     cells, halos, *edges = call(
         functools.partial(deep_body, counts, len(along_z)),
-        [shape((deep, bx, by), F32), shape((deep, bx, 2 * PAD), F32)]
-        + [shape((deep + 2 * deep * PAD // by, PAD, by), BF16)] * len(along_x),
+        [shape((deep, bx, by), F32), shape((deep, bx, 2 * SIDE), F32)]
+        + [shape((deep + 2 * SIDE * deep // by, PAD, by), BF16)] * len(along_x),
         [ANY] + [VMEM] * (2 + len(along_z)),
         nbytes=deep * bx * by * 4,
         name="deep",
     )(own, own, halo, *edges)
     edges = [exchange(cells, (swap, None), *counts) for swap, cells in zip(along_x, edges)]
 
-    yf, yr, xf, xr, share = call(
+    yf, yh, yr, xf, xr, share = call(
         functools.partial(bands_body, views),
         [
-            shape((views, by + 2 * PAD, 2 * by), BF16),
-            shape((views, by + 2 * PAD, 2 * by), BF16),
+            shape((views, by + 2 * SIDE, 2 * by), BF16),
+            shape((views, by + 2 * SIDE, 2 * by), BF16),
+            shape((views, 2 * by, 2 * by), BF16),
             shape((views * bx, 2 * ext), BF16),
             shape((2 * ext, views * bx), BF16),
             shape(block, F32),
@@ -500,36 +581,33 @@
 
     gain = call(
         functools.partial(forward_body, views, block, counts, len(along_x)),
-        shape((views, bz, bx, by), F32),
-        [SMEM] * 2 + [VMEM] * (4 + len(along_x)),
+        shape((views + 1, bz, bx, by), F32),
+        [SMEM] * 2 + [VMEM] * (5 + len(along_x)),
         [
-            pltpu.VMEM((max(1, len(along_x)), deep, PAD, 2 * PAD), F32),
-            pltpu.VMEM((views, deep * bx, by + 2 * PAD), BF16),
+            pltpu.VMEM((max(1, len(along_x)), deep, PAD, 2 * SIDE), F32),
+            pltpu.VMEM((views, deep * bx, by + 2 * SIDE), BF16),
             pltpu.VMEM((deep, bx, by), F32),
         ],
         flops=views * deep * ext * by * 600,
         nbytes=views * bz * bx * by * 8,
         name="forward",
-    )(profiles, view_boxes, cells, halos, yf, xf, *edges)
-
-    side = shape((PAD, views * bz * bx), BF16)
-    quot, first, second = call(
+    )(profiles, view_boxes, cells, halos, yf, yh, xf, *edges)
+
+    quot = call(
         functools.partial(quotient_body, views, block, len(parts)),
-        [shape((views, bz, bx, by), BF16), side, side],
+        shape((views + 1, bz, bx, by), BF16),
         [VMEM] * (1 + len(parts)),
         [pltpu.VMEM((bz, bx, by), F32)],
         flops=views * bz * bx * by * 40,
         nbytes=views * bz * bx * by * 8,
         name="quotient",
     )(gain, *parts)
-    first, second = exchange_y(first, second)
 
     mid, *sums = call(
-        functools.partial(return_body, views, block, count, counts, links),
+        functools.partial(return_body, views, block, links),
         [shape(block, F32)] + [link_shape(link, REACH, F32) for link in links],
-        [SMEM] * 2 + [VMEM] * 5,
+        [SMEM] * 2 + [VMEM] * 3,
         [
-            pltpu.VMEM((views * bz * bx, 2 * PAD), BF16),
             pltpu.VMEM((bz, bx, by), F32),
             pltpu.VMEM((bz + 2 * REACH, views * bx, by), BF16),
             pltpu.VMEM((bz + 2 * REACH, views * bx, by), BF16),
@@ -538,7 +616,7 @@
         flops=views * bz * ext * by * 600,
         nbytes=views * bz * bx * by * 8,
         name="returned",
-    )(profiles, view_boxes, quot, first, second, yr, xr)
+    )(profiles, view_boxes, quot, yr, xr)
     sums = [exchange(cells, link, *counts) for link, cells in zip(links, sums)]
     return call(
         functools.partial(finish_body, counts, links),

time: 47.4 us -> 43.8 us (0.924)
  starting transfers between devices: 17.7 us -> 14.7 us
  waiting for transfers between devices: 10.3 us -> 7.72 us
  Pallas kernels: 16.8 us -> 18.9 us
    ppermute x4 -> x2, waiting for transfers between devices: 2.84 us -> 0.01 us  [exchange_y(): lax.ppermute(cells, 'by', [(i, partner(i, count, swap)) for i in range(co...]
    ppermute x4 -> x2, starting transfers between devices: 6.52 us -> 4.51 us  [exchange_y(): lax.ppermute(cells, 'by', [(i, partner(i, count, swap)) for i in range(co...]
    pallas_call x1, Pallas kernels: 5.24 us -> 6.69 us  [local(): call(functools.partial(forward_body, views, block, counts, len(along_x)),...]
    ppermute x5, starting transfers between devices: 8.45 us -> 7.48 us  [exchange(): return lax.ppermute(cells, ('bx', 'bz'), pairs)]
    pallas_call x5, Pallas kernels: 10.3 us -> 10.9 us  [the longest x1 6.14 us: local(): call(functools.partial(return_body, views, block, links), [shape(block, F...]
  transfers between devices with their start and end apart: 12 -> 10, of which waited for: 5 -> 3; matrix products, arithmetic and copies ran while one was open for 0% -> 0% of each run, Pallas kernels for 18% -> 26%
where the time goes in v4:
time: 43.8 us; the launch traced here: 43.5 us
  Pallas kernels  18.9 us (43%)
  starting transfers between devices  14.7 us (34%)
  waiting for transfers between devices  7.72 us (18%)
  local copies, waits for them, and re-layouts  2.09 us (5%)
    ppermute x5, starting transfers between devices, exchange(): return lax.ppermute(cells, ('bx', 'bz'), pairs)  7.48 us
    pallas_call x1, Pallas kernels, local(): call(functools.partial(forward_body, views, block, counts, len(along_x)),...  6.69 us
    pallas_call x1, Pallas kernels, local(): call(functools.partial(return_body, views, block, links), [shape(block, F...  6.14 us
    ppermute x2, starting transfers between devices, exchange_y(): lax.ppermute(cells, 'by', [(i, partner(i, count, swap)) for i in range(co...  4.51 us
    ppermute x3, waiting for transfers between devices, local(): lax.ppermute(parts[other], 'by', [(i, i ^ other) for i in range(count)])  3.98 us
    ppermute x5, waiting for transfers between devices, exchange(): return lax.ppermute(cells, ('bx', 'bz'), pairs)  3.73 us
    pallas_call x1, Pallas kernels, local(): call(functools.partial(bands_body, views), [shape((views, by + 2 * SIDE,...  3.43 us
    ppermute x3, starting transfers between devices, local(): lax.ppermute(parts[other], 'by', [(i, i ^ other) for i in range(count)])  2.71 us
  transfers between devices with their start and end apart: 10, of which 3 were waited for; matrix products, arithmetic and copies ran while one was open for 0% of the time, Pallas kernels for 26%

profile of v4, /device:TPU:13, one launch (start us, length us, event | category | flops | bytes accessed | tf_op | source)
XLA Modules:
  0.0 43.5 jit_solution(9895524043280476438)
XLA Ops:
  0.0 0.0 copy-start
  0.0 1.1 %copy-done = bf16[6,16,8,512]{3,2,1,0:T(8,128)(2,1)S(1)} copy-done((bf16[6,16,8,512]{3,2,1,0:T(8,128)(2,1)S(1)}, bf16[6,16,8,512]{3,2,1,0:T(8,128)(2,1)}, u32[]{:S(2)}) %copy-start) | copy-done | bytes 786456
  1.1 0.0 copy-start.1
  1.1 0.9 %copy-done.1 = f32[16,32,128]{2,1,0:T(8,128)S(1)} copy-done((f32[16,32,128]{2,1,0:T(8,128)S(1)}, f32[16,32,128]{2,1,0:T(8,128)}, u32[]{:S(2)}) %copy-start.1) | copy-done | bytes 262168
  2.1 0.0 copy-start.2
  2.1 0.0 copy-start.3
  2.1 0.0 copy-start.4
  2.1 0.2 columns.1
  2.3 0.2 collective-permute-start
  2.5 4.3 %collective-permute-start.1 = (bf16[16,512]{1,0:T(8,128)(2,1)S(1)}, bf16[16,512]{1,0:T(8,128)(2,1)S(1)}, u32[]{:S(2)}, u32[]{:S(2)}) collective-permute-start(bf16[16,512]{1,0:T(8,128)(2,1)S(1)} %get-tuple-element.30), channel_id=1, source_target_pairs={{0,0},{4,8},{8,4},{12,12},{1,1},{5,9},{9,5},{13,13},{2,2},{6,10},{... | collective-permute-start | bytes 49160 | tf_op jit(solution)/shard_map/ppermute | solution.py:79
  6.8 0.7 %pieces.1 = (bf16[7,16,8,128]{3,2,1,0:T(8,128)(2,1)S(1)}, bf16[7,16,8,128]{3,2,1,0:T(8,128)(2,1)S(1)}, bf16[7,16,8,128]{3,2,1,0:T(8,128)(2,1)S(1)}, bf16[7,16,8,128]{3,2,1,0:T(8,128)(2,1)S(1)}) custom-call(bf16[16,512]{1,0:T(8,128)(2,1)S(1)} %get-tuple-element.27.order_ref, bf16[6,16,8,512]{3,2,1,0:T(8,128)(2,1)S(1)} %copy-done), custom_call_target="tpu_custom_call" | custom-call | bytes 1258291 | tf_op jit(solution)/shard_map/pieces/pallas_call | solution.py:525
  7.5 0.1 collective-permute-start.4
  7.6 1.2 %collective-permute-start.5 = (bf16[7,16,8,128]{3,2,1,0:T(8,128)(2,1)S(1)}, bf16[7,16,8,128]{3,2,1,0:T(8,128)(2,1)S(1)}, u32[]{:S(2)}, u32[]{:S(2)}) collective-permute-start(bf16[7,16,8,128]{3,2,1,0:T(8,128)(2,1)S(1)} %get-tuple-element.41), channel_id=1, source_target_pairs={{0,8},{4,12},{8,0},{12,4},{1,9},{5,13},{9,1},{13,5},{2,10},{6,14},... | collective-permute-start | bytes 688136 | tf_op jit(solution)/shard_map/ppermute | solution.py:533
  8.7 1.5 %collective-permute-start.6 = (bf16[7,16,8,128]{3,2,1,0:T(8,128)(2,1)S(1)}, bf16[7,16,8,128]{3,2,1,0:T(8,128)(2,1)S(1)}, u32[]{:S(2)}, u32[]{:S(2)}) collective-permute-start(bf16[7,16,8,128]{3,2,1,0:T(8,128)(2,1)S(1)} %get-tuple-element.42), channel_id=1, source_target_pairs={{0,12},{4,8},{8,4},{12,0},{1,13},{5,9},{9,5},{13,1},{2,14},{6,10},... | collective-permute-start | bytes 688136 | tf_op jit(solution)/shard_map/ppermute | solution.py:533
  10.2 0.0 collective-permute-done.first_ref
  10.2 0.0 collective-permute-done.1.second_ref
  10.2 0.3 edges.1
  10.5 2.1 %collective-permute-start.2 = (bf16[10,32,128]{2,1,0:T(8,128)(2,1)S(1)}, bf16[10,32,128]{2,1,0:T(8,128)(2,1)S(1)}, u32[]{:S(2)}, u32[]{:S(2)}) collective-permute-start(bf16[10,32,128]{2,1,0:T(8,128)(2,1)S(1)} %get-tuple-element.32), channel_id=1, source_target_pairs={{0,1},{1,0},{2,3},{3,2},{4,5},{5,4},{6,7},{7,6},{8,9},{9,8},{10,11... | collective-permute-start | bytes 245768 | tf_op jit(solution)/shard_map/ppermute | solution.py:73
  12.5 0.9 %collective-permute-done.2.refs_0_ = bf16[10,32,128]{2,1,0:T(8,128)(2,1)S(1)} collective-permute-done((bf16[10,32,128]{2,1,0:T(8,128)(2,1)S(1)}, bf16[10,32,128]{2,1,0:T(8,128)(2,1)S(1)}, u32[]{:S(2)}, u32[]{:S(2)}) %collective-permute-start.2) | collective-permute-done | bytes 81952 | tf_op jit(solution)/shard_map/ppermute | solution.py:73
  13.4 0.3 deep.1
  13.8 1.2 %collective-permute-start.3 = (bf16[40,8,128]{2,1,0:T(8,128)(2,1)S(1)}, bf16[40,8,128]{2,1,0:T(8,128)(2,1)S(1)}, u32[]{:S(2)}, u32[]{:S(2)}) collective-permute-start(bf16[40,8,128]{2,1,0:T(8,128)(2,1)S(1)} %get-tuple-element.38), channel_id=1, source_target_pairs={{0,2},{1,3},{2,0},{3,1},{4,6},{5,7},{6,4},{7,5},{8,10},{9,11},{10,... | collective-permute-start | bytes 245768 | tf_op jit(solution)/shard_map/ppermute | solution.py:73
  15.0 0.0 copy-done.2
  15.0 0.0 copy-done.3
  15.0 0.0 copy-done.4
  15.0 3.4 %bands.1 = (bf16[6,160,256]{2,1,0:T(8,128)(2,1)S(1)}, bf16[6,160,256]{2,1,0:T(8,128)(2,1)S(1)}, bf16[6,256,256]{2,1,0:T(8,128)(2,1)S(1)}, bf16[192,96]{1,0:T(8,1...) custom-call(bf16[16,512]{1,0:T(8,128)(2,1)S(1)} %get-tuple-element.27.order_ref, ...), custom_call_target="tpu_custom_call" | custom-call | flops 5033164 | bytes 629145 | tf_op jit(solution)/shard_map/bands/pallas_call | solution.py:566
  18.5 0.0 collective-permute-done.3.refs_0_
  18.5 6.7 %forward.1.gain_ref = f32[7,16,32,128]{3,2,1,0:T(8,128)S(1)} custom-call(f32[6,3,15]{2,1,0:T(4,128)S(1)} %copy-done.3, s32[6,6]{1,0:T(8,128)S(1)} %copy-done.4, f32[32,32,128]{2,1,0:T(8,128)S(1)} %get-tuple-element.33.cells_ref, f32[32,32,32]{2,1,0:T(8,128)S(1)} %get-tuple-element.34.halos_ref, bf16[6,160,256]{2,1,0:T(8,128)(2,1)S(1)} %get-tuple-element.35.yf_ref, ...), custom_call_target="tpu_custom_call" | custom-call | flops 566231040 | bytes 2516582 | tf_op jit(solution)/shard_map/forward/pallas_call | solution.py:582
  25.2 0.0 collective-permute-done.4.refs_1_
  25.2 0.0 collective-permute-done.5.refs_2_
  25.2 4.0 %collective-permute-done.6.refs_3_ = bf16[7,16,8,128]{3,2,1,0:T(8,128)(2,1)S(1)} collective-permute-done((bf16[7,16,8,128]{3,2,1,0:T(8,128)(2,1)S(1)}, bf16[7,16,8,128]{3,2,1,0:T(8,128)(2,1)S(1)}, u32[]{:S(2)}, u32[]{:S(2)}) %collective-permute-start.6) | collective-permute-done | bytes 229408 | tf_op jit(solution)/shard_map/ppermute | solution.py:533
  29.2 0.4 quotient.1.quot_ref
  29.6 6.1 %returned.1 = (f32[16,32,128]{2,1,0:T(8,128)S(1)}, f32[7,32,128]{2,1,0:T(8,128)S(1)}, f32[16,8,128]{2,1,0:T(8,128)S(1)}, f32[7,8,128]{2,1,0:T(8,128)S(1)}) custom-call(f32[6,3,15]{2,1,0:T(4,128)S(1)} %copy-done.3, s32[6,6]{1,0:T(8,128)S(1)} %copy-done.4, bf16[7,16,32,128]{3,2,1,0:T(8,128)(2,1)S(1)} %quotient.1.quot_ref, ...), custom_call_target="tpu_custom_call" | custom-call | flops 283115520 | bytes 2516582 | tf_op jit(solution)/shard_map/returned/pallas_call | solution.py:606
  35.7 2.5 %collective-permute-start.7 = (f32[7,32,128]{2,1,0:T(8,128)S(1)}, f32[7,32,128]{2,1,0:T(8,128)S(1)}, u32[]{:S(2)}, u32[]{:S(2)}) collective-permute-start(f32[7,32,128]{2,1,0:T(8,128)S(1)} %get-tuple-element.46), channel_id=1, source_target_pairs={{0,1},{1,0},{2,3},{3,2},{4,5},{5,4},{6,7},{7,6},{8,9},{9,8},{10,11... | collective-permute-start | bytes 344072 | tf_op jit(solution)/shard_map/ppermute | solution.py:73
  38.2 1.2 %collective-permute-start.8 = (f32[16,8,128]{2,1,0:T(8,128)S(1)}, f32[16,8,128]{2,1,0:T(8,128)S(1)}, u32[]{:S(2)}, u32[]{:S(2)}) collective-permute-start(f32[16,8,128]{2,1,0:T(8,128)S(1)} %get-tuple-element.47), channel_id=1, source_target_pairs={{0,2},{1,3},{2,0},{3,1},{4,6},{5,7},{6,4},{7,5},{8,10},{9,11},{10,... | collective-permute-start | bytes 196616 | tf_op jit(solution)/shard_map/ppermute | solution.py:73
  39.4 0.5 %collective-permute-start.9 = (f32[7,8,128]{2,1,0:T(8,128)S(1)}, f32[7,8,128]{2,1,0:T(8,128)S(1)}, u32[]{:S(2)}, u32[]{:S(2)}) collective-permute-start(f32[7,8,128]{2,1,0:T(8,128)S(1)} %get-tuple-element.48), channel_id=1, source_target_pairs={{0,3},{1,2},{2,1},{3,0},{4,7},{5,6},{6,5},{7,4},{8,11},{9,10},{10,... | collective-permute-start | bytes 86024 | tf_op jit(solution)/shard_map/ppermute | solution.py:73
  39.9 2.8 %collective-permute-done.9.refs_2_ = f32[7,8,128]{2,1,0:T(8,128)S(1)} collective-permute-done((f32[7,8,128]{2,1,0:T(8,128)S(1)}, f32[7,8,128]{2,1,0:T(8,128)S(1)}, u32[]{:S(2)}, u32[]{:S(2)}) %collective-permute-start.9) | collective-permute-done | bytes 28704 | tf_op jit(solution)/shard_map/ppermute | solution.py:73
  42.7 0.0 collective-permute-done.8.refs_1_
  42.7 0.0 collective-permute-done.7.refs_0_
  42.7 0.8 %finish.1 = f32[16,32,128]{2,1,0:T(8,128)} custom-call(f32[16,32,128]{2,1,0:T(8,128)S(1)} %get-tuple-element.28.share_ref, f32[16,32,128]{2,1,0:T(8,128)S(1)} %get-tuple-element.45.mid_ref, f32[7,32,128]{2,1,0:T(8,128)S(1)} %collective-permute-done.7.refs_0_, f32[16,8,128]{2,1,0:T(8,128)S(1)} %collective-permute-done.8.refs_1_, ...), custom_call_target="tpu_custom_call" | custom-call | bytes 629145 | tf_op jit(solution)/shard_map/finish/pallas_call | solution.py:621
Async XLA Ops:
  0.0 1.1 %copy-start = (bf16[6,16,8,512]{3,2,1,0:T(8,128)(2,1)S(1)}, bf16[6,16,8,512]{3,2,1,0:T(8,128)(2,1)}, u32[]{:S(2)}) copy-start(bf16[6,16,8,512]{3,2,1,0:T(8,128)(2,1)} %rec_ref.3) | copy-start | bytes 2359300
  1.1 0.9 %copy-start.1 = (f32[16,32,128]{2,1,0:T(8,128)S(1)}, f32[16,32,128]{2,1,0:T(8,128)}, u32[]{:S(2)}) copy-start(f32[16,32,128]{2,1,0:T(8,128)} %est_ref.3) | copy-start | bytes 786436
  2.1 12.9 %copy-start.2 = (f32[16,32,128]{2,1,0:T(8,128)S(1)}, f32[16,32,128]{2,1,0:T(8,128)}, u32[]{:S(2)}) copy-start(f32[16,32,128]{2,1,0:T(8,128)} %est_ref.3) | copy-start | bytes 786436
  2.1 12.9 %copy-start.3 = (f32[6,3,15]{2,1,0:T(4,128)S(1)}, f32[6,3,15]{2,1,0:T(4,128)}, u32[]{:S(2)}) copy-start(f32[6,3,15]{2,1,0:T(4,128)} %prof_ref.5) | copy-start | bytes 3244
  2.1 12.9 %copy-start.4 = (s32[6,6]{1,0:T(8,128)S(1)}, s32[6,6]{1,0:T(8,128)}, u32[]{:S(2)}) copy-start(s32[6,6]{1,0:T(8,128)} %box_ref.5) | copy-start | bytes 436
  2.3 7.9 %collective-permute-start = (bf16[16,512]{1,0:T(8,128)(2,1)S(1)}, bf16[16,512]{1,0:T(8,128)(2,1)S(1)}, u32[]{:S(2)}, u32[]{:S(2)}) collective-permute-start(bf16[16,512]{1,0:T(8,128)(2,1)S(1)} %get-tuple-element.27.order_ref), channel_id=1, source_target_pairs={{0,4},{4,0},{8,12},{12,8},{1,5},{5,1},{9,13},{13,9},{2,6},{6,2},{1... | collective-permute-start | bytes 49160 | tf_op jit(solution)/shard_map/ppermute | solution.py:79
  2.5 7.7 %collective-permute-start.1 = (bf16[16,512]{1,0:T(8,128)(2,1)S(1)}, bf16[16,512]{1,0:T(8,128)(2,1)S(1)}, u32[]{:S(2)}, u32[]{:S(2)}) collective-permute-start(bf16[16,512]{1,0:T(8,128)(2,1)S(1)} %get-tuple-element.30), channel_id=1, source_target_pairs={{0,0},{4,8},{8,4},{12,12},{1,1},{5,9},{9,5},{13,13},{2,2},{6,10},{... | collective-permute-start | bytes 49160 | tf_op jit(solution)/shard_map/ppermute | solution.py:79
  7.5 17.7 %collective-permute-start.4 = (bf16[7,16,8,128]{3,2,1,0:T(8,128)(2,1)S(1)}, bf16[7,16,8,128]{3,2,1,0:T(8,128)(2,1)S(1)}, u32[]{:S(2)}, u32[]{:S(2)}) collective-permute-start(bf16[7,16,8,128]{3,2,1,0:T(8,128)(2,1)S(1)} %get-tuple-element.40), channel_id=1, source_target_pairs={{0,4},{4,0},{8,12},{12,8},{1,5},{5,1},{9,13},{13,9},{2,6},{6,2},{1... | collective-permute-start | bytes 688136 | tf_op jit(solution)/shard_map/ppermute | solution.py:533
  7.6 17.6 %collective-permute-start.5 = (bf16[7,16,8,128]{3,2,1,0:T(8,128)(2,1)S(1)}, bf16[7,16,8,128]{3,2,1,0:T(8,128)(2,1)S(1)}, u32[]{:S(2)}, u32[]{:S(2)}) collective-permute-start(bf16[7,16,8,128]{3,2,1,0:T(8,128)(2,1)S(1)} %get-tuple-element.41), channel_id=1, source_target_pairs={{0,8},{4,12},{8,0},{12,4},{1,9},{5,13},{9,1},{13,5},{2,10},{6,14},... | collective-permute-start | bytes 688136 | tf_op jit(solution)/shard_map/ppermute | solution.py:533
  8.7 20.4 %collective-permute-start.6 = (bf16[7,16,8,128]{3,2,1,0:T(8,128)(2,1)S(1)}, bf16[7,16,8,128]{3,2,1,0:T(8,128)(2,1)S(1)}, u32[]{:S(2)}, u32[]{:S(2)}) collective-permute-start(bf16[7,16,8,128]{3,2,1,0:T(8,128)(2,1)S(1)} %get-tuple-element.42), channel_id=1, source_target_pairs={{0,12},{4,8},{8,4},{12,0},{1,13},{5,9},{9,5},{13,1},{2,14},{6,10},... | collective-permute-start | bytes 688136 | tf_op jit(solution)/shard_map/ppermute | solution.py:533
  10.5 3.0 %collective-permute-start.2 = (bf16[10,32,128]{2,1,0:T(8,128)(2,1)S(1)}, bf16[10,32,128]{2,1,0:T(8,128)(2,1)S(1)}, u32[]{:S(2)}, u32[]{:S(2)}) collective-permute-start(bf16[10,32,128]{2,1,0:T(8,128)(2,1)S(1)} %get-tuple-element.32), channel_id=1, source_target_pairs={{0,1},{1,0},{2,3},{3,2},{4,5},{5,4},{6,7},{7,6},{8,9},{9,8},{10,11... | collective-permute-start | bytes 245768 | tf_op jit(solution)/shard_map/ppermute | solution.py:73
  13.8 4.7 %collective-permute-start.3 = (bf16[40,8,128]{2,1,0:T(8,128)(2,1)S(1)}, bf16[40,8,128]{2,1,0:T(8,128)(2,1)S(1)}, u32[]{:S(2)}, u32[]{:S(2)}) collective-permute-start(bf16[40,8,128]{2,1,0:T(8,128)(2,1)S(1)} %get-tuple-element.38), channel_id=1, source_target_pairs={{0,2},{1,3},{2,0},{3,1},{4,6},{5,7},{6,4},{7,5},{8,10},{9,11},{10,... | collective-permute-start | bytes 245768 | tf_op jit(solution)/shard_map/ppermute | solution.py:73
  35.7 7.0 %collective-permute-start.7 = (f32[7,32,128]{2,1,0:T(8,128)S(1)}, f32[7,32,128]{2,1,0:T(8,128)S(1)}, u32[]{:S(2)}, u32[]{:S(2)}) collective-permute-start(f32[7,32,128]{2,1,0:T(8,128)S(1)} %get-tuple-element.46), channel_id=1, source_target_pairs={{0,1},{1,0},{2,3},{3,2},{4,5},{5,4},{6,7},{7,6},{8,9},{9,8},{10,11... | collective-permute-start | bytes 344072 | tf_op jit(solution)/shard_map/ppermute | solution.py:73
  38.2 4.5 %collective-permute-start.8 = (f32[16,8,128]{2,1,0:T(8,128)S(1)}, f32[16,8,128]{2,1,0:T(8,128)S(1)}, u32[]{:S(2)}, u32[]{:S(2)}) collective-permute-start(f32[16,8,128]{2,1,0:T(8,128)S(1)} %get-tuple-element.47), channel_id=1, source_target_pairs={{0,2},{1,3},{2,0},{3,1},{4,6},{5,7},{6,4},{7,5},{8,10},{9,11},{10,... | collective-permute-start | bytes 196616 | tf_op jit(solution)/shard_map/ppermute | solution.py:73
  39.4 3.3 %collective-permute-start.9 = (f32[7,8,128]{2,1,0:T(8,128)S(1)}, f32[7,8,128]{2,1,0:T(8,128)S(1)}, u32[]{:S(2)}, u32[]{:S(2)}) collective-permute-start(f32[7,8,128]{2,1,0:T(8,128)S(1)} %get-tuple-element.48), channel_id=1, source_target_pairs={{0,3},{1,2},{2,1},{3,0},{4,7},{5,6},{6,5},{7,4},{8,11},{9,10},{10,... | collective-permute-start | bytes 86024 | tf_op jit(solution)/shard_map/ppermute | solution.py:73

commit v5 on v4

--- a/solution.py
+++ b/solution.py
@@ -12,7 +12,8 @@
 PAD = 8
 SIDE = 2 * PAD
 BACKGROUND = 0.05
-WEIGHT = 0.8
+GROUP = 6
+WEIGHT = 0.5
 
 F32 = jnp.float32
 BF16 = jnp.bfloat16
@@ -114,7 +115,7 @@
     return jnp.concatenate([before, after], axis=0).T.astype(BF16)
 
 
-def columns_body(rec_ref, est_ref, cells_ref, first_ref, second_ref):
+def columns_body(est_ref, cells_ref, first_ref, second_ref):
     bz, bx, by = est_ref.shape
     cells_ref[...] = est_ref[...].astype(BF16)
     cells = cells_ref[...].reshape(bz * bx, by)
@@ -209,16 +210,13 @@
                 out_ref[deep + groups * i + j] = part.astype(BF16)
 
 
-def bands_body(views, order_ref, prof_ref, box_ref, est_ref, yf_ref, yh_ref, yr_ref, xf_ref, xr_ref, share_ref):
-    bz, bx, by = est_ref.shape
+def iota(shape, dim):
+    return lax.broadcasted_iota(jnp.int32, shape, dim)
+
+
+def forward_bands_body(views, block, order_ref, prof_ref, yf_ref, yh_ref, xf_ref):
+    bz, bx, by = block
     ext = bx + 2 * PAD
-    start_z = lax.axis_index("bz") * bz
-    start_x = lax.axis_index("bx") * bx
-    start_y = lax.axis_index("by") * by
-
-    def iota(shape, dim):
-        return lax.broadcasted_iota(jnp.int32, shape, dim)
-
     shape_y = (by + 2 * SIDE, by)
     row = iota(shape_y, 0)
     source = jnp.where(row < by, row, jnp.where(row < by + SIDE, row - by - SIDE, row - SIDE))
@@ -226,9 +224,6 @@
     beside_view = lax.div(target, 2 * PAD)
     beside = lax.rem(target, 2 * PAD)
     beside = jnp.where(beside < PAD, beside - PAD, by + beside - PAD)
-    back_row, back_target = iota((by, by), 0), iota((by, by), 1)
-    side_row, side_target = iota((2 * PAD, by), 0), iota((2 * PAD, by), 1)
-    side_row = jnp.where(side_row < PAD, side_row - PAD, by + side_row - PAD)
     shape_x = (bx, 2 * ext)
     col = iota(shape_x, 1)
     is_low = col >= ext
@@ -243,7 +238,25 @@
         high, low = halves(jnp.where(beside_view == k, forward, 0.0))
         yh_ref[k, :, :by] = high
         yh_ref[k, :, by:] = low
-
+        high, low = halves(banded(forward_x + REACH, lambda tap: prof_ref[k, 1, tap]))
+        at = pl.ds(pl.multiple_of(k * bx, bx), bx)
+        xf_ref[at, :] = jnp.where(is_low, low.astype(F32), high.astype(F32)).astype(BF16)
+        return carry
+
+    lax.fori_loop(0, views, view, 0)
+
+
+def return_bands_body(views, order_ref, prof_ref, box_ref, est_ref, yr_ref, xr_ref, share_ref):
+    bz, bx, by = est_ref.shape
+    ext = bx + 2 * PAD
+    start_z = lax.axis_index("bz") * bz
+    start_x = lax.axis_index("bx") * bx
+    start_y = lax.axis_index("by") * by
+    back_row, back_target = iota((by, by), 0), iota((by, by), 1)
+    side_row, side_target = iota((2 * PAD, by), 0), iota((2 * PAD, by), 1)
+    side_row = jnp.where(side_row < PAD, side_row - PAD, by + side_row - PAD)
+
+    def view(k, carry):
         def back(row, target):
             within = (target >= box_ref[k, 4] - start_y) & (target < box_ref[k, 5] - start_y)
             matrix = banded(REACH - row + target, lambda tap: prof_ref[k, 2, tap])
@@ -257,9 +270,6 @@
         high, low = back(side_row, side_target)
         yr_ref[k, at, :by] = high
         yr_ref[k, at, by:] = low
-        high, low = halves(banded(forward_x + REACH, lambda tap: prof_ref[k, 1, tap]))
-        at = pl.ds(pl.multiple_of(k * bx, bx), bx)
-        xf_ref[at, :] = jnp.where(is_low, low.astype(F32), high.astype(F32)).astype(BF16)
         return carry
 
     lax.fori_loop(0, views, view, 0)
@@ -345,19 +355,25 @@
         for tile in range(0, bx, 8):
             at = row_x + tile
             inside.append(jnp.where(within_y & (at >= box_ref[k, 2]) & (at < box_ref[k, 3]), 1.0, 0.0))
-        gain_ref[k] = jnp.zeros((bz, bx, by), F32)
-
-        def plane_of(plane, carry):
-            for tile in range(0, bx, 8):
-                total = taps[0] * rows[plane + 1, tile : tile + 8, :]
-                for tap in range(1, TAPS):
-                    total = total + taps[tap] * rows[plane + 1 + tap, tile : tile + 8, :]
-                gain_ref[k, plane, tile : tile + 8, :] = inside[tile // 8] / (total + BACKGROUND)
-            return carry
-
-        begin = jnp.clip(box_ref[k, 0] - start_z, 0, bz)
-        end = jnp.clip(box_ref[k, 1] - start_z, 0, bz)
-        lax.fori_loop(begin, end, plane_of, 0)
+        low_z = box_ref[k, 0] - start_z
+        high_z = box_ref[k, 1] - start_z
+        for first in range(0, bz, 4):
+            some = (first + 4 > low_z) & (first < high_z)
+
+            @pl.when(some)
+            def _():
+                for tile in range(0, bx, 8):
+                    for plane in range(first, first + 4):
+                        total = taps[0] * rows[plane + 1, tile : tile + 8, :]
+                        for tap in range(1, TAPS):
+                            total = total + taps[tap] * rows[plane + 1 + tap, tile : tile + 8, :]
+                        here = jnp.where((plane >= low_z) & (plane < high_z), 1.0, 0.0)
+                        gain_ref[k, plane, tile : tile + 8, :] = here * inside[tile // 8] / (total + BACKGROUND)
+
+            @pl.when(jnp.logical_not(some))
+            def _():
+                gain_ref[k, first : first + 4] = jnp.zeros((4, bx, by), F32)
+
         return carry
 
     lax.fori_loop(0, views, view, 0)
@@ -406,7 +422,7 @@
     mine = lax.axis_index("by") if count > 1 else 0
 
     def view(k, carry):
-        for part, part_ref in enumerate(parts):
+        for part, part_ref in zip(range(count - 1, -1, -1), parts):
             at = pl.ds(pl.multiple_of((mine ^ part) * rows, rows), rows)
             held[:, at, :] = gain_ref[k, :, at, :] * part_ref[k].astype(F32)
         quot_ref[k] = held[...].astype(BF16)
@@ -430,27 +446,33 @@
         rows[...] = (mixed[:, :by] + mixed[:, by:]).reshape(bz, bx, by)
         taps = [prof_ref[k, 0, tap] for tap in range(TAPS)]
         at = pl.ds(pl.multiple_of(k * bx, bx), bx)
-        for out in range(deep):
-            plane = out - REACH
-            here = (plane + start_z >= box_ref[k, 0]) & (plane + start_z < box_ref[k, 1])
-
-            @pl.when(here)
+        low_z = box_ref[k, 0] - start_z + REACH
+        high_z = box_ref[k, 1] - start_z + REACH
+        for first in range(0, deep, GROUP):
+            some = (first + GROUP > low_z) & (first < high_z)
+
+            @pl.when(some)
             def _():
-                sums = []
-                for tile in range(0, bx, 8):
-                    part = None
-                    for source in range(max(0, plane - REACH), min(bz, plane + REACH + 1)):
-                        term = taps[REACH - source + plane] * rows[source, tile : tile + 8, :]
-                        part = term if part is None else part + term
-                    sums.append(part)
-                high, low = halves(jnp.concatenate(sums, axis=0))
-                high_rows[out, at, :] = high
-                low_rows[out, at, :] = low
-
-            @pl.when(jnp.logical_not(here))
+                for tile in range(0, bx, 16):
+                    for out in range(first, first + GROUP):
+                        plane = out - REACH
+                        parts = []
+                        for half in (tile, tile + 8):
+                            part = None
+                            for source in range(max(0, plane - REACH), min(bz, plane + REACH + 1)):
+                                term = taps[REACH - source + plane] * rows[source, half : half + 8, :]
+                                part = term if part is None else part + term
+                            parts.append(part)
+                        here = jnp.where((out >= low_z) & (out < high_z), 1.0, 0.0)
+                        high, low = halves(here * jnp.concatenate(parts, axis=0))
+                        at_x = pl.ds(pl.multiple_of(k * bx + tile, 16), 16)
+                        high_rows[out, at_x, :] = high
+                        low_rows[out, at_x, :] = low
+
+            @pl.when(jnp.logical_not(some))
             def _():
-                high_rows[out, at, :] = jnp.zeros((bx, by), BF16)
-                low_rows[out, at, :] = jnp.zeros((bx, by), BF16)
+                high_rows[first : first + GROUP, at, :] = jnp.zeros((GROUP, bx, by), BF16)
+                low_rows[first : first + GROUP, at, :] = jnp.zeros((GROUP, bx, by), BF16)
 
         return carry
 
@@ -515,10 +537,10 @@
     own, order, second = call(
         columns_body,
         [shape(block, BF16), side, side],
-        [ANY, VMEM],
+        [VMEM],
         nbytes=bz * bx * by * 4,
         name="columns",
-    )(recorded, estimate)
+    )(estimate)
     first, second = exchange_y(order, second)
 
     if count & (count - 1) == 0 and count <= 4 and part_rows % 8 == 0:
@@ -529,6 +551,7 @@
             nbytes=views * bz * bx * by * 4,
             name="pieces",
         )(order, recorded)]
+        parts, first, second = lax.optimization_barrier((parts, first, second))
         for other in range(1, count):
             parts[other] = lax.ppermute(parts[other], "by", [(i, i ^ other) for i in range(count)])
     else:
@@ -563,21 +586,18 @@
     )(own, own, halo, *edges)
     edges = [exchange(cells, (swap, None), *counts) for swap, cells in zip(along_x, edges)]
 
-    yf, yh, yr, xf, xr, share = call(
-        functools.partial(bands_body, views),
+    yf, yh, xf = call(
+        functools.partial(forward_bands_body, views, block),
         [
             shape((views, by + 2 * SIDE, 2 * by), BF16),
             shape((views, by + 2 * SIDE, 2 * by), BF16),
-            shape((views, 2 * by, 2 * by), BF16),
             shape((views * bx, 2 * ext), BF16),
-            shape((2 * ext, views * bx), BF16),
-            shape(block, F32),
         ],
-        [ANY] + [SMEM] * 2 + [VMEM],
-        flops=views * 64 * by * by,
-        nbytes=views * by * by * 8,
-        name="bands",
-    )(order, profiles, view_boxes, estimate)
+        [ANY, SMEM],
+        flops=views * 32 * by * by,
+        nbytes=views * by * by * 4,
+        name="forward_bands",
+    )(order, profiles)
 
     gain = call(
         functools.partial(forward_body, views, block, counts, len(along_x)),
@@ -593,6 +613,18 @@
         name="forward",
     )(profiles, view_boxes, cells, halos, yf, yh, xf, *edges)
 
+    yr, xr, share = call(
+        functools.partial(return_bands_body, views),
+        [
+            shape((views, 2 * by, 2 * by), BF16),
+            shape((2 * ext, views * bx), BF16),
+            shape(block, F32),
+        ],
+        [ANY] + [SMEM] * 2 + [VMEM],
+        flops=views * 32 * by * by,
+        nbytes=views * by * by * 4,
+        name="return_bands",
+    )(gain, profiles, view_boxes, estimate)
     quot = call(
         functools.partial(quotient_body, views, block, len(parts)),
         shape((views + 1, bz, bx, by), BF16),
@@ -601,7 +633,7 @@
         flops=views * bz * bx * by * 40,
         nbytes=views * bz * bx * by * 8,
         name="quotient",
-    )(gain, *parts)
+    )(gain, *parts[::-1])
 
     mid, *sums = call(
         functools.partial(return_body, views, block, links),

time: 43.8 us -> 42.8 us (0.977)
  the two profiles are of different devices: /device:TPU:13 before, /device:TPU:0 now
where the time goes in v5:
time: 42.8 us; the launch traced here: 42.4 us
  Pallas kernels  17.8 us (42%)
  starting transfers between devices  14.5 us (34%)
  waiting for transfers between devices  6.47 us (15%)
  local copies, waits for them, and re-layouts  3.48 us (8%)
    ppermute x2, starting transfers between devices, exchange_y(): lax.ppermute(cells, 'by', [(i, partner(i, count, swap)) for i in range(co...  6.58 us
    pallas_call x1, Pallas kernels, local(): call(functools.partial(forward_body, views, block, counts, len(along_x)),...  6.52 us
    pallas_call x1, Pallas kernels, local(): call(functools.partial(return_body, views, block, links), [shape(block, F...  4.58 us
    ppermute x3, starting transfers between devices, local(): lax.ppermute(parts[other], 'by', [(i, i ^ other) for i in range(count)])  4.45 us
    ppermute x5, waiting for transfers between devices, exchange(): return lax.ppermute(cells, ('bx', 'bz'), pairs)  4.44 us
    unnamed x10, local copies, waits for them, and re-layouts  3.48 us
    ppermute x5, starting transfers between devices, exchange(): return lax.ppermute(cells, ('bx', 'bz'), pairs)  3.45 us
    pallas_call x1, Pallas kernels, local(): call(functools.partial(forward_bands_body, views, block), [shape((views,...  2.12 us
  transfers between devices with their start and end apart: 10, of which 4 were waited for; matrix products, arithmetic and copies ran while one was open for 0% of the time, Pallas kernels for 28%

profile of v5, /device:TPU:0, one launch (start us, length us, event | category | flops | bytes accessed | tf_op | source)
XLA Modules:
  0.0 42.4 jit_solution(2821317378744993875)
XLA Ops:
  0.0 0.0 copy-start
  0.0 0.9 %copy-done = f32[16,32,128]{2,1,0:T(8,128)S(1)} copy-done((f32[16,32,128]{2,1,0:T(8,128)S(1)}, f32[16,32,128]{2,1,0:T(8,128)}, u32[]{:S(2)}) %copy-start) | copy-done | bytes 262168
  1.0 0.2 columns.1
  1.1 0.7 %collective-permute-start.1 = (bf16[16,512]{1,0:T(8,128)(2,1)S(1)}, bf16[16,512]{1,0:T(8,128)(2,1)S(1)}, u32[]{:S(2)}, u32[]{:S(2)}) collective-permute-start(bf16[16,512]{1,0:T(8,128)(2,1)S(1)} %get-tuple-element.39), channel_id=1, source_target_pairs={{0,0},{4,8},{8,4},{12,12},{1,1},{5,9},{9,5},{13,13},{2,2},{6,10},{... | collective-permute-start | bytes 49160 | tf_op jit(solution)/shard_map/ppermute | solution.py:80
  1.8 5.9 %collective-permute-start = (bf16[16,512]{1,0:T(8,128)(2,1)S(1)}, bf16[16,512]{1,0:T(8,128)(2,1)S(1)}, u32[]{:S(2)}, u32[]{:S(2)}) collective-permute-start(bf16[16,512]{1,0:T(8,128)(2,1)S(1)} %get-tuple-element.34.order_ref), channel_id=1, source_target_pairs={{0,4},{4,0},{8,12},{12,8},{1,5},{5,1},{9,13},{13,9},{2,6},{6,2},{1... | collective-permute-start | bytes 49160 | tf_op jit(solution)/shard_map/ppermute | solution.py:80
  7.7 0.0 copy-start.2
  7.7 1.1 %copy-done.2 = bf16[6,16,8,512]{3,2,1,0:T(8,128)(2,1)S(1)} copy-done((bf16[6,16,8,512]{3,2,1,0:T(8,128)(2,1)S(1)}, bf16[6,16,8,512]{3,2,1,0:T(8,128)(2,1)}, u32[]{:S(2)}) %copy-start.2) | copy-done | bytes 786456
  8.9 0.7 %pieces.1 = (bf16[7,16,8,128]{3,2,1,0:T(8,128)(2,1)S(1)}, bf16[7,16,8,128]{3,2,1,0:T(8,128)(2,1)S(1)}, bf16[7,16,8,128]{3,2,1,0:T(8,128)(2,1)S(1)}, bf16[7,16,8,128]{3,2,1,0:T(8,128)(2,1)S(1)}) custom-call(bf16[16,512]{1,0:T(8,128)(2,1)S(1)} %get-tuple-element.34.order_ref, bf16[6,16,8,512]{3,2,1,0:T(8,128)(2,1)S(1)} %copy-done.2), custom_call_target="tpu_custom_call" | custom-call | bytes 786432 | tf_op jit(solution)/shard_map/pieces/pallas_call | solution.py:547
  9.5 0.0 collective-permute-done.1.second_ref
  9.5 0.0 collective-permute-done.first_ref
  9.5 1.4 %collective-permute-start.4 = (bf16[7,16,8,128]{3,2,1,0:T(8,128)(2,1)S(1)}, bf16[7,16,8,128]{3,2,1,0:T(8,128)(2,1)S(1)}, u32[]{:S(2)}, u32[]{:S(2)}) collective-permute-start(bf16[7,16,8,128]{3,2,1,0:T(8,128)(2,1)S(1)} %get-tuple-element.51), channel_id=1, source_target_pairs={{0,12},{4,8},{8,4},{12,0},{1,13},{5,9},{9,5},{13,1},{2,14},{6,10},... | collective-permute-start | bytes 688136 | tf_op jit(solution)/shard_map/ppermute | solution.py:556
  11.0 2.0 %collective-permute-start.5 = (bf16[7,16,8,128]{3,2,1,0:T(8,128)(2,1)S(1)}, bf16[7,16,8,128]{3,2,1,0:T(8,128)(2,1)S(1)}, u32[]{:S(2)}, u32[]{:S(2)}) collective-permute-start(bf16[7,16,8,128]{3,2,1,0:T(8,128)(2,1)S(1)} %get-tuple-element.52), channel_id=1, source_target_pairs={{0,8},{4,12},{8,0},{12,4},{1,9},{5,13},{9,1},{13,5},{2,10},{6,14},... | collective-permute-start | bytes 688136 | tf_op jit(solution)/shard_map/ppermute | solution.py:556
  12.9 1.1 %collective-permute-start.6 = (bf16[7,16,8,128]{3,2,1,0:T(8,128)(2,1)S(1)}, bf16[7,16,8,128]{3,2,1,0:T(8,128)(2,1)S(1)}, u32[]{:S(2)}, u32[]{:S(2)}) collective-permute-start(bf16[7,16,8,128]{3,2,1,0:T(8,128)(2,1)S(1)} %get-tuple-element.53), channel_id=1, source_target_pairs={{0,4},{4,0},{8,12},{12,8},{1,5},{5,1},{9,13},{13,9},{2,6},{6,2},{1... | collective-permute-start | bytes 688136 | tf_op jit(solution)/shard_map/ppermute | solution.py:556
  14.0 0.2 edges.1
  14.2 0.0 collective-permute-start.2
  14.2 1.3 %collective-permute-done.2.refs_0_ = bf16[10,32,128]{2,1,0:T(8,128)(2,1)S(1)} collective-permute-done((bf16[10,32,128]{2,1,0:T(8,128)(2,1)S(1)}, bf16[10,32,128]{2,1,0:T(8,128)(2,1)S(1)}, u32[]{:S(2)}, u32[]{:S(2)}) %collective-permute-start.2) | collective-permute-done | bytes 81952 | tf_op jit(solution)/shard_map/ppermute | solution.py:74
  15.5 0.3 deep.1
  15.9 1.5 %collective-permute-start.3 = (bf16[40,8,128]{2,1,0:T(8,128)(2,1)S(1)}, bf16[40,8,128]{2,1,0:T(8,128)(2,1)S(1)}, u32[]{:S(2)}, u32[]{:S(2)}) collective-permute-start(bf16[40,8,128]{2,1,0:T(8,128)(2,1)S(1)} %get-tuple-element.49), channel_id=1, source_target_pairs={{0,2},{1,3},{2,0},{3,1},{4,6},{5,7},{6,4},{7,5},{8,10},{9,11},{10,... | collective-permute-start | bytes 245768 | tf_op jit(solution)/shard_map/ppermute | solution.py:74
  17.4 0.0 copy-start.3
  17.4 0.7 %copy-done.3 = f32[6,3,15]{2,1,0:T(4,128)S(1)} copy-done((f32[6,3,15]{2,1,0:T(4,128)S(1)}, f32[6,3,15]{2,1,0:T(4,128)}, u32[]{:S(2)}) %copy-start.3) | copy-done | bytes 1104
  18.1 2.1 %forward_bands.1 = (bf16[6,160,256]{2,1,0:T(8,128)(2,1)S(1)}, bf16[6,160,256]{2,1,0:T(8,128)(2,1)S(1)}, bf16[192,96]{1,0:T(8,128)(2,1)S(1)}) custom-call(bf16[16,512]{1,0:T(8,128)(2,1)S(1)} %get-tuple-element.34.order_ref, f32[6,3,15]{2,1,0:T(4,128)S(1)} %copy-done.3), custom_call_target="tpu_custom_call" | custom-call | flops 1572864 | bytes 196608 | tf_op jit(solution)/shard_map/forward_bands/pallas_call | solution.py:589
  20.2 0.2 collective-permute-done.3.refs_0_
  20.4 0.0 copy-start.4
  20.4 0.7 %copy-done.4 = s32[6,6]{1,0:T(8,128)S(1)} copy-done((s32[6,6]{1,0:T(8,128)S(1)}, s32[6,6]{1,0:T(8,128)}, u32[]{:S(2)}) %copy-start.4) | copy-done | bytes 168
  21.1 0.0 copy-start.1
  21.1 6.5 %forward.1.order_ref.gain_ref = f32[7,16,32,128]{3,2,1,0:T(8,128)S(1)} custom-call(f32[6,3,15]{2,1,0:T(4,128)S(1)} %copy-done.3, s32[6,6]{1,0:T(8,128)S(1)} %copy-done.4, f32[32,32,128]{2,1,0:T(8,128)S(1)} %get-tuple-element.44.cells_ref, f32[32,32,32]{2,1,0:T(8,128)S(1)} %get-tuple-element.45.halos_ref, bf16[6,160,256]{2,1,0:T(8,128)(2,1)S(1)} %get-tuple-element.46.yf_ref, ...), custom_call_target="tpu_custom_call" | custom-call | flops 353894400 | bytes 1572864 | tf_op jit(solution)/shard_map/forward/pallas_call | solution.py:602
  27.6 0.0 copy-done.1
  27.6 2.0 %return_bands.1 = (bf16[6,256,256]{2,1,0:T(8,128)(2,1)S(1)}, bf16[96,192]{1,0:T(8,128)(2,1)S(1)}, f32[16,32,128]{2,1,0:T(8,128)S(1)}) custom-call(f32[7,16,32,128]{3,2,1,0:T(8,128)S(1)} %forward.1.order_ref.gain_ref, f32[6,3,15]{2,1,0:T(4,128)S(1)} %copy-done.3, s32[6,6]{1,0:T(8,128)S(1)} %copy-done.4, f32[16,32,128]{2,1,0:T(8,128)S(1)} %copy-done.1), custom_call_target="tpu_custom_call" | custom-call | flops 1572864 | bytes 196608 | tf_op jit(solution)/shard_map/return_bands/pallas_call | solution.py:616
  29.6 0.0 collective-permute-done.4.refs_0_
  29.6 2.0 %collective-permute-done.5.refs_1_ = bf16[7,16,8,128]{3,2,1,0:T(8,128)(2,1)S(1)} collective-permute-done((bf16[7,16,8,128]{3,2,1,0:T(8,128)(2,1)S(1)}, bf16[7,16,8,128]{3,2,1,0:T(8,128)(2,1)S(1)}, u32[]{:S(2)}, u32[]{:S(2)}) %collective-permute-start.5) | collective-permute-done | bytes 229408 | tf_op jit(solution)/shard_map/ppermute | solution.py:556
  31.6 0.0 collective-permute-done.6.refs_2_
  31.6 0.5 %quotient.1.quot_ref = bf16[7,16,32,128]{3,2,1,0:T(8,128)(2,1)S(1)} custom-call(f32[7,16,32,128]{3,2,1,0:T(8,128)S(1)} %forward.1.order_ref.gain_ref, bf16[7,16,8,128]{3,2,1,0:T(8,128)(2,1)S(1)} %collective-permute-done.4.refs_0_, bf16[7,16,8,128]{3,2,1,0:T(8,128)(2,1)S(1)} %collective-permute-done.5.refs_1_, ...), custom_call_target="tpu_custom_call" | custom-call | flops 7864320 | bytes 1572864 | tf_op jit(solution)/shard_map/quotient/pallas_call | solution.py:628
  32.1 4.6 %returned.1 = (f32[16,32,128]{2,1,0:T(8,128)S(1)}, f32[7,32,128]{2,1,0:T(8,128)S(1)}, f32[16,8,128]{2,1,0:T(8,128)S(1)}, f32[7,8,128]{2,1,0:T(8,128)S(1)}) custom-call(f32[6,3,15]{2,1,0:T(4,128)S(1)} %copy-done.3, s32[6,6]{1,0:T(8,128)S(1)} %copy-done.4, bf16[7,16,32,128]{3,2,1,0:T(8,128)(2,1)S(1)} %quotient.1.quot_ref, ...), custom_call_target="tpu_custom_call" | custom-call | flops 176947200 | bytes 1572864 | tf_op jit(solution)/shard_map/returned/pallas_call | solution.py:638
  36.7 0.1 collective-permute-start.7
  36.7 1.5 %collective-permute-start.8 = (f32[16,8,128]{2,1,0:T(8,128)S(1)}, f32[16,8,128]{2,1,0:T(8,128)S(1)}, u32[]{:S(2)}, u32[]{:S(2)}) collective-permute-start(f32[16,8,128]{2,1,0:T(8,128)S(1)} %get-tuple-element.59), channel_id=1, source_target_pairs={{0,2},{1,3},{2,0},{3,1},{4,6},{5,7},{6,4},{7,5},{8,10},{9,11},{10,... | collective-permute-start | bytes 196616 | tf_op jit(solution)/shard_map/ppermute | solution.py:74
  38.3 0.3 collective-permute-start.9
  38.6 3.0 %collective-permute-done.9.refs_2_ = f32[7,8,128]{2,1,0:T(8,128)S(1)} collective-permute-done((f32[7,8,128]{2,1,0:T(8,128)S(1)}, f32[7,8,128]{2,1,0:T(8,128)S(1)}, u32[]{:S(2)}, u32[]{:S(2)}) %collective-permute-start.9) | collective-permute-done | bytes 28704 | tf_op jit(solution)/shard_map/ppermute | solution.py:74
  41.6 0.0 collective-permute-done.8.refs_1_
  41.6 0.0 collective-permute-done.7.refs_0_
  41.6 0.8 %finish.1 = f32[16,32,128]{2,1,0:T(8,128)} custom-call(f32[16,32,128]{2,1,0:T(8,128)S(1)} %get-tuple-element.50.share_ref, f32[16,32,128]{2,1,0:T(8,128)S(1)} %get-tuple-element.57.mid_ref, f32[7,32,128]{2,1,0:T(8,128)S(1)} %collective-permute-done.7.refs_0_, f32[16,8,128]{2,1,0:T(8,128)S(1)} %collective-permute-done.8.refs_1_, ...), custom_call_target="tpu_custom_call" | custom-call | bytes 393216 | tf_op jit(solution)/shard_map/finish/pallas_call | solution.py:653
Async XLA Ops:
  0.0 0.9 %copy-start = (f32[16,32,128]{2,1,0:T(8,128)S(1)}, f32[16,32,128]{2,1,0:T(8,128)}, u32[]{:S(2)}) copy-start(f32[16,32,128]{2,1,0:T(8,128)} %est_ref.3) | copy-start | bytes 786436
  1.1 8.4 %collective-permute-start.1 = (bf16[16,512]{1,0:T(8,128)(2,1)S(1)}, bf16[16,512]{1,0:T(8,128)(2,1)S(1)}, u32[]{:S(2)}, u32[]{:S(2)}) collective-permute-start(bf16[16,512]{1,0:T(8,128)(2,1)S(1)} %get-tuple-element.39), channel_id=1, source_target_pairs={{0,0},{4,8},{8,4},{12,12},{1,1},{5,9},{9,5},{13,13},{2,2},{6,10},{... | collective-permute-start | bytes 49160 | tf_op jit(solution)/shard_map/ppermute | solution.py:80
  1.8 7.7 %collective-permute-start = (bf16[16,512]{1,0:T(8,128)(2,1)S(1)}, bf16[16,512]{1,0:T(8,128)(2,1)S(1)}, u32[]{:S(2)}, u32[]{:S(2)}) collective-permute-start(bf16[16,512]{1,0:T(8,128)(2,1)S(1)} %get-tuple-element.34.order_ref), channel_id=1, source_target_pairs={{0,4},{4,0},{8,12},{12,8},{1,5},{5,1},{9,13},{13,9},{2,6},{6,2},{1... | collective-permute-start | bytes 49160 | tf_op jit(solution)/shard_map/ppermute | solution.py:80
  7.7 1.1 %copy-start.2 = (bf16[6,16,8,512]{3,2,1,0:T(8,128)(2,1)S(1)}, bf16[6,16,8,512]{3,2,1,0:T(8,128)(2,1)}, u32[]{:S(2)}) copy-start(bf16[6,16,8,512]{3,2,1,0:T(8,128)(2,1)} %rec_ref.1) | copy-start | bytes 2359300
  9.5 20.0 %collective-permute-start.4 = (bf16[7,16,8,128]{3,2,1,0:T(8,128)(2,1)S(1)}, bf16[7,16,8,128]{3,2,1,0:T(8,128)(2,1)S(1)}, u32[]{:S(2)}, u32[]{:S(2)}) collective-permute-start(bf16[7,16,8,128]{3,2,1,0:T(8,128)(2,1)S(1)} %get-tuple-element.51), channel_id=1, source_target_pairs={{0,12},{4,8},{8,4},{12,0},{1,13},{5,9},{9,5},{13,1},{2,14},{6,10},... | collective-permute-start | bytes 688136 | tf_op jit(solution)/shard_map/ppermute | solution.py:556
  11.0 20.6 %collective-permute-start.5 = (bf16[7,16,8,128]{3,2,1,0:T(8,128)(2,1)S(1)}, bf16[7,16,8,128]{3,2,1,0:T(8,128)(2,1)S(1)}, u32[]{:S(2)}, u32[]{:S(2)}) collective-permute-start(bf16[7,16,8,128]{3,2,1,0:T(8,128)(2,1)S(1)} %get-tuple-element.52), channel_id=1, source_target_pairs={{0,8},{4,12},{8,0},{12,4},{1,9},{5,13},{9,1},{13,5},{2,10},{6,14},... | collective-permute-start | bytes 688136 | tf_op jit(solution)/shard_map/ppermute | solution.py:556
  12.9 18.7 %collective-permute-start.6 = (bf16[7,16,8,128]{3,2,1,0:T(8,128)(2,1)S(1)}, bf16[7,16,8,128]{3,2,1,0:T(8,128)(2,1)S(1)}, u32[]{:S(2)}, u32[]{:S(2)}) collective-permute-start(bf16[7,16,8,128]{3,2,1,0:T(8,128)(2,1)S(1)} %get-tuple-element.53), channel_id=1, source_target_pairs={{0,4},{4,0},{8,12},{12,8},{1,5},{5,1},{9,13},{13,9},{2,6},{6,2},{1... | collective-permute-start | bytes 688136 | tf_op jit(solution)/shard_map/ppermute | solution.py:556
  14.2 1.3 %collective-permute-start.2 = (bf16[10,32,128]{2,1,0:T(8,128)(2,1)S(1)}, bf16[10,32,128]{2,1,0:T(8,128)(2,1)S(1)}, u32[]{:S(2)}, u32[]{:S(2)}) collective-permute-start(bf16[10,32,128]{2,1,0:T(8,128)(2,1)S(1)} %get-tuple-element.43), channel_id=1, source_target_pairs={{0,1},{1,0},{2,3},{3,2},{4,5},{5,4},{6,7},{7,6},{8,9},{9,8},{10,11... | collective-permute-start | bytes 245768 | tf_op jit(solution)/shard_map/ppermute | solution.py:74
  15.9 4.5 %collective-permute-start.3 = (bf16[40,8,128]{2,1,0:T(8,128)(2,1)S(1)}, bf16[40,8,128]{2,1,0:T(8,128)(2,1)S(1)}, u32[]{:S(2)}, u32[]{:S(2)}) collective-permute-start(bf16[40,8,128]{2,1,0:T(8,128)(2,1)S(1)} %get-tuple-element.49), channel_id=1, source_target_pairs={{0,2},{1,3},{2,0},{3,1},{4,6},{5,7},{6,4},{7,5},{8,10},{9,11},{10,... | collective-permute-start | bytes 245768 | tf_op jit(solution)/shard_map/ppermute | solution.py:74
  17.4 0.7 %copy-start.3 = (f32[6,3,15]{2,1,0:T(4,128)S(1)}, f32[6,3,15]{2,1,0:T(4,128)}, u32[]{:S(2)}) copy-start(f32[6,3,15]{2,1,0:T(4,128)} %prof_ref.7) | copy-start | bytes 3244
  20.4 0.7 %copy-start.4 = (s32[6,6]{1,0:T(8,128)S(1)}, s32[6,6]{1,0:T(8,128)}, u32[]{:S(2)}) copy-start(s32[6,6]{1,0:T(8,128)} %box_ref.5) | copy-start | bytes 436
  21.1 6.5 %copy-start.1 = (f32[16,32,128]{2,1,0:T(8,128)S(1)}, f32[16,32,128]{2,1,0:T(8,128)}, u32[]{:S(2)}) copy-start(f32[16,32,128]{2,1,0:T(8,128)} %est_ref.3) | copy-start | bytes 786436
  36.7 4.9 %collective-permute-start.7 = (f32[7,32,128]{2,1,0:T(8,128)S(1)}, f32[7,32,128]{2,1,0:T(8,128)S(1)}, u32[]{:S(2)}, u32[]{:S(2)}) collective-permute-start(f32[7,32,128]{2,1,0:T(8,128)S(1)} %get-tuple-element.58), channel_id=1, source_target_pairs={{0,1},{1,0},{2,3},{3,2},{4,5},{5,4},{6,7},{7,6},{8,9},{9,8},{10,11... | collective-permute-start | bytes 344072 | tf_op jit(solution)/shard_map/ppermute | solution.py:74
  36.7 4.8 %collective-permute-start.8 = (f32[16,8,128]{2,1,0:T(8,128)S(1)}, f32[16,8,128]{2,1,0:T(8,128)S(1)}, u32[]{:S(2)}, u32[]{:S(2)}) collective-permute-start(f32[16,8,128]{2,1,0:T(8,128)S(1)} %get-tuple-element.59), channel_id=1, source_target_pairs={{0,2},{1,3},{2,0},{3,1},{4,6},{5,7},{6,4},{7,5},{8,10},{9,11},{10,... | collective-permute-start | bytes 196616 | tf_op jit(solution)/shard_map/ppermute | solution.py:74
  38.3 3.3 %collective-permute-start.9 = (f32[7,8,128]{2,1,0:T(8,128)S(1)}, f32[7,8,128]{2,1,0:T(8,128)S(1)}, u32[]{:S(2)}, u32[]{:S(2)}) collective-permute-start(f32[7,8,128]{2,1,0:T(8,128)S(1)} %get-tuple-element.60), channel_id=1, source_target_pairs={{0,3},{1,2},{2,1},{3,0},{4,7},{5,6},{6,5},{7,4},{8,11},{9,10},{10,... | collective-permute-start | bytes 86024 | tf_op jit(solution)/shard_map/ppermute | solution.py:74

commit v6 on v5

--- a/solution.py
+++ b/solution.py
@@ -13,7 +13,7 @@
 SIDE = 2 * PAD
 BACKGROUND = 0.05
 GROUP = 6
-WEIGHT = 0.5
+WEIGHT = 0.8
 
 F32 = jnp.float32
 BF16 = jnp.bfloat16
@@ -82,6 +82,10 @@
     ]
 
 
+def order_of(count):
+    return [1, 2, 3, 0] if count == 4 else range(count - 1, -1, -1)
+
+
 def banded(offset, tap_of):
     matrix = jnp.zeros(offset.shape, F32)
     for tap in range(TAPS):
@@ -230,15 +234,15 @@
     forward_x = jnp.where(is_low, col - ext, col) - PAD - iota(shape_x, 0)
 
     def view(k, carry):
-        forward = banded(source - target + REACH, lambda tap: prof_ref[k, 2, tap])
+        forward = banded(source - target + REACH, lambda tap: prof_ref[(k * 3 + 2) * TAPS + tap])
         high, low = halves(forward)
         yf_ref[k, :, :by] = high
         yf_ref[k, :, by:] = low
-        forward = banded(source - beside + REACH, lambda tap: prof_ref[k, 2, tap])
+        forward = banded(source - beside + REACH, lambda tap: prof_ref[(k * 3 + 2) * TAPS + tap])
         high, low = halves(jnp.where(beside_view == k, forward, 0.0))
         yh_ref[k, :, :by] = high
         yh_ref[k, :, by:] = low
-        high, low = halves(banded(forward_x + REACH, lambda tap: prof_ref[k, 1, tap]))
+        high, low = halves(banded(forward_x + REACH, lambda tap: prof_ref[(k * 3 + 1) * TAPS + tap]))
         at = pl.ds(pl.multiple_of(k * bx, bx), bx)
         xf_ref[at, :] = jnp.where(is_low, low.astype(F32), high.astype(F32)).astype(BF16)
         return carry
@@ -258,8 +262,8 @@
 
     def view(k, carry):
         def back(row, target):
-            within = (target >= box_ref[k, 4] - start_y) & (target < box_ref[k, 5] - start_y)
-            matrix = banded(REACH - row + target, lambda tap: prof_ref[k, 2, tap])
+            within = (target >= box_ref[k * 6 + 4] - start_y) & (target < box_ref[k * 6 + 5] - start_y)
+            matrix = banded(REACH - row + target, lambda tap: prof_ref[(k * 3 + 2) * TAPS + tap])
             return halves(jnp.where(within, matrix, 0.0))
 
         high, low = back(back_row, back_target)
@@ -280,9 +284,9 @@
 
     def back_view(k, matrix):
         source = col - k * bx
-        back = banded(REACH - source + target, lambda tap: prof_ref[k, 1, tap])
+        back = banded(REACH - source + target, lambda tap: prof_ref[(k * 3 + 1) * TAPS + tap])
         within = (source >= 0) & (source < bx)
-        within = within & (target >= box_ref[k, 2] - start_x) & (target < box_ref[k, 3] - start_x)
+        within = within & (target >= box_ref[k * 6 + 2] - start_x) & (target < box_ref[k * 6 + 3] - start_x)
         return jnp.where(within, back, matrix)
 
     high, low = halves(lax.fori_loop(0, views, back_view, jnp.zeros(shape_x, F32)))
@@ -293,14 +297,14 @@
     col_y = iota((bx, by), 1) + start_y
     flat = []
     for k in range(views):
-        within = (col_y >= box_ref[k, 4]) & (col_y < box_ref[k, 5])
-        within = within & (row_x >= box_ref[k, 2]) & (row_x < box_ref[k, 3])
+        within = (col_y >= box_ref[k * 6 + 4]) & (col_y < box_ref[k * 6 + 5])
+        within = within & (row_x >= box_ref[k * 6 + 2]) & (row_x < box_ref[k * 6 + 3])
         flat.append(jnp.where(within, 1.0, 0.0))
     for plane in range(bz):
         coverage = jnp.zeros((bx, by), F32)
         for k in range(views):
             at = plane + start_z
-            here = (at >= box_ref[k, 0]) & (at < box_ref[k, 1])
+            here = (at >= box_ref[k * 6 + 0]) & (at < box_ref[k * 6 + 1])
             coverage = coverage + jnp.where(here, 1.0, 0.0) * flat[k]
         share_ref[plane] = est_ref[plane] / coverage
 
@@ -349,14 +353,14 @@
                 blurred_x[k, first * bx : (first + step) * bx, :], along_y, preferred_element_type=F32
             )
             rows[first : first + step] = (mixed[:, :by] + mixed[:, by:]).reshape(step, bx, by)
-        taps = [prof_ref[k, 0, tap] for tap in range(TAPS)]
-        within_y = (col_y >= box_ref[k, 4]) & (col_y < box_ref[k, 5])
+        taps = [prof_ref[(k * 3 + 0) * TAPS + tap] for tap in range(TAPS)]
+        within_y = (col_y >= box_ref[k * 6 + 4]) & (col_y < box_ref[k * 6 + 5])
         inside = []
         for tile in range(0, bx, 8):
             at = row_x + tile
-            inside.append(jnp.where(within_y & (at >= box_ref[k, 2]) & (at < box_ref[k, 3]), 1.0, 0.0))
-        low_z = box_ref[k, 0] - start_z
-        high_z = box_ref[k, 1] - start_z
+            inside.append(jnp.where(within_y & (at >= box_ref[k * 6 + 2]) & (at < box_ref[k * 6 + 3]), 1.0, 0.0))
+        low_z = box_ref[k * 6 + 0] - start_z
+        high_z = box_ref[k * 6 + 1] - start_z
         for first in range(0, bz, 4):
             some = (first + 4 > low_z) & (first < high_z)
 
@@ -388,8 +392,8 @@
             start = jnp.where(owner == k, value(k), start)
         return start
 
-    taps = [by_lane(lambda k: prof_ref[k, 0, tap], jnp.zeros((8, by), F32)) for tap in range(TAPS)]
-    box = [by_lane(lambda k: box_ref[k, i], jnp.zeros((8, by), jnp.int32)) for i in range(6)]
+    taps = [by_lane(lambda k: prof_ref[(k * 3 + 0) * TAPS + tap], jnp.zeros((8, by), F32)) for tap in range(TAPS)]
+    box = [by_lane(lambda k: box_ref[k * 6 + i], jnp.zeros((8, by), jnp.int32)) for i in range(6)]
     within_y = (col_y >= box[4]) & (col_y < box[5])
     step = 5
     for first in range(1, deep - 1, step):
@@ -422,7 +426,7 @@
     mine = lax.axis_index("by") if count > 1 else 0
 
     def view(k, carry):
-        for part, part_ref in zip(range(count - 1, -1, -1), parts):
+        for part, part_ref in zip(order_of(count), parts):
             at = pl.ds(pl.multiple_of((mine ^ part) * rows, rows), rows)
             held[:, at, :] = gain_ref[k, :, at, :] * part_ref[k].astype(F32)
         quot_ref[k] = held[...].astype(BF16)
@@ -444,10 +448,10 @@
         cells = jnp.concatenate(cells, axis=1)
         mixed = jnp.dot(cells, yr_ref[k], preferred_element_type=F32)
         rows[...] = (mixed[:, :by] + mixed[:, by:]).reshape(bz, bx, by)
-        taps = [prof_ref[k, 0, tap] for tap in range(TAPS)]
+        taps = [prof_ref[(k * 3 + 0) * TAPS + tap] for tap in range(TAPS)]
         at = pl.ds(pl.multiple_of(k * bx, bx), bx)
-        low_z = box_ref[k, 0] - start_z + REACH
-        high_z = box_ref[k, 1] - start_z + REACH
+        low_z = box_ref[k * 6 + 0] - start_z + REACH
+        high_z = box_ref[k * 6 + 1] - start_z + REACH
         for first in range(0, deep, GROUP):
             some = (first + GROUP > low_z) & (first < high_z)
 
@@ -528,6 +532,7 @@
     ext = bx + 2 * PAD
     deep = bz + 2 * PAD
     shape = jax.ShapeDtypeStruct
+    profiles, view_boxes = profiles.reshape(-1), view_boxes.reshape(-1)
 
     def link_shape(link, reach, dtype):
         x, z = link
@@ -551,7 +556,6 @@
             nbytes=views * bz * bx * by * 4,
             name="pieces",
         )(order, recorded)]
-        parts, first, second = lax.optimization_barrier((parts, first, second))
         for other in range(1, count):
             parts[other] = lax.ppermute(parts[other], "by", [(i, i ^ other) for i in range(count)])
     else:
@@ -633,7 +637,7 @@
         flops=views * bz * bx * by * 40,
         nbytes=views * bz * bx * by * 8,
         name="quotient",
-    )(gain, *parts[::-1])
+    )(gain, *[parts[part] for part in order_of(len(parts))])
 
     mid, *sums = call(
         functools.partial(return_body, views, block, links),

time: 42.8 us -> 41.8 us (0.977)
  the two profiles are of different devices: /device:TPU:0 before, /device:TPU:13 now
where the time goes in v6:
time: 41.8 us; the launch traced here: 41.5 us
  Pallas kernels  17 us (41%)
  starting transfers between devices  14.4 us (34%)
  waiting for transfers between devices  6.28 us (15%)
  local copies, waits for them, and re-layouts  3.65 us (9%)
    ppermute x5, starting transfers between devices, exchange(): return lax.ppermute(cells, ('bx', 'bz'), pairs)  7.21 us
    pallas_call x1, Pallas kernels, local(): call(functools.partial(forward_body, views, block, counts, len(along_x)),...  6.27 us
    ppermute x2, starting transfers between devices, exchange_y(): lax.ppermute(cells, 'by', [(i, partner(i, count, swap)) for i in range(co...  4.51 us
    pallas_call x1, Pallas kernels, local(): call(functools.partial(return_body, views, block, links), [shape(block, F...  4.35 us
    ppermute x5, waiting for transfers between devices, exchange(): return lax.ppermute(cells, ('bx', 'bz'), pairs)  3.73 us
    ppermute x3, starting transfers between devices, local(): lax.ppermute(parts[other], 'by', [(i, i ^ other) for i in range(count)])  2.71 us
    ppermute x3, waiting for transfers between devices, local(): lax.ppermute(parts[other], 'by', [(i, i ^ other) for i in range(count)])  2.54 us
    unnamed x6, local copies, waits for them, and re-layouts  2.08 us
  transfers between devices with their start and end apart: 10, of which 3 were waited for; matrix products, arithmetic and copies ran while one was open for 4% of the time, Pallas kernels for 27%

profile of v6, /device:TPU:13, one launch (start us, length us, event | category | flops | bytes accessed | tf_op | source)
XLA Modules:
  0.0 41.5 jit_solution(6991464765833430453)
XLA Ops:
  0.0 0.0 copy-start
  0.0 0.9 %copy-done = f32[16,32,128]{2,1,0:T(8,128)S(1)} copy-done((f32[16,32,128]{2,1,0:T(8,128)S(1)}, f32[16,32,128]{2,1,0:T(8,128)}, u32[]{:S(2)}) %copy-start) | copy-done | bytes 262168
  1.0 0.2 columns.1
  1.1 0.2 collective-permute-start
  1.3 4.3 %collective-permute-start.1 = (bf16[16,512]{1,0:T(8,128)(2,1)S(1)}, bf16[16,512]{1,0:T(8,128)(2,1)S(1)}, u32[]{:S(2)}, u32[]{:S(2)}) collective-permute-start(bf16[16,512]{1,0:T(8,128)(2,1)S(1)} %get-tuple-element.29), channel_id=1, source_target_pairs={{0,0},{4,8},{8,4},{12,12},{1,1},{5,9},{9,5},{13,13},{2,2},{6,10},{... | collective-permute-start | bytes 49160 | tf_op jit(solution)/shard_map/ppermute | solution.py:80
  5.6 0.0 copy-start.2
  5.7 1.1 %copy-done.2 = bf16[6,16,8,512]{3,2,1,0:T(8,128)(2,1)S(1)} copy-done((bf16[6,16,8,512]{3,2,1,0:T(8,128)(2,1)S(1)}, bf16[6,16,8,512]{3,2,1,0:T(8,128)(2,1)}, u32[]{:S(2)}) %copy-start.2) | copy-done | bytes 786456
  6.8 0.7 %pieces.1 = (bf16[7,16,8,128]{3,2,1,0:T(8,128)(2,1)S(1)}, bf16[7,16,8,128]{3,2,1,0:T(8,128)(2,1)S(1)}, bf16[7,16,8,128]{3,2,1,0:T(8,128)(2,1)S(1)}, bf16[7,16,8,128]{3,2,1,0:T(8,128)(2,1)S(1)}) custom-call(bf16[16,512]{1,0:T(8,128)(2,1)S(1)} %get-tuple-element.28.order_ref, bf16[6,16,8,512]{3,2,1,0:T(8,128)(2,1)S(1)} %copy-done.2), custom_call_target="tpu_custom_call" | custom-call | bytes 1258291 | tf_op jit(solution)/shard_map/pieces/pallas_call | solution.py:552
  7.5 0.1 collective-permute-start.4
  7.5 1.2 %collective-permute-start.5 = (bf16[7,16,8,128]{3,2,1,0:T(8,128)(2,1)S(1)}, bf16[7,16,8,128]{3,2,1,0:T(8,128)(2,1)S(1)}, u32[]{:S(2)}, u32[]{:S(2)}) collective-permute-start(bf16[7,16,8,128]{3,2,1,0:T(8,128)(2,1)S(1)} %get-tuple-element.40), channel_id=1, source_target_pairs={{0,8},{4,12},{8,0},{12,4},{1,9},{5,13},{9,1},{13,5},{2,10},{6,14},... | collective-permute-start | bytes 688136 | tf_op jit(solution)/shard_map/ppermute | solution.py:560
  8.7 1.5 %collective-permute-start.6 = (bf16[7,16,8,128]{3,2,1,0:T(8,128)(2,1)S(1)}, bf16[7,16,8,128]{3,2,1,0:T(8,128)(2,1)S(1)}, u32[]{:S(2)}, u32[]{:S(2)}) collective-permute-start(bf16[7,16,8,128]{3,2,1,0:T(8,128)(2,1)S(1)} %get-tuple-element.41), channel_id=1, source_target_pairs={{0,12},{4,8},{8,4},{12,0},{1,13},{5,9},{9,5},{13,1},{2,14},{6,10},... | collective-permute-start | bytes 688136 | tf_op jit(solution)/shard_map/ppermute | solution.py:560
  10.2 0.0 collective-permute-done.first_ref
  10.2 0.0 collective-permute-done.1.second_ref
  10.2 0.3 edges.1
  10.4 2.1 %collective-permute-start.2 = (bf16[10,32,128]{2,1,0:T(8,128)(2,1)S(1)}, bf16[10,32,128]{2,1,0:T(8,128)(2,1)S(1)}, u32[]{:S(2)}, u32[]{:S(2)}) collective-permute-start(bf16[10,32,128]{2,1,0:T(8,128)(2,1)S(1)} %get-tuple-element.31), channel_id=1, source_target_pairs={{0,1},{1,0},{2,3},{3,2},{4,5},{5,4},{6,7},{7,6},{8,9},{9,8},{10,11... | collective-permute-start | bytes 245768 | tf_op jit(solution)/shard_map/ppermute | solution.py:74
  12.5 0.9 %collective-permute-done.2.refs_0_ = bf16[10,32,128]{2,1,0:T(8,128)(2,1)S(1)} collective-permute-done((bf16[10,32,128]{2,1,0:T(8,128)(2,1)S(1)}, bf16[10,32,128]{2,1,0:T(8,128)(2,1)S(1)}, u32[]{:S(2)}, u32[]{:S(2)}) %collective-permute-start.2) | collective-permute-done | bytes 81952 | tf_op jit(solution)/shard_map/ppermute | solution.py:74
  13.5 0.3 deep.1
  13.8 1.2 %collective-permute-start.3 = (bf16[40,8,128]{2,1,0:T(8,128)(2,1)S(1)}, bf16[40,8,128]{2,1,0:T(8,128)(2,1)S(1)}, u32[]{:S(2)}, u32[]{:S(2)}) collective-permute-start(bf16[40,8,128]{2,1,0:T(8,128)(2,1)S(1)} %get-tuple-element.37), channel_id=1, source_target_pairs={{0,2},{1,3},{2,0},{3,1},{4,6},{5,7},{6,4},{7,5},{8,10},{9,11},{10,... | collective-permute-start | bytes 245768 | tf_op jit(solution)/shard_map/ppermute | solution.py:74
  15.0 0.8 %reshape.6.prof_ref = f32[270]{0:T(512)S(1)} reshape(f32[6,3,15]{2,1,0:T(4,128)} %param.6) | data formatting | bytes 2160 | tf_op jit(solution)/shard_map/reshape | solution.py:535
  15.8 0.8 %reshape.7.box_ref = s32[36]{0:T(128)S(1)} reshape(s32[6,6]{1,0:T(8,128)} %param.7) | data formatting | bytes 288 | tf_op jit(solution)/shard_map/reshape | solution.py:535
  16.6 2.0 %forward_bands.1 = (bf16[6,160,256]{2,1,0:T(8,128)(2,1)S(1)}, bf16[6,160,256]{2,1,0:T(8,128)(2,1)S(1)}, bf16[192,96]{1,0:T(8,128)(2,1)S(1)}) custom-call(bf16[16,512]{1,0:T(8,128)(2,1)S(1)} %get-tuple-element.28.order_ref, f32[270]{0:T(512)S(1)} %reshape.6.prof_ref), custom_call_target="tpu_custom_call" | custom-call | flops 2516582 | bytes 314572 | tf_op jit(solution)/shard_map/forward_bands/pallas_call | solution.py:593
  18.5 0.0 collective-permute-done.3.refs_0_
  18.5 0.0 copy-start.1
  18.6 6.3 %forward.1.order_ref.gain_ref = f32[7,16,32,128]{3,2,1,0:T(8,128)S(1)} custom-call(f32[270]{0:T(512)S(1)} %reshape.6.prof_ref, s32[36]{0:T(128)S(1)} %reshape.7.box_ref, f32[32,32,128]{2,1,0:T(8,128)S(1)} %get-tuple-element.32.cells_ref, f32[32,32,32]{2,1,0:T(8,128)S(1)} %get-tuple-element.33.halos_ref, bf16[6,160,256]{2,1,0:T(8,128)(2,1)S(1)} %get-tuple-element.34.yf_ref, ...), custom_call_target="tpu_custom_call" | custom-call | flops 566231040 | bytes 2516582 | tf_op jit(solution)/shard_map/forward/pallas_call | solution.py:606
  24.8 0.0 copy-done.1
  24.8 1.7 %return_bands.1 = (bf16[6,256,256]{2,1,0:T(8,128)(2,1)S(1)}, bf16[96,192]{1,0:T(8,128)(2,1)S(1)}, f32[16,32,128]{2,1,0:T(8,128)S(1)}) custom-call(f32[7,16,32,128]{3,2,1,0:T(8,128)S(1)} %forward.1.order_ref.gain_ref, f32[270]{0:T(512)S(1)} %reshape.6.prof_ref, s32[36]{0:T(128)S(1)} %reshape.7.box_ref, f32[16,32,128]{2,1,0:T(8,128)S(1)} %copy-done.1), custom_call_target="tpu_custom_call" | custom-call | flops 2516582 | bytes 314572 | tf_op jit(solution)/shard_map/return_bands/pallas_call | solution.py:620
  26.6 0.0 collective-permute-done.4.refs_0_
  26.6 0.0 collective-permute-done.5.refs_1_
  26.6 2.5 %collective-permute-done.6.refs_2_ = bf16[7,16,8,128]{3,2,1,0:T(8,128)(2,1)S(1)} collective-permute-done((bf16[7,16,8,128]{3,2,1,0:T(8,128)(2,1)S(1)}, bf16[7,16,8,128]{3,2,1,0:T(8,128)(2,1)S(1)}, u32[]{:S(2)}, u32[]{:S(2)}) %collective-permute-start.6) | collective-permute-done | bytes 229408 | tf_op jit(solution)/shard_map/ppermute | solution.py:560
  29.1 0.5 %quotient.1.quot_ref = bf16[7,16,32,128]{3,2,1,0:T(8,128)(2,1)S(1)} custom-call(f32[7,16,32,128]{3,2,1,0:T(8,128)S(1)} %forward.1.order_ref.gain_ref, bf16[7,16,8,128]{3,2,1,0:T(8,128)(2,1)S(1)} %collective-permute-done.4.refs_0_, bf16[7,16,8,128]{3,2,1,0:T(8,128)(2,1)S(1)} %collective-permute-done.5.refs_1_, ...), custom_call_target="tpu_custom_call" | custom-call | flops 12582912 | bytes 2516582 | tf_op jit(solution)/shard_map/quotient/pallas_call | solution.py:632
  29.6 4.3 %returned.1 = (f32[16,32,128]{2,1,0:T(8,128)S(1)}, f32[7,32,128]{2,1,0:T(8,128)S(1)}, f32[16,8,128]{2,1,0:T(8,128)S(1)}, f32[7,8,128]{2,1,0:T(8,128)S(1)}) custom-call(f32[270]{0:T(512)S(1)} %reshape.6.prof_ref, s32[36]{0:T(128)S(1)} %reshape.7.box_ref, bf16[7,16,32,128]{3,2,1,0:T(8,128)(2,1)S(1)} %quotient.1.quot_ref, ...), custom_call_target="tpu_custom_call" | custom-call | flops 283115520 | bytes 2516582 | tf_op jit(solution)/shard_map/returned/pallas_call | solution.py:642
  33.9 2.2 %collective-permute-start.7 = (f32[7,32,128]{2,1,0:T(8,128)S(1)}, f32[7,32,128]{2,1,0:T(8,128)S(1)}, u32[]{:S(2)}, u32[]{:S(2)}) collective-permute-start(f32[7,32,128]{2,1,0:T(8,128)S(1)} %get-tuple-element.46), channel_id=1, source_target_pairs={{0,1},{1,0},{2,3},{3,2},{4,5},{5,4},{6,7},{7,6},{8,9},{9,8},{10,11... | collective-permute-start | bytes 344072 | tf_op jit(solution)/shard_map/ppermute | solution.py:74
  36.1 1.2 %collective-permute-start.8 = (f32[16,8,128]{2,1,0:T(8,128)S(1)}, f32[16,8,128]{2,1,0:T(8,128)S(1)}, u32[]{:S(2)}, u32[]{:S(2)}) collective-permute-start(f32[16,8,128]{2,1,0:T(8,128)S(1)} %get-tuple-element.47), channel_id=1, source_target_pairs={{0,2},{1,3},{2,0},{3,1},{4,6},{5,7},{6,4},{7,5},{8,10},{9,11},{10,... | collective-permute-start | bytes 196616 | tf_op jit(solution)/shard_map/ppermute | solution.py:74
  37.4 0.5 %collective-permute-start.9 = (f32[7,8,128]{2,1,0:T(8,128)S(1)}, f32[7,8,128]{2,1,0:T(8,128)S(1)}, u32[]{:S(2)}, u32[]{:S(2)}) collective-permute-start(f32[7,8,128]{2,1,0:T(8,128)S(1)} %get-tuple-element.48), channel_id=1, source_target_pairs={{0,3},{1,2},{2,1},{3,0},{4,7},{5,6},{6,5},{7,4},{8,11},{9,10},{10,... | collective-permute-start | bytes 86024 | tf_op jit(solution)/shard_map/ppermute | solution.py:74
  37.8 2.8 %collective-permute-done.9.refs_2_ = f32[7,8,128]{2,1,0:T(8,128)S(1)} collective-permute-done((f32[7,8,128]{2,1,0:T(8,128)S(1)}, f32[7,8,128]{2,1,0:T(8,128)S(1)}, u32[]{:S(2)}, u32[]{:S(2)}) %collective-permute-start.9) | collective-permute-done | bytes 28704 | tf_op jit(solution)/shard_map/ppermute | solution.py:74
  40.7 0.0 collective-permute-done.8.refs_1_
  40.7 0.0 collective-permute-done.7.refs_0_
  40.7 0.8 %finish.1 = f32[16,32,128]{2,1,0:T(8,128)} custom-call(f32[16,32,128]{2,1,0:T(8,128)S(1)} %get-tuple-element.38.share_ref, f32[16,32,128]{2,1,0:T(8,128)S(1)} %get-tuple-element.45.mid_ref, f32[7,32,128]{2,1,0:T(8,128)S(1)} %collective-permute-done.7.refs_0_, f32[16,8,128]{2,1,0:T(8,128)S(1)} %collective-permute-done.8.refs_1_, ...), custom_call_target="tpu_custom_call" | custom-call | bytes 629145 | tf_op jit(solution)/shard_map/finish/pallas_call | solution.py:657
Async XLA Ops:
  0.0 0.9 %copy-start = (f32[16,32,128]{2,1,0:T(8,128)S(1)}, f32[16,32,128]{2,1,0:T(8,128)}, u32[]{:S(2)}) copy-start(f32[16,32,128]{2,1,0:T(8,128)} %est_ref.3) | copy-start | bytes 786436
  1.1 9.0 %collective-permute-start = (bf16[16,512]{1,0:T(8,128)(2,1)S(1)}, bf16[16,512]{1,0:T(8,128)(2,1)S(1)}, u32[]{:S(2)}, u32[]{:S(2)}) collective-permute-start(bf16[16,512]{1,0:T(8,128)(2,1)S(1)} %get-tuple-element.28.order_ref), channel_id=1, source_target_pairs={{0,4},{4,0},{8,12},{12,8},{1,5},{5,1},{9,13},{13,9},{2,6},{6,2},{1... | collective-permute-start | bytes 49160 | tf_op jit(solution)/shard_map/ppermute | solution.py:80
  1.3 8.9 %collective-permute-start.1 = (bf16[16,512]{1,0:T(8,128)(2,1)S(1)}, bf16[16,512]{1,0:T(8,128)(2,1)S(1)}, u32[]{:S(2)}, u32[]{:S(2)}) collective-permute-start(bf16[16,512]{1,0:T(8,128)(2,1)S(1)} %get-tuple-element.29), channel_id=1, source_target_pairs={{0,0},{4,8},{8,4},{12,12},{1,1},{5,9},{9,5},{13,13},{2,2},{6,10},{... | collective-permute-start | bytes 49160 | tf_op jit(solution)/shard_map/ppermute | solution.py:80
  5.6 1.1 %copy-start.2 = (bf16[6,16,8,512]{3,2,1,0:T(8,128)(2,1)S(1)}, bf16[6,16,8,512]{3,2,1,0:T(8,128)(2,1)}, u32[]{:S(2)}) copy-start(bf16[6,16,8,512]{3,2,1,0:T(8,128)(2,1)} %rec_ref.1) | copy-start | bytes 2359300
  7.5 19.1 %collective-permute-start.4 = (bf16[7,16,8,128]{3,2,1,0:T(8,128)(2,1)S(1)}, bf16[7,16,8,128]{3,2,1,0:T(8,128)(2,1)S(1)}, u32[]{:S(2)}, u32[]{:S(2)}) collective-permute-start(bf16[7,16,8,128]{3,2,1,0:T(8,128)(2,1)S(1)} %get-tuple-element.39), channel_id=1, source_target_pairs={{0,4},{4,0},{8,12},{12,8},{1,5},{5,1},{9,13},{13,9},{2,6},{6,2},{1... | collective-permute-start | bytes 688136 | tf_op jit(solution)/shard_map/ppermute | solution.py:560
  7.5 19.0 %collective-permute-start.5 = (bf16[7,16,8,128]{3,2,1,0:T(8,128)(2,1)S(1)}, bf16[7,16,8,128]{3,2,1,0:T(8,128)(2,1)S(1)}, u32[]{:S(2)}, u32[]{:S(2)}) collective-permute-start(bf16[7,16,8,128]{3,2,1,0:T(8,128)(2,1)S(1)} %get-tuple-element.40), channel_id=1, source_target_pairs={{0,8},{4,12},{8,0},{12,4},{1,9},{5,13},{9,1},{13,5},{2,10},{6,14},... | collective-permute-start | bytes 688136 | tf_op jit(solution)/shard_map/ppermute | solution.py:560
  8.7 20.4 %collective-permute-start.6 = (bf16[7,16,8,128]{3,2,1,0:T(8,128)(2,1)S(1)}, bf16[7,16,8,128]{3,2,1,0:T(8,128)(2,1)S(1)}, u32[]{:S(2)}, u32[]{:S(2)}) collective-permute-start(bf16[7,16,8,128]{3,2,1,0:T(8,128)(2,1)S(1)} %get-tuple-element.41), channel_id=1, source_target_pairs={{0,12},{4,8},{8,4},{12,0},{1,13},{5,9},{9,5},{13,1},{2,14},{6,10},... | collective-permute-start | bytes 688136 | tf_op jit(solution)/shard_map/ppermute | solution.py:560
  10.4 3.0 %collective-permute-start.2 = (bf16[10,32,128]{2,1,0:T(8,128)(2,1)S(1)}, bf16[10,32,128]{2,1,0:T(8,128)(2,1)S(1)}, u32[]{:S(2)}, u32[]{:S(2)}) collective-permute-start(bf16[10,32,128]{2,1,0:T(8,128)(2,1)S(1)} %get-tuple-element.31), channel_id=1, source_target_pairs={{0,1},{1,0},{2,3},{3,2},{4,5},{5,4},{6,7},{7,6},{8,9},{9,8},{10,11... | collective-permute-start | bytes 245768 | tf_op jit(solution)/shard_map/ppermute | solution.py:74
  13.8 4.7 %collective-permute-start.3 = (bf16[40,8,128]{2,1,0:T(8,128)(2,1)S(1)}, bf16[40,8,128]{2,1,0:T(8,128)(2,1)S(1)}, u32[]{:S(2)}, u32[]{:S(2)}) collective-permute-start(bf16[40,8,128]{2,1,0:T(8,128)(2,1)S(1)} %get-tuple-element.37), channel_id=1, source_target_pairs={{0,2},{1,3},{2,0},{3,1},{4,6},{5,7},{6,4},{7,5},{8,10},{9,11},{10,... | collective-permute-start | bytes 245768 | tf_op jit(solution)/shard_map/ppermute | solution.py:74
  18.5 6.3 %copy-start.1 = (f32[16,32,128]{2,1,0:T(8,128)S(1)}, f32[16,32,128]{2,1,0:T(8,128)}, u32[]{:S(2)}) copy-start(f32[16,32,128]{2,1,0:T(8,128)} %est_ref.3) | copy-start | bytes 786436
  33.9 6.7 %collective-permute-start.7 = (f32[7,32,128]{2,1,0:T(8,128)S(1)}, f32[7,32,128]{2,1,0:T(8,128)S(1)}, u32[]{:S(2)}, u32[]{:S(2)}) collective-permute-start(f32[7,32,128]{2,1,0:T(8,128)S(1)} %get-tuple-element.46), channel_id=1, source_target_pairs={{0,1},{1,0},{2,3},{3,2},{4,5},{5,4},{6,7},{7,6},{8,9},{9,8},{10,11... | collective-permute-start | bytes 344072 | tf_op jit(solution)/shard_map/ppermute | solution.py:74
  36.1 4.5 %collective-permute-start.8 = (f32[16,8,128]{2,1,0:T(8,128)S(1)}, f32[16,8,128]{2,1,0:T(8,128)S(1)}, u32[]{:S(2)}, u32[]{:S(2)}) collective-permute-start(f32[16,8,128]{2,1,0:T(8,128)S(1)} %get-tuple-element.47), channel_id=1, source_target_pairs={{0,2},{1,3},{2,0},{3,1},{4,6},{5,7},{6,4},{7,5},{8,10},{9,11},{10,... | collective-permute-start | bytes 196616 | tf_op jit(solution)/shard_map/ppermute | solution.py:74
  37.4 3.3 %collective-permute-start.9 = (f32[7,8,128]{2,1,0:T(8,128)S(1)}, f32[7,8,128]{2,1,0:T(8,128)S(1)}, u32[]{:S(2)}, u32[]{:S(2)}) collective-permute-start(f32[7,8,128]{2,1,0:T(8,128)S(1)} %get-tuple-element.48), channel_id=1, source_target_pairs={{0,3},{1,2},{2,1},{3,0},{4,7},{5,6},{6,5},{7,4},{8,11},{9,10},{10,... | collective-permute-start | bytes 86024 | tf_op jit(solution)/shard_map/ppermute | solution.py:74

commit v7 on v6

--- a/solution.py
+++ b/solution.py
@@ -13,7 +13,7 @@
 SIDE = 2 * PAD
 BACKGROUND = 0.05
 GROUP = 6
-WEIGHT = 0.8
+WEIGHT = 0.5
 
 F32 = jnp.float32
 BF16 = jnp.bfloat16
@@ -82,10 +82,6 @@
     ]
 
 
-def order_of(count):
-    return [1, 2, 3, 0] if count == 4 else range(count - 1, -1, -1)
-
-
 def banded(offset, tap_of):
     matrix = jnp.zeros(offset.shape, F32)
     for tap in range(TAPS):
@@ -250,7 +246,7 @@
     lax.fori_loop(0, views, view, 0)
 
 
-def return_bands_body(views, order_ref, prof_ref, box_ref, est_ref, yr_ref, xr_ref, share_ref):
+def return_bands_body(views, paired, order_ref, prof_ref, box_ref, est_ref, yr_ref, xr_ref, share_ref):
     bz, bx, by = est_ref.shape
     ext = bx + 2 * PAD
     start_z = lax.axis_index("bz") * bz
@@ -278,16 +274,19 @@
 
     lax.fori_loop(0, views, view, 0)
 
+    half_rows = bx // 2
     shape_x = (ext, views * bx)
     target = iota(shape_x, 0) - PAD
     col = iota(shape_x, 1)
+    slot = lax.div(col, views * half_rows)
+    half = jnp.where(slot == 0, half_of(0, paired), half_of(1, paired))
+    owner = lax.div(lax.rem(col, views * half_rows), half_rows)
+    source = half * half_rows + lax.rem(col, half_rows)
 
     def back_view(k, matrix):
-        source = col - k * bx
         back = banded(REACH - source + target, lambda tap: prof_ref[(k * 3 + 1) * TAPS + tap])
-        within = (source >= 0) & (source < bx)
-        within = within & (target >= box_ref[k * 6 + 2] - start_x) & (target < box_ref[k * 6 + 3] - start_x)
-        return jnp.where(within, back, matrix)
+        within = (target >= box_ref[k * 6 + 2] - start_x) & (target < box_ref[k * 6 + 3] - start_x)
+        return jnp.where(owner == k, jnp.where(within, back, 0.0), matrix)
 
     high, low = halves(lax.fori_loop(0, views, back_view, jnp.zeros(shape_x, F32)))
     xr_ref[:ext] = high
@@ -418,38 +417,38 @@
     lax.fori_loop(0, bz, beside_plane, 0)
 
 
-def quotient_body(views, block, count, gain_ref, *refs):
+def half_of(slot, paired):
+    return lax.div(lax.axis_index("by"), 2) ^ slot if paired else slot
+
+
+def half_body(views, block, slot, paired, count, prof_ref, box_ref, gain_ref, yr_ref, *refs):
     parts = refs[:count]
-    quot_ref, held = refs[count:]
+    high_ref, low_ref, quot, held, rows = refs[count:]
     bz, bx, by = block
-    rows = bx // count
-    mine = lax.axis_index("by") if count > 1 else 0
+    deep = bz + 2 * REACH
+    half_rows = bx // 2
+    part_rows = half_rows // count
+    begin = half_of(slot, paired) * half_rows
+    start_z = lax.axis_index("bz") * bz
+
+    def quotient(k, carry):
+        for i, part_ref in enumerate(parts):
+            at = lax.rem(lax.axis_index("by") ^ i, 2) * part_rows if count == 2 else 0
+            gain = gain_ref[k, :, pl.ds(pl.multiple_of(begin + at, 8), part_rows), :]
+            at = pl.ds(pl.multiple_of(at, 8), part_rows)
+            held[:, at, :] = gain * part_ref[k].astype(F32)
+        quot[k] = held[...].astype(BF16)
+        return carry
+
+    lax.fori_loop(0, views + 1, quotient, 0)
 
     def view(k, carry):
-        for part, part_ref in zip(order_of(count), parts):
-            at = pl.ds(pl.multiple_of((mine ^ part) * rows, rows), rows)
-            held[:, at, :] = gain_ref[k, :, at, :] * part_ref[k].astype(F32)
-        quot_ref[k] = held[...].astype(BF16)
-        return carry
-
-    lax.fori_loop(0, views + 1, view, 0)
-
-
-def return_body(views, block, links, prof_ref, box_ref, quot_ref, yr_ref, xr_ref, mid_ref, *refs):
-    bz, bx, by = block
-    ext = bx + 2 * PAD
-    deep = bz + 2 * REACH
-    link_refs = refs[: len(links)]
-    rows, high_rows, low_rows, total = refs[len(links) :]
-    start_z = lax.axis_index("bz") * bz
-
-    def view(k, carry):
-        cells = [quot_ref[i].reshape(bz * bx, by) for i in (k, views)]
+        cells = [quot[i].reshape(bz * half_rows, by) for i in (k, views)]
         cells = jnp.concatenate(cells, axis=1)
         mixed = jnp.dot(cells, yr_ref[k], preferred_element_type=F32)
-        rows[...] = (mixed[:, :by] + mixed[:, by:]).reshape(bz, bx, by)
+        rows[...] = (mixed[:, :by] + mixed[:, by:]).reshape(bz, half_rows, by)
         taps = [prof_ref[(k * 3 + 0) * TAPS + tap] for tap in range(TAPS)]
-        at = pl.ds(pl.multiple_of(k * bx, bx), bx)
+        at = pl.ds(pl.multiple_of(k * half_rows, half_rows), half_rows)
         low_z = box_ref[k * 6 + 0] - start_z + REACH
         high_z = box_ref[k * 6 + 1] - start_z + REACH
         for first in range(0, deep, GROUP):
@@ -457,33 +456,45 @@
 
             @pl.when(some)
             def _():
-                for tile in range(0, bx, 16):
-                    for out in range(first, first + GROUP):
-                        plane = out - REACH
-                        parts = []
-                        for half in (tile, tile + 8):
-                            part = None
-                            for source in range(max(0, plane - REACH), min(bz, plane + REACH + 1)):
-                                term = taps[REACH - source + plane] * rows[source, half : half + 8, :]
-                                part = term if part is None else part + term
-                            parts.append(part)
-                        here = jnp.where((out >= low_z) & (out < high_z), 1.0, 0.0)
-                        high, low = halves(here * jnp.concatenate(parts, axis=0))
-                        at_x = pl.ds(pl.multiple_of(k * bx + tile, 16), 16)
-                        high_rows[out, at_x, :] = high
-                        low_rows[out, at_x, :] = low
+                for out in range(first, first + GROUP):
+                    plane = out - REACH
+                    parts = []
+                    for tile in range(0, half_rows, 8):
+                        part = None
+                        for source in range(max(0, plane - REACH), min(bz, plane + REACH + 1)):
+                            term = taps[REACH - source + plane] * rows[source, tile : tile + 8, :]
+                            part = term if part is None else part + term
+                        parts.append(part)
+                    here = jnp.where((out >= low_z) & (out < high_z), 1.0, 0.0)
+                    high, low = halves(here * jnp.concatenate(parts, axis=0))
+                    high_ref[out, at, :] = high
+                    low_ref[out, at, :] = low
 
             @pl.when(jnp.logical_not(some))
             def _():
-                high_rows[first : first + GROUP, at, :] = jnp.zeros((GROUP, bx, by), BF16)
-                low_rows[first : first + GROUP, at, :] = jnp.zeros((GROUP, bx, by), BF16)
+                high_ref[first : first + GROUP, at, :] = jnp.zeros((GROUP, half_rows, by), BF16)
+                low_ref[first : first + GROUP, at, :] = jnp.zeros((GROUP, half_rows, by), BF16)
 
         return carry
 
     lax.fori_loop(0, views, view, 0)
+
+
+def return_body(block, links, xr_ref, *refs):
+    rows_refs, mid_ref, link_refs, total = refs[:4], refs[4], refs[5:-1], refs[-1]
+    bz, bx, by = block
+    ext = bx + 2 * PAD
+    deep = bz + 2 * REACH
+
+    def both(first_ref, second_ref, out):
+        planes = [
+            jnp.concatenate([first_ref[i], second_ref[i]], axis=0) for i in (out, out + 1)
+        ]
+        return jnp.concatenate(planes, axis=1)
+
     for out in range(0, deep, 2):
-        high = jnp.concatenate([high_rows[out], high_rows[out + 1]], axis=1)
-        low = jnp.concatenate([low_rows[out], low_rows[out + 1]], axis=1)
+        high = both(rows_refs[0], rows_refs[2], out)
+        low = both(rows_refs[1], rows_refs[3], out)
         mixed = jnp.dot(xr_ref[...], high, preferred_element_type=F32)
         mixed = mixed[:ext] + mixed[ext:] + jnp.dot(xr_ref[:ext], low, preferred_element_type=F32)
         total[out] = mixed[:, :by]
@@ -548,7 +559,7 @@
     )(estimate)
     first, second = exchange_y(order, second)
 
-    if count & (count - 1) == 0 and count <= 4 and part_rows % 8 == 0:
+    if count == 4 and part_rows % 8 == 0:
         parts = [*call(
             pieces_body,
             [shape((views + 1, bz, part_rows, by), BF16)] * count,
@@ -556,7 +567,9 @@
             nbytes=views * bz * bx * by * 4,
             name="pieces",
         )(order, recorded)]
-        for other in range(1, count):
+        parts[1] = lax.ppermute(parts[1], "by", [(i, i ^ 1) for i in range(count)])
+        parts[2:], first, second = lax.optimization_barrier((parts[2:], first, second))
+        for other in range(2, count):
             parts[other] = lax.ppermute(parts[other], "by", [(i, i ^ other) for i in range(count)])
     else:
         tiles = jnp.moveaxis(recorded.reshape(views, bz, part_rows, count, by), 3, 0)
@@ -568,6 +581,12 @@
         tiles = jnp.concatenate([tiles, beside], axis=1)
         tiles = lax.all_to_all(tiles, "by", split_axis=0, concat_axis=0, tiled=True)
         parts = [jnp.moveaxis(tiles, 0, 2).reshape(views + 1, bz, bx, by)]
+
+    paired = len(parts) == 4
+    if paired:
+        halves_of = [parts[:2], parts[2:]]
+    else:
+        halves_of = [[parts[0][:, :, : bx // 2]], [parts[0][:, :, bx // 2 :]]]
 
     along_x, along_z = swaps_of(counts[0]), swaps_of(counts[1])
     halo, *edges = call(
@@ -618,7 +637,7 @@
     )(profiles, view_boxes, cells, halos, yf, yh, xf, *edges)
 
     yr, xr, share = call(
-        functools.partial(return_bands_body, views),
+        functools.partial(return_bands_body, views, paired),
         [
             shape((views, 2 * by, 2 * by), BF16),
             shape((2 * ext, views * bx), BF16),
@@ -629,30 +648,32 @@
         nbytes=views * by * by * 4,
         name="return_bands",
     )(gain, profiles, view_boxes, estimate)
-    quot = call(
-        functools.partial(quotient_body, views, block, len(parts)),
-        shape((views + 1, bz, bx, by), BF16),
-        [VMEM] * (1 + len(parts)),
-        [pltpu.VMEM((bz, bx, by), F32)],
-        flops=views * bz * bx * by * 40,
-        nbytes=views * bz * bx * by * 8,
-        name="quotient",
-    )(gain, *[parts[part] for part in order_of(len(parts))])
+    half_rows = shape((bz + 2 * REACH, views * bx // 2, by), BF16)
+    half_sums = []
+    for slot, cells in enumerate(halves_of):
+        half_sums += call(
+            functools.partial(half_body, views, block, slot, paired, len(cells)),
+            [half_rows, half_rows],
+            [SMEM] * 2 + [VMEM] * (2 + len(cells)),
+            [
+                pltpu.VMEM((views + 1, bz, bx // 2, by), BF16),
+                pltpu.VMEM((bz, bx // 2, by), F32),
+                pltpu.VMEM((bz, bx // 2, by), F32),
+            ],
+            flops=views * bz * ext * by * 300,
+            nbytes=views * bz * bx * by * 4,
+            name="half" + str(slot),
+        )(profiles, view_boxes, gain, yr, *cells)
 
     mid, *sums = call(
-        functools.partial(return_body, views, block, links),
+        functools.partial(return_body, block, links),
         [shape(block, F32)] + [link_shape(link, REACH, F32) for link in links],
-        [SMEM] * 2 + [VMEM] * 3,
-        [
-            pltpu.VMEM((bz, bx, by), F32),
-            pltpu.VMEM((bz + 2 * REACH, views * bx, by), BF16),
-            pltpu.VMEM((bz + 2 * REACH, views * bx, by), BF16),
-            pltpu.VMEM((bz + 2 * REACH, ext, by), F32),
-        ],
-        flops=views * bz * ext * by * 600,
-        nbytes=views * bz * bx * by * 8,
+        [VMEM] * 5,
+        [pltpu.VMEM((bz + 2 * REACH, ext, by), F32)],
+        flops=views * bz * ext * by * 100,
+        nbytes=views * bz * bx * by * 4,
         name="returned",
-    )(profiles, view_boxes, quot, yr, xr)
+    )(xr, *half_sums)
     sums = [exchange(cells, link, *counts) for link, cells in zip(links, sums)]
     return call(
         functools.partial(finish_body, counts, links),

time: 41.8 us -> 41 us (0.981)
  waiting for transfers between devices: 6.28 us -> 3.75 us
  Pallas kernels: 17 us -> 18.7 us
    ppermute x3 -> x2, waiting for transfers between devices: 2.54 us -> 0.01 us  [local(): lax.ppermute(parts[other], 'by', [(i, i ^ other) for i in range(count)])]
    pallas_call x3 -> x4, Pallas kernels: 6.51 us -> 8.39 us  [the longest x2 6 us: local(): call(functools.partial(half_body, views, block, slot, paired, len(cells))...]
    ppermute x3 -> x2, starting transfers between devices: 2.71 us -> 2.62 us  [local(): lax.ppermute(parts[other], 'by', [(i, i ^ other) for i in range(count)])]
  transfers between devices with their start and end apart: 10 -> 10, of which waited for: 3 -> 2; matrix products, arithmetic and copies ran while one was open for 4% -> 4% of each run, Pallas kernels for 27% -> 35%
where the time goes in v7:
time: 41 us; the launch traced here: 40.6 us
  Pallas kernels  18.7 us (46%)
  starting transfers between devices  14.4 us (35%)
  waiting for transfers between devices  3.75 us (9%)
  local copies, waits for them, and re-layouts  3.65 us (9%)
    ppermute x5, starting transfers between devices, exchange(): return lax.ppermute(cells, ('bx', 'bz'), pairs)  7.16 us
    pallas_call x1, Pallas kernels, local(): call(functools.partial(forward_body, views, block, counts, len(along_x)),...  6.11 us
    pallas_call x2, Pallas kernels, local(): call(functools.partial(half_body, views, block, slot, paired, len(cells))...  6 us
    ppermute x2, starting transfers between devices, exchange_y(): lax.ppermute(cells, 'by', [(i, partner(i, count, swap)) for i in range(co...  4.51 us
    ppermute x5, waiting for transfers between devices, exchange(): return lax.ppermute(cells, ('bx', 'bz'), pairs)  3.74 us
    ppermute x2, starting transfers between devices, local(): lax.ppermute(parts[other], 'by', [(i, i ^ other) for i in range(count)])  2.62 us
    unnamed x6, local copies, waits for them, and re-layouts  2.08 us
    pallas_call x1, Pallas kernels, local(): call(functools.partial(forward_bands_body, views, block), [shape((views,...  1.96 us
  transfers between devices with their start and end apart: 10, of which 2 were waited for; matrix products, arithmetic and copies ran while one was open for 4% of the time, Pallas kernels for 35%

profile of v7, /device:TPU:13, one launch (start us, length us, event | category | flops | bytes accessed | tf_op | source)
XLA Modules:
  0.0 40.6 jit_solution(17385456766605442510)
XLA Ops:
  0.0 0.0 copy-start
  0.0 0.9 %copy-done = f32[16,32,128]{2,1,0:T(8,128)S(1)} copy-done((f32[16,32,128]{2,1,0:T(8,128)S(1)}, f32[16,32,128]{2,1,0:T(8,128)}, u32[]{:S(2)}) %copy-start) | copy-done | bytes 262168
  1.0 0.2 columns.1
  1.1 0.2 collective-permute-start
  1.3 4.3 %collective-permute-start.1 = (bf16[16,512]{1,0:T(8,128)(2,1)S(1)}, bf16[16,512]{1,0:T(8,128)(2,1)S(1)}, u32[]{:S(2)}, u32[]{:S(2)}) collective-permute-start(bf16[16,512]{1,0:T(8,128)(2,1)S(1)} %get-tuple-element.39), channel_id=1, source_target_pairs={{0,0},{4,8},{8,4},{12,12},{1,1},{5,9},{9,5},{13,13},{2,2},{6,10},{... | collective-permute-start | bytes 49160 | tf_op jit(solution)/shard_map/ppermute | solution.py:80
  5.6 0.0 copy-start.2
  5.7 1.1 %copy-done.2 = bf16[6,16,8,512]{3,2,1,0:T(8,128)(2,1)S(1)} copy-done((bf16[6,16,8,512]{3,2,1,0:T(8,128)(2,1)S(1)}, bf16[6,16,8,512]{3,2,1,0:T(8,128)(2,1)}, u32[]{:S(2)}) %copy-start.2) | copy-done | bytes 786456
  6.8 0.7 %pieces.1 = (bf16[7,16,8,128]{3,2,1,0:T(8,128)(2,1)S(1)}, bf16[7,16,8,128]{3,2,1,0:T(8,128)(2,1)S(1)}, bf16[7,16,8,128]{3,2,1,0:T(8,128)(2,1)S(1)}, bf16[7,16,8,128]{3,2,1,0:T(8,128)(2,1)S(1)}) custom-call(bf16[16,512]{1,0:T(8,128)(2,1)S(1)} %get-tuple-element.36.order_ref, bf16[6,16,8,512]{3,2,1,0:T(8,128)(2,1)S(1)} %copy-done.2), custom_call_target="tpu_custom_call" | custom-call | bytes 786432 | tf_op jit(solution)/shard_map/pieces/pallas_call | solution.py:563
  7.5 0.1 collective-permute-start.4
  7.5 0.0 collective-permute-done.first_ref
  7.5 0.0 collective-permute-done.1.second_ref
  7.6 1.2 %collective-permute-start.5 = (bf16[7,16,8,128]{3,2,1,0:T(8,128)(2,1)S(1)}, bf16[7,16,8,128]{3,2,1,0:T(8,128)(2,1)S(1)}, u32[]{:S(2)}, u32[]{:S(2)}) collective-permute-start(bf16[7,16,8,128]{3,2,1,0:T(8,128)(2,1)S(1)} %get-tuple-element.57), channel_id=1, source_target_pairs={{0,8},{4,12},{8,0},{12,4},{1,9},{5,13},{9,1},{13,5},{2,10},{6,14},... | collective-permute-start | bytes 688136 | tf_op jit(solution)/shard_map/ppermute | solution.py:573
  8.7 1.5 %collective-permute-start.6 = (bf16[7,16,8,128]{3,2,1,0:T(8,128)(2,1)S(1)}, bf16[7,16,8,128]{3,2,1,0:T(8,128)(2,1)S(1)}, u32[]{:S(2)}, u32[]{:S(2)}) collective-permute-start(bf16[7,16,8,128]{3,2,1,0:T(8,128)(2,1)S(1)} %get-tuple-element.58), channel_id=1, source_target_pairs={{0,12},{4,8},{8,4},{12,0},{1,13},{5,9},{9,5},{13,1},{2,14},{6,10},... | collective-permute-start | bytes 688136 | tf_op jit(solution)/shard_map/ppermute | solution.py:573
  10.2 0.3 edges.1
  10.4 2.1 %collective-permute-start.2 = (bf16[10,32,128]{2,1,0:T(8,128)(2,1)S(1)}, bf16[10,32,128]{2,1,0:T(8,128)(2,1)S(1)}, u32[]{:S(2)}, u32[]{:S(2)}) collective-permute-start(bf16[10,32,128]{2,1,0:T(8,128)(2,1)S(1)} %get-tuple-element.43), channel_id=1, source_target_pairs={{0,1},{1,0},{2,3},{3,2},{4,5},{5,4},{6,7},{7,6},{8,9},{9,8},{10,11... | collective-permute-start | bytes 245768 | tf_op jit(solution)/shard_map/ppermute | solution.py:74
  12.5 0.9 %collective-permute-done.2.refs_0_ = bf16[10,32,128]{2,1,0:T(8,128)(2,1)S(1)} collective-permute-done((bf16[10,32,128]{2,1,0:T(8,128)(2,1)S(1)}, bf16[10,32,128]{2,1,0:T(8,128)(2,1)S(1)}, u32[]{:S(2)}, u32[]{:S(2)}) %collective-permute-start.2) | collective-permute-done | bytes 81952 | tf_op jit(solution)/shard_map/ppermute | solution.py:74
  13.4 0.3 deep.1
  13.8 1.2 %collective-permute-start.3 = (bf16[40,8,128]{2,1,0:T(8,128)(2,1)S(1)}, bf16[40,8,128]{2,1,0:T(8,128)(2,1)S(1)}, u32[]{:S(2)}, u32[]{:S(2)}) collective-permute-start(bf16[40,8,128]{2,1,0:T(8,128)(2,1)S(1)} %get-tuple-element.49), channel_id=1, source_target_pairs={{0,2},{1,3},{2,0},{3,1},{4,6},{5,7},{6,4},{7,5},{8,10},{9,11},{10,... | collective-permute-start | bytes 245768 | tf_op jit(solution)/shard_map/ppermute | solution.py:74
  15.0 0.8 %reshape.6.prof_ref = f32[270]{0:T(512)S(1)} reshape(f32[6,3,15]{2,1,0:T(4,128)} %param.6) | data formatting | bytes 2160 | tf_op jit(solution)/shard_map/reshape | solution.py:546
  15.8 0.8 %reshape.7.box_ref = s32[36]{0:T(128)S(1)} reshape(s32[6,6]{1,0:T(8,128)} %param.7) | data formatting | bytes 288 | tf_op jit(solution)/shard_map/reshape | solution.py:546
  16.6 2.0 %forward_bands.1 = (bf16[6,160,256]{2,1,0:T(8,128)(2,1)S(1)}, bf16[6,160,256]{2,1,0:T(8,128)(2,1)S(1)}, bf16[192,96]{1,0:T(8,128)(2,1)S(1)}) custom-call(bf16[16,512]{1,0:T(8,128)(2,1)S(1)} %get-tuple-element.36.order_ref, f32[270]{0:T(512)S(1)} %reshape.6.prof_ref), custom_call_target="tpu_custom_call" | custom-call | flops 1572864 | bytes 196608 | tf_op jit(solution)/shard_map/forward_bands/pallas_call | solution.py:612
  18.5 0.0 collective-permute-done.3.refs_0_
  18.5 0.0 copy-start.1
  18.5 6.1 %forward.1.order_ref.gain_ref = f32[7,16,32,128]{3,2,1,0:T(8,128)S(1)} custom-call(f32[270]{0:T(512)S(1)} %reshape.6.prof_ref, s32[36]{0:T(128)S(1)} %reshape.7.box_ref, f32[32,32,128]{2,1,0:T(8,128)S(1)} %get-tuple-element.44.cells_ref, f32[32,32,32]{2,1,0:T(8,128)S(1)} %get-tuple-element.45.halos_ref, bf16[6,160,256]{2,1,0:T(8,128)(2,1)S(1)} %get-tuple-element.46.yf_ref, ...), custom_call_target="tpu_custom_call" | custom-call | flops 353894400 | bytes 1572864 | tf_op jit(solution)/shard_map/forward/pallas_call | solution.py:625
  24.7 0.0 copy-done.1
  24.7 1.7 %return_bands.1 = (bf16[6,256,256]{2,1,0:T(8,128)(2,1)S(1)}, bf16[96,192]{1,0:T(8,128)(2,1)S(1)}, f32[16,32,128]{2,1,0:T(8,128)S(1)}) custom-call(f32[7,16,32,128]{3,2,1,0:T(8,128)S(1)} %forward.1.order_ref.gain_ref, f32[270]{0:T(512)S(1)} %reshape.6.prof_ref, s32[36]{0:T(128)S(1)} %reshape.7.box_ref, f32[16,32,128]{2,1,0:T(8,128)S(1)} %copy-done.1), custom_call_target="tpu_custom_call" | custom-call | flops 1572864 | bytes 196608 | tf_op jit(solution)/shard_map/return_bands/pallas_call | solution.py:639
  26.4 0.0 collective-permute-done.4.refs_1_
  26.4 3.0 %half0.1 = (bf16[30,96,128]{2,1,0:T(8,128)(2,1)S(1)}, bf16[30,96,128]{2,1,0:T(8,128)(2,1)S(1)}) custom-call(f32[270]{0:T(512)S(1)} %reshape.6.prof_ref, s32[36]{0:T(128)S(1)} %reshape.7.box_ref, f32[7,16,32,128]{3,2,1,0:T(8,128)S(1)} %forward.1.order_ref.gain_ref, bf16[6,256,256]{2,1,0:T(8,128)(2,1)S(1)} %get-tuple-element.52.yr_ref, ...), custom_call_target="tpu_custom_call" | custom-call | flops 88473600 | bytes 786432 | tf_op jit(solution)/shard_map/half0/pallas_call | solution.py:654
  29.4 0.0 collective-permute-done.5.refs_0_
  29.4 0.0 collective-permute-done.6.refs_1_
  29.4 3.0 %half1.1 = (bf16[30,96,128]{2,1,0:T(8,128)(2,1)S(1)}, bf16[30,96,128]{2,1,0:T(8,128)(2,1)S(1)}) custom-call(f32[270]{0:T(512)S(1)} %reshape.6.prof_ref, s32[36]{0:T(128)S(1)} %reshape.7.box_ref, f32[7,16,32,128]{3,2,1,0:T(8,128)S(1)} %forward.1.order_ref.gain_ref, bf16[6,256,256]{2,1,0:T(8,128)(2,1)S(1)} %get-tuple-element.52.yr_ref, ...), custom_call_target="tpu_custom_call" | custom-call | flops 88473600 | bytes 786432 | tf_op jit(solution)/shard_map/half1/pallas_call | solution.py:654
  32.4 0.7 %returned.1 = (f32[16,32,128]{2,1,0:T(8,128)S(1)}, f32[7,32,128]{2,1,0:T(8,128)S(1)}, f32[16,8,128]{2,1,0:T(8,128)S(1)}, f32[7,8,128]{2,1,0:T(8,128)S(1)}) custom-call(bf16[96,192]{1,0:T(8,128)(2,1)S(1)} %get-tuple-element.51.xr_ref, bf16[30,96,128]{2,1,0:T(8,128)(2,1)S(1)} %get-tuple-element.55.refs_0_, bf16[30,96,128]{2,1,0:T(8,128)(2,1)S(1)} %get-tuple-element.56.refs_1_, ...), custom_call_target="tpu_custom_call" | custom-call | flops 29491200 | bytes 786432 | tf_op jit(solution)/shard_map/returned/pallas_call | solution.py:668
  33.1 2.1 %collective-permute-start.7 = (f32[7,32,128]{2,1,0:T(8,128)S(1)}, f32[7,32,128]{2,1,0:T(8,128)S(1)}, u32[]{:S(2)}, u32[]{:S(2)}) collective-permute-start(f32[7,32,128]{2,1,0:T(8,128)S(1)} %get-tuple-element.62), channel_id=1, source_target_pairs={{0,1},{1,0},{2,3},{3,2},{4,5},{5,4},{6,7},{7,6},{8,9},{9,8},{10,11... | collective-permute-start | bytes 344072 | tf_op jit(solution)/shard_map/ppermute | solution.py:74
  35.3 1.2 %collective-permute-start.8 = (f32[16,8,128]{2,1,0:T(8,128)S(1)}, f32[16,8,128]{2,1,0:T(8,128)S(1)}, u32[]{:S(2)}, u32[]{:S(2)}) collective-permute-start(f32[16,8,128]{2,1,0:T(8,128)S(1)} %get-tuple-element.63), channel_id=1, source_target_pairs={{0,2},{1,3},{2,0},{3,1},{4,6},{5,7},{6,4},{7,5},{8,10},{9,11},{10,... | collective-permute-start | bytes 196616 | tf_op jit(solution)/shard_map/ppermute | solution.py:74
  36.5 0.5 %collective-permute-start.9 = (f32[7,8,128]{2,1,0:T(8,128)S(1)}, f32[7,8,128]{2,1,0:T(8,128)S(1)}, u32[]{:S(2)}, u32[]{:S(2)}) collective-permute-start(f32[7,8,128]{2,1,0:T(8,128)S(1)} %get-tuple-element.64), channel_id=1, source_target_pairs={{0,3},{1,2},{2,1},{3,0},{4,7},{5,6},{6,5},{7,4},{8,11},{9,10},{10,... | collective-permute-start | bytes 86024 | tf_op jit(solution)/shard_map/ppermute | solution.py:74
  37.0 2.8 %collective-permute-done.9.refs_2_ = f32[7,8,128]{2,1,0:T(8,128)S(1)} collective-permute-done((f32[7,8,128]{2,1,0:T(8,128)S(1)}, f32[7,8,128]{2,1,0:T(8,128)S(1)}, u32[]{:S(2)}, u32[]{:S(2)}) %collective-permute-start.9) | collective-permute-done | bytes 28704 | tf_op jit(solution)/shard_map/ppermute | solution.py:74
  39.8 0.0 collective-permute-done.8.refs_1_
  39.8 0.0 collective-permute-done.7.refs_0_
  39.8 0.8 %finish.1 = f32[16,32,128]{2,1,0:T(8,128)} custom-call(f32[16,32,128]{2,1,0:T(8,128)S(1)} %get-tuple-element.50.share_ref, f32[16,32,128]{2,1,0:T(8,128)S(1)} %get-tuple-element.61.mid_ref, f32[7,32,128]{2,1,0:T(8,128)S(1)} %collective-permute-done.7.refs_0_, f32[16,8,128]{2,1,0:T(8,128)S(1)} %collective-permute-done.8.refs_1_, ...), custom_call_target="tpu_custom_call" | custom-call | bytes 393216 | tf_op jit(solution)/shard_map/finish/pallas_call | solution.py:678
Async XLA Ops:
  0.0 0.9 %copy-start = (f32[16,32,128]{2,1,0:T(8,128)S(1)}, f32[16,32,128]{2,1,0:T(8,128)}, u32[]{:S(2)}) copy-start(f32[16,32,128]{2,1,0:T(8,128)} %est_ref.3) | copy-start | bytes 786436
  1.1 6.4 %collective-permute-start = (bf16[16,512]{1,0:T(8,128)(2,1)S(1)}, bf16[16,512]{1,0:T(8,128)(2,1)S(1)}, u32[]{:S(2)}, u32[]{:S(2)}) collective-permute-start(bf16[16,512]{1,0:T(8,128)(2,1)S(1)} %get-tuple-element.36.order_ref), channel_id=1, source_target_pairs={{0,4},{4,0},{8,12},{12,8},{1,5},{5,1},{9,13},{13,9},{2,6},{6,2},{1... | collective-permute-start | bytes 49160 | tf_op jit(solution)/shard_map/ppermute | solution.py:80
  1.3 6.2 %collective-permute-start.1 = (bf16[16,512]{1,0:T(8,128)(2,1)S(1)}, bf16[16,512]{1,0:T(8,128)(2,1)S(1)}, u32[]{:S(2)}, u32[]{:S(2)}) collective-permute-start(bf16[16,512]{1,0:T(8,128)(2,1)S(1)} %get-tuple-element.39), channel_id=1, source_target_pairs={{0,0},{4,8},{8,4},{12,12},{1,1},{5,9},{9,5},{13,13},{2,2},{6,10},{... | collective-permute-start | bytes 49160 | tf_op jit(solution)/shard_map/ppermute | solution.py:80
  5.6 1.1 %copy-start.2 = (bf16[6,16,8,512]{3,2,1,0:T(8,128)(2,1)S(1)}, bf16[6,16,8,512]{3,2,1,0:T(8,128)(2,1)}, u32[]{:S(2)}) copy-start(bf16[6,16,8,512]{3,2,1,0:T(8,128)(2,1)} %rec_ref.1) | copy-start | bytes 2359300
  7.5 18.9 %collective-permute-start.4 = (bf16[7,16,8,128]{3,2,1,0:T(8,128)(2,1)S(1)}, bf16[7,16,8,128]{3,2,1,0:T(8,128)(2,1)S(1)}, u32[]{:S(2)}, u32[]{:S(2)}) collective-permute-start(bf16[7,16,8,128]{3,2,1,0:T(8,128)(2,1)S(1)} %get-tuple-element.54), channel_id=1, source_target_pairs={{0,4},{4,0},{8,12},{12,8},{1,5},{5,1},{9,13},{13,9},{2,6},{6,2},{1... | collective-permute-start | bytes 688136 | tf_op jit(solution)/shard_map/ppermute | solution.py:570
  7.6 21.9 %collective-permute-start.5 = (bf16[7,16,8,128]{3,2,1,0:T(8,128)(2,1)S(1)}, bf16[7,16,8,128]{3,2,1,0:T(8,128)(2,1)S(1)}, u32[]{:S(2)}, u32[]{:S(2)}) collective-permute-start(bf16[7,16,8,128]{3,2,1,0:T(8,128)(2,1)S(1)} %get-tuple-element.57), channel_id=1, source_target_pairs={{0,8},{4,12},{8,0},{12,4},{1,9},{5,13},{9,1},{13,5},{2,10},{6,14},... | collective-permute-start | bytes 688136 | tf_op jit(solution)/shard_map/ppermute | solution.py:573
  8.7 20.7 %collective-permute-start.6 = (bf16[7,16,8,128]{3,2,1,0:T(8,128)(2,1)S(1)}, bf16[7,16,8,128]{3,2,1,0:T(8,128)(2,1)S(1)}, u32[]{:S(2)}, u32[]{:S(2)}) collective-permute-start(bf16[7,16,8,128]{3,2,1,0:T(8,128)(2,1)S(1)} %get-tuple-element.58), channel_id=1, source_target_pairs={{0,12},{4,8},{8,4},{12,0},{1,13},{5,9},{9,5},{13,1},{2,14},{6,10},... | collective-permute-start | bytes 688136 | tf_op jit(solution)/shard_map/ppermute | solution.py:573
  10.4 3.0 %collective-permute-start.2 = (bf16[10,32,128]{2,1,0:T(8,128)(2,1)S(1)}, bf16[10,32,128]{2,1,0:T(8,128)(2,1)S(1)}, u32[]{:S(2)}, u32[]{:S(2)}) collective-permute-start(bf16[10,32,128]{2,1,0:T(8,128)(2,1)S(1)} %get-tuple-element.43), channel_id=1, source_target_pairs={{0,1},{1,0},{2,3},{3,2},{4,5},{5,4},{6,7},{7,6},{8,9},{9,8},{10,11... | collective-permute-start | bytes 245768 | tf_op jit(solution)/shard_map/ppermute | solution.py:74
  13.8 4.7 %collective-permute-start.3 = (bf16[40,8,128]{2,1,0:T(8,128)(2,1)S(1)}, bf16[40,8,128]{2,1,0:T(8,128)(2,1)S(1)}, u32[]{:S(2)}, u32[]{:S(2)}) collective-permute-start(bf16[40,8,128]{2,1,0:T(8,128)(2,1)S(1)} %get-tuple-element.49), channel_id=1, source_target_pairs={{0,2},{1,3},{2,0},{3,1},{4,6},{5,7},{6,4},{7,5},{8,10},{9,11},{10,... | collective-permute-start | bytes 245768 | tf_op jit(solution)/shard_map/ppermute | solution.py:74
  18.5 6.1 %copy-start.1 = (f32[16,32,128]{2,1,0:T(8,128)S(1)}, f32[16,32,128]{2,1,0:T(8,128)}, u32[]{:S(2)}) copy-start(f32[16,32,128]{2,1,0:T(8,128)} %est_ref.3) | copy-start | bytes 786436
  33.1 6.7 %collective-permute-start.7 = (f32[7,32,128]{2,1,0:T(8,128)S(1)}, f32[7,32,128]{2,1,0:T(8,128)S(1)}, u32[]{:S(2)}, u32[]{:S(2)}) collective-permute-start(f32[7,32,128]{2,1,0:T(8,128)S(1)} %get-tuple-element.62), channel_id=1, source_target_pairs={{0,1},{1,0},{2,3},{3,2},{4,5},{5,4},{6,7},{7,6},{8,9},{9,8},{10,11... | collective-permute-start | bytes 344072 | tf_op jit(solution)/shard_map/ppermute | solution.py:74
  35.3 4.5 %collective-permute-start.8 = (f32[16,8,128]{2,1,0:T(8,128)S(1)}, f32[16,8,128]{2,1,0:T(8,128)S(1)}, u32[]{:S(2)}, u32[]{:S(2)}) collective-permute-start(f32[16,8,128]{2,1,0:T(8,128)S(1)} %get-tuple-element.63), channel_id=1, source_target_pairs={{0,2},{1,3},{2,0},{3,1},{4,6},{5,7},{6,4},{7,5},{8,10},{9,11},{10,... | collective-permute-start | bytes 196616 | tf_op jit(solution)/shard_map/ppermute | solution.py:74
  36.5 3.3 %collective-permute-start.9 = (f32[7,8,128]{2,1,0:T(8,128)S(1)}, f32[7,8,128]{2,1,0:T(8,128)S(1)}, u32[]{:S(2)}, u32[]{:S(2)}) collective-permute-start(f32[7,8,128]{2,1,0:T(8,128)S(1)} %get-tuple-element.64), channel_id=1, source_target_pairs={{0,3},{1,2},{2,1},{3,0},{4,7},{5,6},{6,5},{7,4},{8,11},{9,10},{10,... | collective-permute-start | bytes 86024 | tf_op jit(solution)/shard_map/ppermute | solution.py:74

commit v8 on v7

--- a/solution.py
+++ b/solution.py
@@ -430,6 +430,8 @@
     part_rows = half_rows // count
     begin = half_of(slot, paired) * half_rows
     start_z = lax.axis_index("bz") * bz
+    start_x = lax.axis_index("bx") * bx + begin
+    start_y = lax.axis_index("by") * by
 
     def quotient(k, carry):
         for i, part_ref in enumerate(parts):
@@ -443,16 +445,22 @@
     lax.fori_loop(0, views + 1, quotient, 0)
 
     def view(k, carry):
-        cells = [quot[i].reshape(bz * half_rows, by) for i in (k, views)]
-        cells = jnp.concatenate(cells, axis=1)
-        mixed = jnp.dot(cells, yr_ref[k], preferred_element_type=F32)
-        rows[...] = (mixed[:, :by] + mixed[:, by:]).reshape(bz, half_rows, by)
+        meets = (box_ref[k * 6 + 2] < start_x + half_rows) & (box_ref[k * 6 + 3] > start_x)
+        meets = meets & (box_ref[k * 6 + 4] < start_y + by) & (box_ref[k * 6 + 5] > start_y)
+
+        @pl.when(meets)
+        def _():
+            cells = [quot[i].reshape(bz * half_rows, by) for i in (k, views)]
+            cells = jnp.concatenate(cells, axis=1)
+            mixed = jnp.dot(cells, yr_ref[k], preferred_element_type=F32)
+            rows[...] = (mixed[:, :by] + mixed[:, by:]).reshape(bz, half_rows, by)
+
         taps = [prof_ref[(k * 3 + 0) * TAPS + tap] for tap in range(TAPS)]
         at = pl.ds(pl.multiple_of(k * half_rows, half_rows), half_rows)
         low_z = box_ref[k * 6 + 0] - start_z + REACH
         high_z = box_ref[k * 6 + 1] - start_z + REACH
         for first in range(0, deep, GROUP):
-            some = (first + GROUP > low_z) & (first < high_z)
+            some = meets & (first + GROUP > low_z) & (first < high_z)
 
             @pl.when(some)
             def _():

time: 41 us -> 41 us (level)
  Pallas kernels: 18.7 us -> 18.1 us
  starting transfers between devices: 14.4 us -> 14.9 us
    ppermute x5, starting transfers between devices: 7.16 us -> 7.68 us  [exchange(): return lax.ppermute(cells, ('bx', 'bz'), pairs)]
    ppermute x2, waiting for transfers between devices: 0.01 us -> 0.42 us  [local(): lax.ppermute(parts[other], 'by', [(i, i ^ other) for i in range(count)])]
  transfers between devices with their start and end apart: 10 -> 10, of which waited for: 2 -> 3; matrix products, arithmetic and copies ran while one was open for 4% -> 4% of each run, Pallas kernels for 35% -> 33%
where the time goes in v8:
time: 41 us; the launch traced here: 40.8 us
  Pallas kernels  18.1 us (44%)
  starting transfers between devices  14.9 us (36%)
  waiting for transfers between devices  4.1 us (10%)
  local copies, waits for them, and re-layouts  3.65 us (9%)
    ppermute x5, starting transfers between devices, exchange(): return lax.ppermute(cells, ('bx', 'bz'), pairs)  7.68 us
    pallas_call x1, Pallas kernels, local(): call(functools.partial(forward_body, views, block, counts, len(along_x)),...  5.8 us
    pallas_call x2, Pallas kernels, local(): call(functools.partial(half_body, views, block, slot, paired, len(cells))...  5.7 us
    ppermute x2, starting transfers between devices, exchange_y(): lax.ppermute(cells, 'by', [(i, partner(i, count, swap)) for i in range(co...  4.51 us
    ppermute x5, waiting for transfers between devices, exchange(): return lax.ppermute(cells, ('bx', 'bz'), pairs)  3.67 us
    ppermute x2, starting transfers between devices, local(): lax.ppermute(parts[other], 'by', [(i, i ^ other) for i in range(count)])  2.62 us
    unnamed x6, local copies, waits for them, and re-layouts  2.08 us
    pallas_call x1, Pallas kernels, local(): call(functools.partial(forward_bands_body, views, block), [shape((views,...  1.96 us
  transfers between devices with their start and end apart: 10, of which 3 were waited for; matrix products, arithmetic and copies ran while one was open for 4% of the time, Pallas kernels for 33%

profile of v8, /device:TPU:13, one launch (start us, length us, event | category | flops | bytes accessed | tf_op | source)
XLA Modules:
  0.0 40.8 jit_solution(8100576009577222260)
XLA Ops:
  0.0 0.0 copy-start
  0.0 0.9 %copy-done = f32[16,32,128]{2,1,0:T(8,128)S(1)} copy-done((f32[16,32,128]{2,1,0:T(8,128)S(1)}, f32[16,32,128]{2,1,0:T(8,128)}, u32[]{:S(2)}) %copy-start) | copy-done | bytes 262168
  1.0 0.2 columns.1
  1.1 0.2 collective-permute-start
  1.3 4.3 %collective-permute-start.1 = (bf16[16,512]{1,0:T(8,128)(2,1)S(1)}, bf16[16,512]{1,0:T(8,128)(2,1)S(1)}, u32[]{:S(2)}, u32[]{:S(2)}) collective-permute-start(bf16[16,512]{1,0:T(8,128)(2,1)S(1)} %get-tuple-element.39), channel_id=1, source_target_pairs={{0,0},{4,8},{8,4},{12,12},{1,1},{5,9},{9,5},{13,13},{2,2},{6,10},{... | collective-permute-start | bytes 49160 | tf_op jit(solution)/shard_map/ppermute | solution.py:80
  5.6 0.0 copy-start.2
  5.7 1.1 %copy-done.2 = bf16[6,16,8,512]{3,2,1,0:T(8,128)(2,1)S(1)} copy-done((bf16[6,16,8,512]{3,2,1,0:T(8,128)(2,1)S(1)}, bf16[6,16,8,512]{3,2,1,0:T(8,128)(2,1)}, u32[]{:S(2)}) %copy-start.2) | copy-done | bytes 786456
  6.8 0.7 %pieces.1 = (bf16[7,16,8,128]{3,2,1,0:T(8,128)(2,1)S(1)}, bf16[7,16,8,128]{3,2,1,0:T(8,128)(2,1)S(1)}, bf16[7,16,8,128]{3,2,1,0:T(8,128)(2,1)S(1)}, bf16[7,16,8,128]{3,2,1,0:T(8,128)(2,1)S(1)}) custom-call(bf16[16,512]{1,0:T(8,128)(2,1)S(1)} %get-tuple-element.36.order_ref, bf16[6,16,8,512]{3,2,1,0:T(8,128)(2,1)S(1)} %copy-done.2), custom_call_target="tpu_custom_call" | custom-call | bytes 786432 | tf_op jit(solution)/shard_map/pieces/pallas_call | solution.py:571
  7.5 0.1 collective-permute-start.4
  7.5 0.0 collective-permute-done.first_ref
  7.5 0.0 collective-permute-done.1.second_ref
  7.6 1.2 %collective-permute-start.5 = (bf16[7,16,8,128]{3,2,1,0:T(8,128)(2,1)S(1)}, bf16[7,16,8,128]{3,2,1,0:T(8,128)(2,1)S(1)}, u32[]{:S(2)}, u32[]{:S(2)}) collective-permute-start(bf16[7,16,8,128]{3,2,1,0:T(8,128)(2,1)S(1)} %get-tuple-element.57), channel_id=1, source_target_pairs={{0,8},{4,12},{8,0},{12,4},{1,9},{5,13},{9,1},{13,5},{2,10},{6,14},... | collective-permute-start | bytes 688136 | tf_op jit(solution)/shard_map/ppermute | solution.py:581
  8.7 1.5 %collective-permute-start.6 = (bf16[7,16,8,128]{3,2,1,0:T(8,128)(2,1)S(1)}, bf16[7,16,8,128]{3,2,1,0:T(8,128)(2,1)S(1)}, u32[]{:S(2)}, u32[]{:S(2)}) collective-permute-start(bf16[7,16,8,128]{3,2,1,0:T(8,128)(2,1)S(1)} %get-tuple-element.58), channel_id=1, source_target_pairs={{0,12},{4,8},{8,4},{12,0},{1,13},{5,9},{9,5},{13,1},{2,14},{6,10},... | collective-permute-start | bytes 688136 | tf_op jit(solution)/shard_map/ppermute | solution.py:581
  10.2 0.3 edges.1
  10.4 2.1 %collective-permute-start.2 = (bf16[10,32,128]{2,1,0:T(8,128)(2,1)S(1)}, bf16[10,32,128]{2,1,0:T(8,128)(2,1)S(1)}, u32[]{:S(2)}, u32[]{:S(2)}) collective-permute-start(bf16[10,32,128]{2,1,0:T(8,128)(2,1)S(1)} %get-tuple-element.43), channel_id=1, source_target_pairs={{0,1},{1,0},{2,3},{3,2},{4,5},{5,4},{6,7},{7,6},{8,9},{9,8},{10,11... | collective-permute-start | bytes 245768 | tf_op jit(solution)/shard_map/ppermute | solution.py:74
  12.5 0.9 %collective-permute-done.2.refs_0_ = bf16[10,32,128]{2,1,0:T(8,128)(2,1)S(1)} collective-permute-done((bf16[10,32,128]{2,1,0:T(8,128)(2,1)S(1)}, bf16[10,32,128]{2,1,0:T(8,128)(2,1)S(1)}, u32[]{:S(2)}, u32[]{:S(2)}) %collective-permute-start.2) | collective-permute-done | bytes 81952 | tf_op jit(solution)/shard_map/ppermute | solution.py:74
  13.4 0.3 deep.1
  13.8 1.2 %collective-permute-start.3 = (bf16[40,8,128]{2,1,0:T(8,128)(2,1)S(1)}, bf16[40,8,128]{2,1,0:T(8,128)(2,1)S(1)}, u32[]{:S(2)}, u32[]{:S(2)}) collective-permute-start(bf16[40,8,128]{2,1,0:T(8,128)(2,1)S(1)} %get-tuple-element.49), channel_id=1, source_target_pairs={{0,2},{1,3},{2,0},{3,1},{4,6},{5,7},{6,4},{7,5},{8,10},{9,11},{10,... | collective-permute-start | bytes 245768 | tf_op jit(solution)/shard_map/ppermute | solution.py:74
  15.0 0.8 %reshape.6.prof_ref = f32[270]{0:T(512)S(1)} reshape(f32[6,3,15]{2,1,0:T(4,128)} %param.6) | data formatting | bytes 2160 | tf_op jit(solution)/shard_map/reshape | solution.py:554
  15.8 0.8 %reshape.7.box_ref = s32[36]{0:T(128)S(1)} reshape(s32[6,6]{1,0:T(8,128)} %param.7) | data formatting | bytes 288 | tf_op jit(solution)/shard_map/reshape | solution.py:554
  16.6 2.0 %forward_bands.1 = (bf16[6,160,256]{2,1,0:T(8,128)(2,1)S(1)}, bf16[6,160,256]{2,1,0:T(8,128)(2,1)S(1)}, bf16[192,96]{1,0:T(8,128)(2,1)S(1)}) custom-call(bf16[16,512]{1,0:T(8,128)(2,1)S(1)} %get-tuple-element.36.order_ref, f32[270]{0:T(512)S(1)} %reshape.6.prof_ref), custom_call_target="tpu_custom_call" | custom-call | flops 1572864 | bytes 196608 | tf_op jit(solution)/shard_map/forward_bands/pallas_call | solution.py:620
  18.5 0.0 collective-permute-done.3.refs_0_
  18.5 0.0 copy-start.1
  18.5 5.8 %forward.1.order_ref.gain_ref = f32[7,16,32,128]{3,2,1,0:T(8,128)S(1)} custom-call(f32[270]{0:T(512)S(1)} %reshape.6.prof_ref, s32[36]{0:T(128)S(1)} %reshape.7.box_ref, f32[32,32,128]{2,1,0:T(8,128)S(1)} %get-tuple-element.44.cells_ref, f32[32,32,32]{2,1,0:T(8,128)S(1)} %get-tuple-element.45.halos_ref, bf16[6,160,256]{2,1,0:T(8,128)(2,1)S(1)} %get-tuple-element.46.yf_ref, ...), custom_call_target="tpu_custom_call" | custom-call | flops 353894400 | bytes 1572864 | tf_op jit(solution)/shard_map/forward/pallas_call | solution.py:633
  24.4 0.0 copy-done.1
  24.4 1.7 %return_bands.1 = (bf16[6,256,256]{2,1,0:T(8,128)(2,1)S(1)}, bf16[96,192]{1,0:T(8,128)(2,1)S(1)}, f32[16,32,128]{2,1,0:T(8,128)S(1)}) custom-call(f32[7,16,32,128]{3,2,1,0:T(8,128)S(1)} %forward.1.order_ref.gain_ref, f32[270]{0:T(512)S(1)} %reshape.6.prof_ref, s32[36]{0:T(128)S(1)} %reshape.7.box_ref, f32[16,32,128]{2,1,0:T(8,128)S(1)} %copy-done.1), custom_call_target="tpu_custom_call" | custom-call | flops 1572864 | bytes 196608 | tf_op jit(solution)/shard_map/return_bands/pallas_call | solution.py:647
  26.1 0.0 collective-permute-done.4.refs_1_
  26.1 2.6 %half0.1 = (bf16[30,96,128]{2,1,0:T(8,128)(2,1)S(1)}, bf16[30,96,128]{2,1,0:T(8,128)(2,1)S(1)}) custom-call(f32[270]{0:T(512)S(1)} %reshape.6.prof_ref, s32[36]{0:T(128)S(1)} %reshape.7.box_ref, f32[7,16,32,128]{3,2,1,0:T(8,128)S(1)} %forward.1.order_ref.gain_ref, bf16[6,256,256]{2,1,0:T(8,128)(2,1)S(1)} %get-tuple-element.52.yr_ref, ...), custom_call_target="tpu_custom_call" | custom-call | flops 88473600 | bytes 786432 | tf_op jit(solution)/shard_map/half0/pallas_call | solution.py:662
  28.7 0.0 collective-permute-done.5.refs_0_
  28.7 0.4 %collective-permute-done.6.refs_1_ = bf16[7,16,8,128]{3,2,1,0:T(8,128)(2,1)S(1)} collective-permute-done((bf16[7,16,8,128]{3,2,1,0:T(8,128)(2,1)S(1)}, bf16[7,16,8,128]{3,2,1,0:T(8,128)(2,1)S(1)}, u32[]{:S(2)}, u32[]{:S(2)}) %collective-permute-start.6) | collective-permute-done | bytes 229408 | tf_op jit(solution)/shard_map/ppermute | solution.py:581
  29.1 3.1 %half1.1 = (bf16[30,96,128]{2,1,0:T(8,128)(2,1)S(1)}, bf16[30,96,128]{2,1,0:T(8,128)(2,1)S(1)}) custom-call(f32[270]{0:T(512)S(1)} %reshape.6.prof_ref, s32[36]{0:T(128)S(1)} %reshape.7.box_ref, f32[7,16,32,128]{3,2,1,0:T(8,128)S(1)} %forward.1.order_ref.gain_ref, bf16[6,256,256]{2,1,0:T(8,128)(2,1)S(1)} %get-tuple-element.52.yr_ref, ...), custom_call_target="tpu_custom_call" | custom-call | flops 88473600 | bytes 786432 | tf_op jit(solution)/shard_map/half1/pallas_call | solution.py:662
  32.2 0.7 %returned.1 = (f32[16,32,128]{2,1,0:T(8,128)S(1)}, f32[7,32,128]{2,1,0:T(8,128)S(1)}, f32[16,8,128]{2,1,0:T(8,128)S(1)}, f32[7,8,128]{2,1,0:T(8,128)S(1)}) custom-call(bf16[96,192]{1,0:T(8,128)(2,1)S(1)} %get-tuple-element.51.xr_ref, bf16[30,96,128]{2,1,0:T(8,128)(2,1)S(1)} %get-tuple-element.55.refs_0_, bf16[30,96,128]{2,1,0:T(8,128)(2,1)S(1)} %get-tuple-element.56.refs_1_, ...), custom_call_target="tpu_custom_call" | custom-call | flops 29491200 | bytes 786432 | tf_op jit(solution)/shard_map/returned/pallas_call | solution.py:676
  32.9 2.7 %collective-permute-start.7 = (f32[7,32,128]{2,1,0:T(8,128)S(1)}, f32[7,32,128]{2,1,0:T(8,128)S(1)}, u32[]{:S(2)}, u32[]{:S(2)}) collective-permute-start(f32[7,32,128]{2,1,0:T(8,128)S(1)} %get-tuple-element.62), channel_id=1, source_target_pairs={{0,1},{1,0},{2,3},{3,2},{4,5},{5,4},{6,7},{7,6},{8,9},{9,8},{10,11... | collective-permute-start | bytes 344072 | tf_op jit(solution)/shard_map/ppermute | solution.py:74
  35.6 0.7 %collective-permute-start.8 = (f32[16,8,128]{2,1,0:T(8,128)S(1)}, f32[16,8,128]{2,1,0:T(8,128)S(1)}, u32[]{:S(2)}, u32[]{:S(2)}) collective-permute-start(f32[16,8,128]{2,1,0:T(8,128)S(1)} %get-tuple-element.63), channel_id=1, source_target_pairs={{0,2},{1,3},{2,0},{3,1},{4,6},{5,7},{6,4},{7,5},{8,10},{9,11},{10,... | collective-permute-start | bytes 196616 | tf_op jit(solution)/shard_map/ppermute | solution.py:74
  36.3 1.0 %collective-permute-start.9 = (f32[7,8,128]{2,1,0:T(8,128)S(1)}, f32[7,8,128]{2,1,0:T(8,128)S(1)}, u32[]{:S(2)}, u32[]{:S(2)}) collective-permute-start(f32[7,8,128]{2,1,0:T(8,128)S(1)} %get-tuple-element.64), channel_id=1, source_target_pairs={{0,3},{1,2},{2,1},{3,0},{4,7},{5,6},{6,5},{7,4},{8,11},{9,10},{10,... | collective-permute-start | bytes 86024 | tf_op jit(solution)/shard_map/ppermute | solution.py:74
  37.3 2.7 %collective-permute-done.9.refs_2_ = f32[7,8,128]{2,1,0:T(8,128)S(1)} collective-permute-done((f32[7,8,128]{2,1,0:T(8,128)S(1)}, f32[7,8,128]{2,1,0:T(8,128)S(1)}, u32[]{:S(2)}, u32[]{:S(2)}) %collective-permute-start.9) | collective-permute-done | bytes 28704 | tf_op jit(solution)/shard_map/ppermute | solution.py:74
  40.0 0.0 collective-permute-done.8.refs_1_
  40.0 0.0 collective-permute-done.7.refs_0_
  40.0 0.8 %finish.1 = f32[16,32,128]{2,1,0:T(8,128)} custom-call(f32[16,32,128]{2,1,0:T(8,128)S(1)} %get-tuple-element.50.share_ref, f32[16,32,128]{2,1,0:T(8,128)S(1)} %get-tuple-element.61.mid_ref, f32[7,32,128]{2,1,0:T(8,128)S(1)} %collective-permute-done.7.refs_0_, f32[16,8,128]{2,1,0:T(8,128)S(1)} %collective-permute-done.8.refs_1_, ...), custom_call_target="tpu_custom_call" | custom-call | bytes 393216 | tf_op jit(solution)/shard_map/finish/pallas_call | solution.py:686
Async XLA Ops:
  0.0 0.9 %copy-start = (f32[16,32,128]{2,1,0:T(8,128)S(1)}, f32[16,32,128]{2,1,0:T(8,128)}, u32[]{:S(2)}) copy-start(f32[16,32,128]{2,1,0:T(8,128)} %est_ref.3) | copy-start | bytes 786436
  1.1 6.4 %collective-permute-start = (bf16[16,512]{1,0:T(8,128)(2,1)S(1)}, bf16[16,512]{1,0:T(8,128)(2,1)S(1)}, u32[]{:S(2)}, u32[]{:S(2)}) collective-permute-start(bf16[16,512]{1,0:T(8,128)(2,1)S(1)} %get-tuple-element.36.order_ref), channel_id=1, source_target_pairs={{0,4},{4,0},{8,12},{12,8},{1,5},{5,1},{9,13},{13,9},{2,6},{6,2},{1... | collective-permute-start | bytes 49160 | tf_op jit(solution)/shard_map/ppermute | solution.py:80
  1.3 6.2 %collective-permute-start.1 = (bf16[16,512]{1,0:T(8,128)(2,1)S(1)}, bf16[16,512]{1,0:T(8,128)(2,1)S(1)}, u32[]{:S(2)}, u32[]{:S(2)}) collective-permute-start(bf16[16,512]{1,0:T(8,128)(2,1)S(1)} %get-tuple-element.39), channel_id=1, source_target_pairs={{0,0},{4,8},{8,4},{12,12},{1,1},{5,9},{9,5},{13,13},{2,2},{6,10},{... | collective-permute-start | bytes 49160 | tf_op jit(solution)/shard_map/ppermute | solution.py:80
  5.6 1.1 %copy-start.2 = (bf16[6,16,8,512]{3,2,1,0:T(8,128)(2,1)S(1)}, bf16[6,16,8,512]{3,2,1,0:T(8,128)(2,1)}, u32[]{:S(2)}) copy-start(bf16[6,16,8,512]{3,2,1,0:T(8,128)(2,1)} %rec_ref.1) | copy-start | bytes 2359300
  7.5 18.6 %collective-permute-start.4 = (bf16[7,16,8,128]{3,2,1,0:T(8,128)(2,1)S(1)}, bf16[7,16,8,128]{3,2,1,0:T(8,128)(2,1)S(1)}, u32[]{:S(2)}, u32[]{:S(2)}) collective-permute-start(bf16[7,16,8,128]{3,2,1,0:T(8,128)(2,1)S(1)} %get-tuple-element.54), channel_id=1, source_target_pairs={{0,4},{4,0},{8,12},{12,8},{1,5},{5,1},{9,13},{13,9},{2,6},{6,2},{1... | collective-permute-start | bytes 688136 | tf_op jit(solution)/shard_map/ppermute | solution.py:578
  7.6 21.1 %collective-permute-start.5 = (bf16[7,16,8,128]{3,2,1,0:T(8,128)(2,1)S(1)}, bf16[7,16,8,128]{3,2,1,0:T(8,128)(2,1)S(1)}, u32[]{:S(2)}, u32[]{:S(2)}) collective-permute-start(bf16[7,16,8,128]{3,2,1,0:T(8,128)(2,1)S(1)} %get-tuple-element.57), channel_id=1, source_target_pairs={{0,8},{4,12},{8,0},{12,4},{1,9},{5,13},{9,1},{13,5},{2,10},{6,14},... | collective-permute-start | bytes 688136 | tf_op jit(solution)/shard_map/ppermute | solution.py:581
  8.7 20.4 %collective-permute-start.6 = (bf16[7,16,8,128]{3,2,1,0:T(8,128)(2,1)S(1)}, bf16[7,16,8,128]{3,2,1,0:T(8,128)(2,1)S(1)}, u32[]{:S(2)}, u32[]{:S(2)}) collective-permute-start(bf16[7,16,8,128]{3,2,1,0:T(8,128)(2,1)S(1)} %get-tuple-element.58), channel_id=1, source_target_pairs={{0,12},{4,8},{8,4},{12,0},{1,13},{5,9},{9,5},{13,1},{2,14},{6,10},... | collective-permute-start | bytes 688136 | tf_op jit(solution)/shard_map/ppermute | solution.py:581
  10.4 3.0 %collective-permute-start.2 = (bf16[10,32,128]{2,1,0:T(8,128)(2,1)S(1)}, bf16[10,32,128]{2,1,0:T(8,128)(2,1)S(1)}, u32[]{:S(2)}, u32[]{:S(2)}) collective-permute-start(bf16[10,32,128]{2,1,0:T(8,128)(2,1)S(1)} %get-tuple-element.43), channel_id=1, source_target_pairs={{0,1},{1,0},{2,3},{3,2},{4,5},{5,4},{6,7},{7,6},{8,9},{9,8},{10,11... | collective-permute-start | bytes 245768 | tf_op jit(solution)/shard_map/ppermute | solution.py:74
  13.8 4.7 %collective-permute-start.3 = (bf16[40,8,128]{2,1,0:T(8,128)(2,1)S(1)}, bf16[40,8,128]{2,1,0:T(8,128)(2,1)S(1)}, u32[]{:S(2)}, u32[]{:S(2)}) collective-permute-start(bf16[40,8,128]{2,1,0:T(8,128)(2,1)S(1)} %get-tuple-element.49), channel_id=1, source_target_pairs={{0,2},{1,3},{2,0},{3,1},{4,6},{5,7},{6,4},{7,5},{8,10},{9,11},{10,... | collective-permute-start | bytes 245768 | tf_op jit(solution)/shard_map/ppermute | solution.py:74
  18.5 5.8 %copy-start.1 = (f32[16,32,128]{2,1,0:T(8,128)S(1)}, f32[16,32,128]{2,1,0:T(8,128)}, u32[]{:S(2)}) copy-start(f32[16,32,128]{2,1,0:T(8,128)} %est_ref.3) | copy-start | bytes 786436
  32.9 7.1 %collective-permute-start.7 = (f32[7,32,128]{2,1,0:T(8,128)S(1)}, f32[7,32,128]{2,1,0:T(8,128)S(1)}, u32[]{:S(2)}, u32[]{:S(2)}) collective-permute-start(f32[7,32,128]{2,1,0:T(8,128)S(1)} %get-tuple-element.62), channel_id=1, source_target_pairs={{0,1},{1,0},{2,3},{3,2},{4,5},{5,4},{6,7},{7,6},{8,9},{9,8},{10,11... | collective-permute-start | bytes 344072 | tf_op jit(solution)/shard_map/ppermute | solution.py:74
  35.6 4.5 %collective-permute-start.8 = (f32[16,8,128]{2,1,0:T(8,128)S(1)}, f32[16,8,128]{2,1,0:T(8,128)S(1)}, u32[]{:S(2)}, u32[]{:S(2)}) collective-permute-start(f32[16,8,128]{2,1,0:T(8,128)S(1)} %get-tuple-element.63), channel_id=1, source_target_pairs={{0,2},{1,3},{2,0},{3,1},{4,6},{5,7},{6,4},{7,5},{8,10},{9,11},{10,... | collective-permute-start | bytes 196616 | tf_op jit(solution)/shard_map/ppermute | solution.py:74
  36.3 3.8 %collective-permute-start.9 = (f32[7,8,128]{2,1,0:T(8,128)S(1)}, f32[7,8,128]{2,1,0:T(8,128)S(1)}, u32[]{:S(2)}, u32[]{:S(2)}) collective-permute-start(f32[7,8,128]{2,1,0:T(8,128)S(1)} %get-tuple-element.64), channel_id=1, source_target_pairs={{0,3},{1,2},{2,1},{3,0},{4,7},{5,6},{6,5},{7,4},{8,11},{9,10},{10,... | collective-permute-start | bytes 86024 | tf_op jit(solution)/shard_map/ppermute | solution.py:74
